TPU v7x, 128 devices: a whole 4x4x4 slice. The times are simulated.
128 devices in a mesh: blk: 32 (over z_lo, y, x), head: 4 (over z_hi, core).
Axes of the slice: x: 4, y: 4, z: 4 (z_hi: 2, z_lo: 2; z = z_hi * 2 + z_lo), core: 2. Of those that a mesh axis runs over, the one named last changes fastest.
Arguments:
- query_vectors: bfloat16 [4096, 2560], P('blk', 'head'), may hold values from -8 to 8
- key_vectors: bfloat16 [4096, 2560], P('blk', 'head'), may hold values from -8 to 8, as said below
- value_vectors: bfloat16 [4096, 2560], P('blk', 'head'), may hold values from -6 to 6
- tangent_queries: bfloat16 [4096, 2560], P('blk', 'head'), may hold values from -6 to 6
- tangent_keys: bfloat16 [4096, 2560], P('blk', 'head'), may hold values from -6 to 6
- tangent_values: bfloat16 [4096, 2560], P('blk', 'head'), may hold values from -6 to 6
- target_gap: bfloat16 [4096, 2560], P(('blk', 'head')), may hold values from -6 to 6
Outputs:
- primal_out: bfloat16 [4096, 2560], P(('blk', 'head'))
- tangent_out: bfloat16 [4096, 2560], P(('blk', 'head'))
- query_grad: bfloat16 [4096, 2560], P('blk', 'head')
- key_grad: bfloat16 [4096, 2560], P('blk', 'head')
- value_grad: bfloat16 [4096, 2560], P('blk', 'head')
Inputs may be any that keep to these rules, and one draw needn't show every extreme that they name: `key_vectors`: keys are real-valued draws.
All inputs are finite; a program needn't handle non-finite values.
Results may differ from a plain program's by a relative error of at most 0.015.
Values may be sent and summed in bfloat16 or wider, within the bound.
No kernel may reach another device: no remote copies, remote signals or barrier semaphores. Data moves between devices by JAX's collectives and lax.ppermute only.
A program may use at most 128 MiB of HBM per device.

v0:
```python
from functools import partial
import math

import jax
import jax.numpy as jnp
from jax import lax
from jax.sharding import PartitionSpec as P

HD = 128


scale_loss = 64.0
floor_value = -1e30


def split_heads(matrix, head_count):
    return matrix.reshape(matrix.shape[0], head_count, matrix.shape[1] // head_count)


def fold_blocks(advance, running, operands, length):
    block_rows = length
    while block_rows > 512 and block_rows % 2 == 0:
        block_rows = block_rows // 2
    block_total = length // block_rows

    def one_block(position, carried):
        slices = tuple(
            (
                lax.dynamic_slice_in_dim(member, position * block_rows, block_rows, 0)
                for member in operands
            )
        )
        return advance(carried, slices)

    return lax.fori_loop(0, block_total, one_block, running)


def forward_update(nearby, running, slices):
    near_queries, near_tangents, inverse = nearby
    far_keys, far_values, far_tan_keys, far_tan_values = slices
    row_peak, denominator, tan_weight, primal_sum, tangent_sum = running
    scores = (
        jnp.einsum("qhd,khd->qhk", near_queries, far_keys, preferred_element_type=jnp.float32)
        * inverse
    )
    tan_scores = (
        jnp.einsum("qhd,khd->qhk", near_tangents, far_keys, preferred_element_type=jnp.float32)
        + jnp.einsum("qhd,khd->qhk", near_queries, far_tan_keys, preferred_element_type=jnp.float32)
    ) * inverse
    new_peak = jnp.maximum(row_peak, jnp.max(scores, axis=2))
    factor = jnp.exp(row_peak - new_peak)
    weights = jnp.exp(scores - new_peak[:, :, None])
    weighted_tan = weights * tan_scores
    denominator = factor * denominator + jnp.sum(weights, axis=2)
    tan_weight = factor * tan_weight + jnp.sum(weighted_tan, axis=2)
    weights_low = weights.astype(jnp.bfloat16)
    tan_low = weighted_tan.astype(jnp.bfloat16)
    primal_sum = factor[:, :, None] * primal_sum + jnp.einsum(
        "qhk,khd->qhd", weights_low, far_values, preferred_element_type=jnp.float32
    )
    tangent_sum = (
        factor[:, :, None] * tangent_sum
        + jnp.einsum("qhk,khd->qhd", tan_low, far_values, preferred_element_type=jnp.float32)
        + jnp.einsum(
            "qhk,khd->qhd", weights_low, far_tan_values, preferred_element_type=jnp.float32
        )
    )
    return (new_peak, denominator, tan_weight, primal_sum, tangent_sum)


def query_update(nearby, running, slices):
    near_queries, near_cotangent, log_total, inner_sums, inverse = nearby
    far_keys, far_values = slices
    scores = (
        jnp.einsum("qhd,khd->qhk", near_queries, far_keys, preferred_element_type=jnp.float32)
        * inverse
    )
    chances = jnp.exp(scores - log_total[:, :, None])
    prob_grad = jnp.einsum(
        "qhd,khd->qhk", near_cotangent, far_values, preferred_element_type=jnp.float32
    )
    score_grad = (chances * (prob_grad - inner_sums[:, :, None])).astype(jnp.bfloat16)
    return running + jnp.einsum(
        "qhk,khd->qhd", score_grad, far_keys, preferred_element_type=jnp.float32
    )


def key_update(nearby, running, slices):
    near_keys, near_values, inverse = nearby
    far_queries, far_cotangent, far_log, far_inner = slices
    key_acc, value_acc = running
    scores = (
        jnp.einsum("qhd,khd->qhk", far_queries, near_keys, preferred_element_type=jnp.float32)
        * inverse
    )
    chances = jnp.exp(scores - far_log[:, :, None])
    value_acc = value_acc + jnp.einsum(
        "qhk,qhd->khd",
        chances.astype(jnp.bfloat16),
        far_cotangent,
        preferred_element_type=jnp.float32,
    )
    prob_grad = jnp.einsum(
        "qhd,khd->qhk", far_cotangent, near_values, preferred_element_type=jnp.float32
    )
    score_grad = (chances * (prob_grad - far_inner[:, :, None])).astype(jnp.bfloat16)
    key_acc = key_acc + jnp.einsum(
        "qhk,qhd->khd", score_grad, far_queries, preferred_element_type=jnp.float32
    )
    return (key_acc, value_acc)


def per_device(
    query_vectors,
    key_vectors,
    value_vectors,
    tangent_queries,
    tangent_keys,
    tangent_values,
    target_gap,
):
    local_rows = query_vectors.shape[0]
    local_feat = query_vectors.shape[1]
    head_count = local_feat // HD
    inverse = 1.0 / math.sqrt(HD)
    near_queries = split_heads(query_vectors, head_count)
    near_tangents = split_heads(tangent_queries, head_count)
    near_keys = split_heads(key_vectors, head_count)
    near_values = split_heads(value_vectors, head_count)
    row_zeros = jnp.zeros((local_rows, head_count), jnp.float32)
    sum_zeros = jnp.zeros((local_rows, head_count, HD), jnp.float32)
    stats_start = (
        jnp.full((local_rows, head_count), floor_value, jnp.float32),
        row_zeros,
        row_zeros,
        sum_zeros,
        sum_zeros,
    )
    extra_start = ()
    shards = (
        lax.all_gather(key_vectors, "blk", axis=0, tiled=True),
        lax.all_gather(value_vectors, "blk", axis=0, tiled=True),
        lax.all_gather(tangent_keys, "blk", axis=0, tiled=True),
        lax.all_gather(tangent_values, "blk", axis=0, tiled=True),
    )
    stats = stats_start
    extras = extra_start
    operands = tuple((split_heads(member, head_count) for member in shards))
    stats = fold_blocks(
        partial(forward_update, (near_queries, near_tangents, inverse)),
        stats,
        operands,
        shards[0].shape[0],
    )
    stats, extras = (stats, extras)
    row_peak, denominator, tan_weight, primal_sum, tangent_sum = stats
    primal = primal_sum / denominator[:, :, None]
    tangent = (
        tangent_sum / denominator[:, :, None] - (tan_weight / denominator)[:, :, None] * primal
    )
    primal_low = primal.astype(jnp.bfloat16)
    tangent_low = tangent.astype(jnp.bfloat16).reshape(local_rows, -1)
    primal_out, tangent_out = (
        lax.all_to_all(
            primal_low.reshape(local_rows, -1), "head", split_axis=0, concat_axis=1, tiled=True
        ),
        lax.all_to_all(tangent_low, "head", split_axis=0, concat_axis=1, tiled=True),
    )
    token_cotangent = (
        scale_loss * (target_gap.astype(jnp.float32) + tangent_out.astype(jnp.float32))
    ).astype(jnp.bfloat16)
    cotangent = lax.all_to_all(token_cotangent, "head", split_axis=1, concat_axis=0, tiled=True)
    near_cotangent = split_heads(cotangent, head_count)
    log_total = row_peak + jnp.log(denominator)
    inner_sums = jnp.sum(
        near_cotangent.astype(jnp.float32) * primal_low.astype(jnp.float32), axis=2
    )
    all_log, all_inner = (
        lax.all_gather(log_total, "blk", axis=0, tiled=True),
        lax.all_gather(inner_sums, "blk", axis=0, tiled=True),
    )
    query_nearby = (near_queries, near_cotangent, log_total, inner_sums, inverse)
    key_nearby = (near_keys, near_values, inverse)
    shards = (
        lax.all_gather(key_vectors, "blk", axis=0, tiled=True),
        lax.all_gather(value_vectors, "blk", axis=0, tiled=True),
        lax.all_gather(query_vectors, "blk", axis=0, tiled=True),
        lax.all_gather(cotangent, "blk", axis=0, tiled=True),
    )
    query_acc = sum_zeros
    key_acc = sum_zeros
    value_acc = sum_zeros
    length = shards[0].shape[0]
    far_keys, far_values, far_queries, far_cotangent = tuple(
        (split_heads(member, head_count) for member in shards)
    )
    query_acc = fold_blocks(
        partial(query_update, query_nearby), query_acc, (far_keys, far_values), length
    )
    key_acc, value_acc = fold_blocks(
        partial(key_update, key_nearby),
        (key_acc, value_acc),
        (far_queries, far_cotangent, all_log, all_inner),
        length,
    )
    query_acc, key_acc, value_acc = (query_acc, key_acc, value_acc)
    query_grad = (query_acc * inverse).astype(jnp.bfloat16).reshape(local_rows, -1)
    key_grad = (key_acc * inverse).astype(jnp.bfloat16).reshape(local_rows, -1)
    value_grad = value_acc.astype(jnp.bfloat16).reshape(local_rows, -1)
    return (primal_out, tangent_out, query_grad, key_grad, value_grad)


def solution(mesh):
    return jax.shard_map(
        per_device,
        mesh=mesh,
        in_specs=(
            P("blk", "head"),
            P("blk", "head"),
            P("blk", "head"),
            P("blk", "head"),
            P("blk", "head"),
            P("blk", "head"),
            P(("blk", "head"), None),
        ),
        out_specs=(
            P(("blk", "head"), None),
            P(("blk", "head"), None),
            P("blk", "head"),
            P("blk", "head"),
            P("blk", "head"),
        ),
        check_vma=False,
    )
```

profile of v0, /device:TPU:78, one launch (start us, length us, event | category | flops | bytes accessed | tf_op | source)
XLA Modules:
  0.0 1064.1 jit_solution(17173733373195373709)
XLA Ops:
  14.2 140.8 %all-gather.7.cloned.1.call-done = bf16[4096,640]{0,1:T(8,128)(2,1)} async-done(((bf16[128,640]{0,1:T(8,128)(2,1)}), bf16[4096,640]{0,1:T(8,128)(2,1)}) %all-gather.7.cloned.1.call-update) | async-done | bytes 5242896 | tf_op jit(solution)/shard_map/all_gather | solution.py:141
  155.0 7.9 copy.151
  162.8 143.4 %all-gather.13.cloned.1.call-done = bf16[4096,640]{1,0:T(8,128)(2,1)} async-done(((bf16[128,640]{1,0:T(8,128)(2,1)}), bf16[4096,640]{1,0:T(8,128)(2,1)}) %all-gather.13.cloned.1.call-update) | async-done | bytes 5242896 | tf_op jit(solution)/shard_map/all_gather | solution.py:144
  306.3 8.0 copy.150
  314.2 148.9 %all-gather.11.cloned.1.call-done = bf16[4096,640]{0,1:T(8,128)(2,1)} async-done(((bf16[128,640]{0,1:T(8,128)(2,1)}), bf16[4096,640]{0,1:T(8,128)(2,1)}) %all-gather.11.cloned.1.call-update) | async-done | bytes 5242896 | tf_op jit(solution)/shard_map/all_gather | solution.py:142
  463.1 146.8 %all-gather.9.cloned.1.call-done = bf16[4096,640]{0,1:T(8,128)(2,1)} async-done(((bf16[128,640]{0,1:T(8,128)(2,1)}), bf16[4096,640]{0,1:T(8,128)(2,1)}) %all-gather.9.cloned.1.call-update) | async-done | bytes 5242896 | tf_op jit(solution)/shard_map/all_gather | solution.py:143
  609.9 73.8 %while.52 = (s32[]{:T(128)}, f32[128,5]{0,1:T(8,128)S(1)}, f32[128,5]{0,1:T(8,128)S(1)}, f32[128,5]{0,1:T(8,128)S(1)}, f32[128,5,128]{0,2,1:T(8,128)S(1)}, /*ind...) while((s32[]{:T(128)}, f32[128,5]{0,1:T(8,128)S(1)}, ...), condition=%wide.region_4.0_spmd.clone, body=%wide.region_0.0_spmd.clone.sunk | while | flops 508481920 | bytes 16937192 | solution.py:35
  685.0 8.1 all_to_all.57
  693.2 9.5 all_to_all.58
  703.7 63.6 %all_gather.31 = f32[4096,5]{0,1:T(8,128)S(1)} all-gather(f32[128,5]{0,1:T(8,128)S(1)} %get-tuple-element.1071), channel_id=1, replica_groups=mesh['blk'=32,'head'=4] {'blk'}, dimensions={0}, use_global_device_ids=true | all-gather | bytes 84480 | tf_op jit(solution)/shard_map/all_gather | solution.py:179
  768.9 106.4 %all_gather.33 = f32[4096,5]{1,0:T(8,128)} all-gather(f32[128,5]{1,0:T(8,128)S(1)} %get-tuple-element.814), channel_id=1, replica_groups=mesh['blk'=32,'head'=4] {'blk'}, dimensions={0}, use_global_device_ids=true | all-gather | bytes 84480 | tf_op jit(solution)/shard_map/all_gather | solution.py:180
  875.2 2.2 copy.175
  878.4 4.8 all-to-all-start
  883.2 28.4 %while.53 = (s32[]{:T(128)}, f32[128,5,128]{0,2,1:T(8,128)S(1)}, bf16[4096,5,128]{2,0,1:T(8,128)(2,1)}, bf16[128,5,128]{2,0,1:T(8,128)(2,1)S(1)}, f32[128,5]{0,1...) while((s32[]{:T(128)}, f32[128,5,128]{0,2,1:T(8,128)S(1)}, ...), condition=%wide.region_7.0_spmd.clone, body=%wide.region_6.0_spmd.clone.sunk | while | flops 253460480 | bytes 5577392 | solution.py:35
  884.6 2.0 fusion.137
  888.2 2.0 fusion.137
  891.7 2.0 fusion.137
  895.3 2.1 fusion.137
  898.9 2.0 fusion.137
  902.4 2.0 fusion.137
  906.0 2.1 fusion.137
  913.1 8.0 copy.169
  921.1 91.7 %all-gather.15.cloned.1.call-done = bf16[4096,640]{0,1:T(8,128)(2,1)} async-done(((bf16[128,640]{0,1:T(8,128)(2,1)}), bf16[4096,640]{0,1:T(8,128)(2,1)}) %all-gather.15.cloned.1.call-update) | async-done | bytes 5242896 | tf_op jit(solution)/shard_map/all_gather | solution.py:187
  1012.8 42.7 %while.54 = (s32[]{:T(128)}, f32[128,5,128]{0,2,1:T(8,128)S(1)}, f32[128,5,128]{0,2,1:T(8,128)S(1)}, bf16[4096,5,128]{0,2,1:T(8,128)(2,1)}, bf16[128,5,128]{2,0,...) while((s32[]{:T(128)}, f32[128,5,128]{0,2,1:T(8,128)S(1)}, ...), condition=%wide.region_9.0_spmd.clone, body=%wide.region_8.0_spmd.clone.sunk | while | flops 337838080 | bytes 8255169 | solution.py:35
  1016.0 2.1 fusion.146
  1021.3 2.1 fusion.146
  1026.7 2.1 fusion.146
  1032.0 2.1 fusion.146
  1037.4 2.1 fusion.146
  1042.7 2.1 fusion.146
  1048.1 2.1 fusion.146
  1053.4 2.1 fusion.146
  (188 shorter events, 127.1 us)
Async XLA Ops:
  7.2 6.3 copy-start.4
  7.2 6.7 copy-start.5
  7.2 147.8 %all-gather.7.cloned.1.call-start = ((), (), s32[]{:S(2)}) async-start(), calls=%async_computation.3 | async-start | bytes 5406720 | tf_op jit(solution)/shard_map/all_gather | solution.py:141
  9.1 297.2 %all-gather.13.cloned.1.call-start = ((), (), s32[]{:S(2)}) async-start(), calls=%async_computation.6 | async-start | bytes 5406720 | tf_op jit(solution)/shard_map/all_gather | solution.py:144
  9.8 453.3 %all-gather.11.cloned.1.call-start = ((), (), s32[]{:S(2)}) async-start(), calls=%async_computation.5 | async-start | bytes 5406720 | tf_op jit(solution)/shard_map/all_gather | solution.py:142
  11.6 598.3 %all-gather.9.cloned.1.call-start = ((), (), s32[]{:S(2)}) async-start(), calls=%async_computation.4 | async-start | bytes 5406720 | tf_op jit(solution)/shard_map/all_gather | solution.py:143
  13.4 899.7 %all-gather.17.cloned.1.call-start = ((), (), s32[]{:S(2)}) async-start(), calls=%async_computation.8 | async-start | bytes 5406720 | tf_op jit(solution)/shard_map/all_gather | solution.py:188
  13.7 149.2 %copy-start = (bf16[128,640]{0,1:T(8,128)(2,1)}, bf16[128,640]{0,1:T(8,128)(2,1)S(1)}, u32[]{:S(2)}) copy-start(bf16[128,640]{0,1:T(8,128)(2,1)S(1)} %copy.146) | copy-start | bytes 491524
  684.4 8.7 copy-start.6
  684.8 18.6 %copy-start.1 = (bf16[128,640]{0,1:T(8,128)(2,1)S(1)}, bf16[128,640]{0,1:T(8,128)(2,1)}, u32[]{:S(2)}) copy-start(bf16[128,640]{0,1:T(8,128)(2,1)} %copy.145) | copy-start | bytes 491524
  685.0 18.5 %copy-start.2 = (bf16[128,640]{0,1:T(8,128)(2,1)S(1)}, bf16[128,640]{0,1:T(8,128)(2,1)}, u32[]{:S(2)}) copy-start(bf16[128,640]{0,1:T(8,128)(2,1)} %copy.149) | copy-start | bytes 491524
  693.1 75.3 %copy-start.3 = (bf16[4,4,8,640]{3,2,0,1:T(8,128)(2,1)}, bf16[4,4,8,640]{3,2,0,1:T(8,128)(2,1)S(1)}, u32[]{:S(2)}) copy-start(bf16[4,4,8,640]{3,2,0,1:T(8,128)(2,1)S(1)} %copy.192) | copy-start | bytes 491524
  702.7 310.1 %all-gather.15.cloned.1.call-start = ((), (), s32[]{:S(2)}) async-start(), calls=%async_computation.7 | async-start | bytes 5406720 | tf_op jit(solution)/shard_map/all_gather | solution.py:187
  878.4 34.1 %all-to-all-start = ((bf16[4,32,640]{2,1,0:T(8,128)(2,1)}), bf16[4,32,640]{2,1,0:T(8,128)(2,1)S(1)}, u32[]{:S(2)}, u32[]{:S(2)}) async-start(bf16[4,32,640]{2,1,0:T(8,128)(2,1)} %all_to_all.42), calls=%async_computation | async-start | bytes 327680 | tf_op jit(solution)/shard_map/all_to_all | solution.py:164
Sparse Core Ops, SparseCore 0:
  10.1 144.7 all-gather.6
  156.6 149.6 all-gather.12
  308.4 154.6 all-gather.10
  465.1 144.7 all-gather.8
  702.8 152.3 all-gather.16
  856.6 156.1 all-gather.14
where the time goes:
time: 1070 us; the launch traced here: 1060 us
  waiting for transfers between devices  673 us (63%)
  blocking collectives  188 us (18%)
  matrix products  142 us (13%)
  local copies, waits for them, and re-layouts  38.6 us (4%)
  between operations  14.4 us (1%)
    all_gather x1, waiting for transfers between devices, per_device(): lax.all_gather(value_vectors, 'blk', axis=0, tiled=True)  149 us
    all_gather x1, waiting for transfers between devices, per_device(): lax.all_gather(tangent_keys, 'blk', axis=0, tiled=True)  147 us
    all_gather x1, waiting for transfers between devices, per_device(): lax.all_gather(tangent_values, 'blk', axis=0, tiled=True)  143 us
    all_gather x1, waiting for transfers between devices, per_device(): lax.all_gather(key_vectors, 'blk', axis=0, tiled=True)  141 us
    all_gather x1, blocking collectives, per_device(): lax.all_gather(inner_sums, 'blk', axis=0, tiled=True)  106 us
    all_gather x1, waiting for transfers between devices, per_device(): lax.all_gather(query_vectors, 'blk', axis=0, tiled=True)  91.7 us
    all_gather x1, blocking collectives, per_device(): lax.all_gather(log_total, 'blk', axis=0, tiled=True)  63.6 us
  transfers between devices with their start and end apart: 7, of which 5 were waited for; matrix products, arithmetic and copies ran while one was open for 6% of the time, Pallas kernels for 0%

commit v1 on v0

v1 whole, which is shorter than its diff:
```python
from functools import partial
import math

import jax
import jax.numpy as jnp
from jax import lax
from jax.experimental import pallas as pl
from jax.experimental.pallas import tpu as pltpu
from jax.sharding import Mesh, PartitionSpec as P

BF = jnp.bfloat16
F32 = jnp.float32
HD = 128
LOSS = 64.0
PARTS = 3
PIECE = 24
KROWS = 64
QPACK = 16
INV = 1.0 / math.sqrt(HD)
EXP_SCALE = INV * math.log2(math.e)
VMEM = pl.BlockSpec(memory_space=pltpu.VMEM)


def call(body, outs, ins, name, limit, scratch=(), aliases=None, cost=None):
    return pl.pallas_call(
        body,
        out_shape=outs,
        in_specs=[VMEM] * ins,
        out_specs=jax.tree.map(lambda _: VMEM, outs),
        scratch_shapes=list(scratch),
        input_output_aliases=aliases or {},
        compiler_params=pltpu.CompilerParams(vmem_limit_bytes=limit * 1024 * 1024),
        cost_estimate=cost,
        name=name,
    )


def nt(a, b):
    return lax.dot_general(a, b, (((1,), (1,)), ((), ())), preferred_element_type=F32)


def nn(a, b):
    return lax.dot_general(a, b, (((1,), (0,)), ((), ())), preferred_element_type=F32)


def split_tokens(*refs):
    ins, out = refs[:-1], refs[-1]
    for at, ref in enumerate(ins):
        for core in range(2):
            out[core, at, 0:32, :] = ref[32 * core : 32 * core + 32, :]
            out[core, at, 32:64, :] = ref[64 + 32 * core : 96 + 32 * core, :]


def pack_heads(e_ref, g_ref, out):
    heads = 2 * (e_ref.shape[3] // HD)
    half = heads // 2
    for chip in range(out.shape[0]):
        head, part = chip // PARTS, chip % PARTS
        if head >= heads:
            out[chip] = jnp.zeros(out.shape[1:], BF)
            continue
        core, cols = head // half, slice((head % half) * HD, (head % half + 1) * HD)
        out[chip, 0:64, 0:HD] = e_ref[core, 1, :, cols]
        out[chip, 0:64, HD:] = e_ref[core, 4, :, cols]
        out[chip, 64:128, 0:HD] = e_ref[core, 2, :, cols]
        out[chip, 64:128, HD:] = e_ref[core, 5, :, cols]
        low = PIECE * part
        rows = min(PIECE, KROWS - low)
        for side, at in ((0, 0), (1, 3)):
            lanes = slice(side * HD, side * HD + HD)
            out[chip, 128 : 128 + rows, lanes] = e_ref[core, at, low : low + rows, cols]
            if rows < PIECE:
                out[chip, 128 + rows : 128 + PIECE, lanes] = jnp.zeros((PIECE - rows, HD), BF)
        gcols = slice(head * HD, head * HD + HD)
        for eight in range(PIECE // 8):
            lanes = slice(0, HD) if eight < 2 else slice(HD, 2 * HD)
            to = 152 + 8 * (eight % 2)
            row = low + 8 * eight
            if row < KROWS:
                out[chip, to : to + 8, lanes] = g_ref[row // 32, row % 32 : row % 32 + 8, gcols]
            else:
                out[chip, to : to + 8, lanes] = jnp.zeros((8, HD), BF)
        out[chip, 160:168, HD:] = jnp.zeros((8, HD), BF)


def attention(
    mine, theirs, mask, out, out_theirs,
    s_ref, stage, vt_ref, kt_ref, qq_ref, q_ref, cot_ref, acc_ref, acct_ref, dq_ref, *, kc, qt
):
    slots = mine.shape[0]
    rows = slots * PIECE
    per = kc // KROWS
    steps = slots // per
    tiles = rows // qt
    sides = ((mine, out, 0), (theirs, out_theirs, slots * KROWS))
    for s in range(slots):
        at = slice(PIECE * s, PIECE * s + PIECE)
        stage[at, 0 : 2 * HD] = mine[s, 128:152, :].astype(F32)
        stage[PIECE * s : PIECE * s + 16, 2 * HD :] = mine[s, 152:168, 0:HD].astype(F32)
        stage[PIECE * s + 16 : PIECE * s + 24, 2 * HD :] = mine[s, 152:160, HD:].astype(F32)
    q_ref[...] = stage[:, 0:HD].astype(BF)
    qq_ref[:, 0:HD] = stage[:, HD : 2 * HD].astype(BF)
    qq_ref[:, HD:] = stage[:, 0:HD].astype(BF)

    def keys(ref, i, low, lanes):
        return ref[pl.ds(i * per, per), low : low + KROWS, lanes].reshape(kc, -1)

    left, right, both = slice(0, HD), slice(HD, 2 * HD), slice(0, 2 * HD)

    peak = jnp.full((8, rows), -jnp.inf, F32)
    for ref, _, base in sides:

        def scores_step(i, peak, ref=ref, base=base):
            at = pl.multiple_of(base + i * kc, kc)
            step = base // kc + i
            k = keys(ref, i, 0, left)
            kt_ref[step] = k.astype(F32).T.astype(BF)
            vt_ref[step] = keys(ref, i, KROWS, both).astype(F32).T.astype(BF)
            new = []
            for t in range(tiles):
                cols = slice(t * qt, t * qt + qt)
                s = nt(k, q_ref[cols, :])
                s_ref[pl.ds(at, kc), cols] = s
                new.append(jnp.maximum(peak[:, cols], jnp.max(s.reshape(kc // 8, 8, qt), axis=0)))
            return jnp.concatenate(new, axis=1)

        peak = lax.fori_loop(0, steps, scores_step, peak)
    peak = jnp.max(peak, axis=0, keepdims=True)

    acc_ref[...] = jnp.zeros_like(acc_ref)
    acct_ref[...] = jnp.zeros_like(acct_ref)
    sums = (jnp.zeros((8, rows), F32), jnp.zeros((8, rows), F32))
    for ref, _, base in sides:

        def forward_step(i, sums, ref=ref, base=base):
            at = pl.multiple_of(base + i * kc, kc)
            step = base // kc + i
            total, tan_total = sums
            kk = keys(ref, i, 0, both)
            vt = vt_ref[step]
            new, new_tan = [], []
            for t in range(tiles):
                cols = slice(t * qt, t * qt + qt)
                ts = nt(kk, qq_ref[cols, :])
                w = jnp.exp2((s_ref[pl.ds(at, kc), cols] - peak[:, cols]) * EXP_SCALE)
                s_ref[pl.ds(at, kc), cols] = w
                wt = w * ts
                new.append(total[:, cols] + jnp.sum(w.reshape(kc // 8, 8, qt), axis=0))
                new_tan.append(tan_total[:, cols] + jnp.sum(wt.reshape(kc // 8, 8, qt), axis=0))
                acc_ref[:, cols] += nn(vt, w.astype(BF))
                acct_ref[:, cols] += nn(vt[0:HD, :], wt.astype(BF))
            return jnp.concatenate(new, axis=1), jnp.concatenate(new_tan, axis=1)

        sums = lax.fori_loop(0, steps, forward_step, sums)
    total = jnp.sum(sums[0], axis=0, keepdims=True)
    tan_total = jnp.sum(sums[1], axis=0, keepdims=True) * INV
    share = 1.0 / total
    primal = acc_ref[0:HD, :] * share
    tangent = (acct_ref[...] * INV + acc_ref[HD:, :]) * share - (tan_total * share) * primal
    primal_low = primal.astype(BF).astype(F32)
    tangent_low = tangent.astype(BF).astype(F32)
    cot = (LOSS * (stage[:, 2 * HD :].T + tangent_low)) * mask[...]
    cot = cot.astype(BF).astype(F32)
    inner = jnp.sum(cot * primal_low, axis=0, keepdims=True)
    cot_ref[...] = cot.T.astype(BF)
    stage[:, 0:HD] = primal_low.T
    stage[:, HD : 2 * HD] = tangent_low.T

    dq_ref[...] = jnp.zeros_like(dq_ref)
    for ref, dst, base in sides:

        def backward_step(i, carry, ref=ref, dst=dst, base=base):
            at = pl.multiple_of(base + i * kc, kc)
            step = base // kc + i
            v = keys(ref, i, KROWS, left)
            kt = kt_ref[step]
            dk = jnp.zeros((kc, HD), F32)
            dv = jnp.zeros((kc, HD), F32)
            for t in range(tiles):
                cols = slice(t * qt, t * qt + qt)
                p = s_ref[pl.ds(at, kc), cols] * share[:, cols]
                ds = (p * (nt(v, cot_ref[cols, :]) - inner[:, cols])).astype(BF)
                dv = dv + nn(p.astype(BF), cot_ref[cols, :])
                dk = dk + nn(ds, q_ref[cols, :])
                dq_ref[:, cols] += nn(kt, ds)
            dst[pl.ds(i * per, per), 0:KROWS, left] = (dk * INV).astype(BF).reshape(per, KROWS, HD)
            dst[pl.ds(i * per, per), 0:KROWS, right] = dv.astype(BF).reshape(per, KROWS, HD)
            return carry

        lax.fori_loop(0, steps, backward_step, 0)
    stage[:, 2 * HD :] = (dq_ref[...] * INV).T
    for s in range(slots):
        at = slice(PIECE * s, PIECE * s + PIECE)
        out[s, 64:88, :] = stage[at, 0 : 2 * HD].astype(BF)
        out[s, 88:104, left] = stage[PIECE * s : PIECE * s + 16, 2 * HD :].astype(BF)
        out[s, 88:96, right] = stage[PIECE * s + 16 : PIECE * s + 24, 2 * HD :].astype(BF)
        out[s, 96:104, right] = jnp.zeros((8, HD), BF)


def add_partner(b_ref, d_ref, out):
    for s in range(d_ref.shape[0]):
        out[s, 0:KROWS, :] = (
            b_ref[s, 0:KROWS, :].astype(F32) + d_ref[s].astype(F32)
        ).astype(BF)


def unpack_heads(r_ref, f_ref, o_ref):
    half = f_ref.shape[3] // HD
    for head in range(2 * half):
        core, cols = head // half, slice((head % half) * HD, (head % half + 1) * HD)
        first = PARTS * head
        both = sum(r_ref[first + part, 0:KROWS, :].astype(F32) for part in range(PARTS))
        f_ref[core, 1, :, cols] = both[:, 0:HD].astype(BF)
        f_ref[core, 2, :, cols] = both[:, HD:].astype(BF)
        ocols = slice(head * HD, head * HD + HD)
        for eight in range(KROWS // 8):
            chip, low = first + eight // 3, 8 * (eight % 3)
            row = 8 * eight
            lanes = slice(0, HD) if low < 16 else slice(HD, 2 * HD)
            f_ref[core, 0, row : row + 8, cols] = r_ref[chip, 88 + low % 16 : 96 + low % 16, lanes]
            for side in range(2):
                o_ref[row // 32, side, row % 32 : row % 32 + 8, ocols] = r_ref[
                    chip, 64 + low : 72 + low, side * HD : side * HD + HD
                ]


def finish(f_ref, o_ref, primal, tangent, dq, dk, dv):
    for core in range(2):
        for at, ref in enumerate((dq, dk, dv)):
            ref[32 * core : 32 * core + 32, :] = f_ref[core, at, 0:32, :]
            ref[64 + 32 * core : 96 + 32 * core, :] = f_ref[core, at, 32:64, :]
    wide = o_ref.shape[3]
    for side, ref in enumerate((primal, tangent)):
        for group in range(2):
            ref[:, group * wide : group * wide + wide] = o_ref[group, side]


def shape(*dims, dtype=BF):
    return jax.ShapeDtypeStruct(dims, dtype)


SWAP = [(0, 1), (1, 0)]
BLOCK_AXES = ("zl", "y", "x")


def main_kernel(chips, kc, qt):
    rows = chips * PIECE
    keys = 2 * chips * KROWS
    steps = keys // kc
    flops = 2 * 8 * rows * keys * HD
    return call(
        partial(attention, kc=kc, qt=qt),
        (shape(chips, 104, 2 * HD), shape(chips, KROWS, 2 * HD)),
        3,
        "attention",
        48,
        scratch=(
            pltpu.VMEM((keys, rows), F32),
            pltpu.VMEM((rows, 3 * HD), F32),
            pltpu.VMEM((steps, 2 * HD, kc), BF),
            pltpu.VMEM((steps, HD, kc), BF),
            pltpu.VMEM((rows, 2 * HD), BF),
            pltpu.VMEM((rows, HD), BF),
            pltpu.VMEM((rows, HD), BF),
            pltpu.VMEM((2 * HD, rows), F32),
            pltpu.VMEM((HD, rows), F32),
            pltpu.VMEM((HD, rows), F32),
        ),
        cost=pl.CostEstimate(flops=flops, bytes_accessed=9_000_000, transcendentals=rows * keys),
    )


def per_device(q, k, v, tq, tk, tv, gap):
    chips = lax.axis_size(BLOCK_AXES)
    local, feat = q.shape
    wide = gap.shape[1] // 2
    group = lax.axis_index("zh")
    low, high = gap[:, :wide], gap[:, wide:]
    got = lax.ppermute(jnp.where(group == 0, high, low), "zh", SWAP)
    sent = call(split_tokens, shape(2, 6, KROWS, feat), 6, "split_tokens", 8)(q, k, v, tq, tk, tv)
    here = lax.all_to_all(sent, "c", 0, 0, tiled=True)
    own = jnp.where(group == 0, low, high)
    gaps = jnp.stack([jnp.where(group == 0, own, got), jnp.where(group == 0, got, own)])
    packed = call(pack_heads, shape(chips, 168, 2 * HD), 2, "pack_heads", 12)(here, gaps)
    mine = lax.all_to_all(packed, BLOCK_AXES, 0, 0, tiled=True)
    theirs = lax.ppermute(mine, "c", SWAP)
    rows = chips * PIECE
    part = lax.axis_index(BLOCK_AXES) % PARTS
    short = (jnp.arange(rows) % PIECE >= KROWS - PIECE * (PARTS - 1)) & (part == PARTS - 1)
    mask = jnp.where(short, 0.0, 1.0).astype(F32)[None]
    out, out_theirs = main_kernel(chips, 256, 256)(mine, theirs, mask)
    partner = lax.ppermute(out_theirs, "c", SWAP)
    back = call(add_partner, shape(chips, 104, 2 * HD), 2, "add_partner", 8, aliases={0: 0})(out, partner)
    back = lax.all_to_all(back, BLOCK_AXES, 0, 0, tiled=True)
    grads, outs = call(
        unpack_heads, (shape(2, 3, KROWS, feat), shape(2, 2, 32, wide)), 1, "unpack_heads", 12
    )(back)
    other = jnp.where(group == 0, outs[1], outs[0])
    got = lax.ppermute(other, "zh", SWAP)
    grads = lax.all_to_all(grads, "c", 0, 0, tiled=True)
    own = jnp.where(group == 0, outs[0], outs[1])
    outs = jnp.stack([jnp.where(group == 0, own, got), jnp.where(group == 0, got, own)])
    small, large = shape(32, 2 * wide), shape(local, feat)
    return call(finish, (small, small, large, large, large), 2, "finish", 8)(grads, outs)


def solution(mesh):
    zl, y, x, zh, c = 2, 4, 4, 2, 2
    inner = Mesh(mesh.devices.reshape(zl, y, x, zh, c), BLOCK_AXES + ("zh", "c"))
    both = P(BLOCK_AXES, ("zh", "c"))
    rows = P(BLOCK_AXES + ("zh", "c"), None)
    return jax.shard_map(
        per_device,
        mesh=inner,
        in_specs=(both,) * 6 + (rows,),
        out_specs=(rows, rows, both, both, both),
        check_vma=False,
    )
```

time: 1070 us -> 140 us (0.13)
  the two profiles are of different devices: /device:TPU:78 before, /device:TPU:1 now
where the time goes in v1:
time: 140 us; the launch traced here: 139 us
  blocking collectives  68.1 us (49%)
  Pallas kernels  35.4 us (25%)
  starting transfers between devices  18.2 us (13%)
  waiting for transfers between devices  10.1 us (7%)
  local copies, waits for them, and re-layouts  5.5 us (4%)
    all_to_all x1, blocking collectives, per_device(): mine = lax.all_to_all(packed, BLOCK_AXES, 0, 0, tiled=True)  41.3 us
    pallas_call x1, Pallas kernels, per_device(): out, out_theirs = main_kernel(chips, 256, 256)(mine, theirs, mask)  31.3 us
    all_to_all x1, blocking collectives, per_device(): back = lax.all_to_all(back, BLOCK_AXES, 0, 0, tiled=True)  26.8 us
    all_to_all x1, starting transfers between devices, per_device(): grads = lax.all_to_all(grads, 'c', 0, 0, tiled=True)  5.78 us
    unnamed x14, local copies, waits for them, and re-layouts  5.5 us
    ppermute x1, waiting for transfers between devices, per_device(): theirs = lax.ppermute(mine, 'c', SWAP)  4.83 us
    all_to_all x1, starting transfers between devices, per_device(): here = lax.all_to_all(sent, 'c', 0, 0, tiled=True)  4.51 us
    ppermute x1, starting transfers between devices, per_device(): got = lax.ppermute(jnp.where(group == 0, high, low), 'zh', SWAP)  4.49 us
  transfers between devices with their start and end apart: 6, of which 4 were waited for; matrix products, arithmetic and copies ran while one was open for 0% of the time, Pallas kernels for 1%

profile of v1, /device:TPU:1, one launch (start us, length us, event | category | flops | bytes accessed | tf_op | source)
XLA Modules:
  0.0 139.1 jit_solution(2059342188656464233)
XLA Ops:
  0.6 0.0 copy-start.6
  0.6 1.0 broadcast_select_fusion.1
  1.6 4.5 %collective-permute-start = (bf16[32,1280]{1,0:T(8,128)(2,1)S(1)}, bf16[32,1280]{1,0:T(8,128)(2,1)S(1)}, u32[]{:S(2)}, u32[]{:S(2)}) collective-permute-start(bf16[32,1280]{1,0:T(8,128)(2,1)S(1)} %broadcast_select_fusion.1), channel_id=1, source_target_pairs={{0,2},{2,0},{1,3},{3,1},{4,6},{6,4},{5,7},{7,5},{8,10},{10,8},{9,1... | collective-permute-start | bytes 245768 | tf_op jit(solution)/shard_map/ppermute | solution.py:279
  6.1 0.0 copy-start
  6.1 0.9 copy-done
  7.0 0.0 copy-start.1
  7.0 0.9 copy-done.1
  8.0 0.0 copy-start.2
  8.0 0.9 copy-done.2
  8.9 0.9 copy-done.3
  9.8 0.9 copy-done.4
  10.7 0.9 copy-done.5
  11.6 1.0 split_tokens.1
  12.7 4.5 %all-to-all-start = ((bf16[2,6,64,640]{3,2,1,0:T(8,128)(2,1)}), bf16[2,6,64,640]{3,2,1,0:T(8,128)(2,1)S(1)}, u32[]{:S(2)}, u32[]{:S(2)}) async-start(bf16[2,6,64,640]{3,2,1,0:T(8,128)(2,1)} %split_tokens.1), calls=%async_computation | async-start | bytes 1966080 | tf_op jit(solution)/shard_map/all_to_all | solution.py:281
  17.2 0.0 collective-permute-done
  17.2 0.0 copy-done.6
  17.2 1.6 %all-to-all-done.e_ref = bf16[2,6,64,640]{3,2,1,0:T(8,128)(2,1)S(1)} async-done(((bf16[2,6,64,640]{3,2,1,0:T(8,128)(2,1)}), bf16[2,6,64,640]{3,2,1,0:T(8,128)(2,1)S(1)}, u32[]{:S(2)}, u32[]{:S(2)}) %all-to-all-start) | async-done | bytes 983072 | tf_op jit(solution)/shard_map/all_to_all | solution.py:281
  18.9 0.3 pack_heads.1
  19.2 41.3 %all_to_all.20.mine = bf16[32,168,256]{2,1,0:T(8,128)(2,1)S(1)} all-to-all(bf16[32,168,256]{2,1,0:T(8,128)(2,1)S(1)} %pack_heads.1), channel_id=1, replica_groups=mesh['zl'=2,'y'=4,'x'=4,'zh'=2,'c'=2] {'zl','y','x'}, dimensions={0} | all-to-all | bytes 5505024 | tf_op jit(solution)/shard_map/all_to_all | solution.py:285
  60.5 2.0 %collective-permute-start.1 = (bf16[32,168,256]{2,1,0:T(8,128)(2,1)S(1)}, bf16[32,168,256]{2,1,0:T(8,128)(2,1)}, u32[]{:S(2)}, u32[]{:S(2)}) collective-permute-start(bf16[32,168,256]{2,1,0:T(8,128)(2,1)S(1)} %all_to_all.20.mine), channel_id=1, source_target_pairs={{0,1},{1,0},{2,3},{3,2},{4,5},{5,4},{6,7},{7,6},{8,9},{9,8},{10,11... | collective-permute-start | bytes 8257544 | tf_op jit(solution)/shard_map/ppermute | solution.py:286
  62.6 4.8 %collective-permute-done.1.theirs = bf16[32,168,256]{2,1,0:T(8,128)(2,1)} collective-permute-done((bf16[32,168,256]{2,1,0:T(8,128)(2,1)S(1)}, bf16[32,168,256]{2,1,0:T(8,128)(2,1)}, u32[]{:S(2)}, u32[]{:S(2)}) %collective-permute-start.1) | collective-permute-done | bytes 2752544 | tf_op jit(solution)/shard_map/ppermute | solution.py:286
  67.4 31.3 %attention.1 = (bf16[32,104,256]{2,1,0:T(8,128)(2,1)S(1)}, bf16[32,64,256]{2,1,0:T(8,128)(2,1)S(1)}) custom-call(bf16[32,168,256]{2,1,0:T(8,128)(2,1)S(1)} %all_to_all.20.mine, bf16[32,168,256]{2,1,0:T(8,128)(2,1)} %collective-permute-done.1.theirs, f32[1,768]{1,0:T(1,128)S(1)} %and_select_fusion.mask), custom_call_target="tpu_custom_call" | custom-call | flops 6442450944 | bytes 9000000 | tf_op jit(solution)/shard_map/attention/pallas_call | solution.py:291
  98.7 0.4 collective-permute-start.2
  99.2 2.3 %collective-permute-done.2.d_ref = bf16[32,64,256]{2,1,0:T(8,128)(2,1)S(1)} collective-permute-done((bf16[32,64,256]{2,1,0:T(8,128)(2,1)S(1)}, bf16[32,64,256]{2,1,0:T(8,128)(2,1)S(1)}, u32[]{:S(2)}, u32[]{:S(2)}) %collective-permute-start.2) | collective-permute-done | bytes 1048608 | tf_op jit(solution)/shard_map/ppermute | solution.py:292
  101.5 0.8 add_partner.1
  102.3 26.8 %all_to_all.21.r_ref = bf16[32,104,256]{2,1,0:T(8,128)(2,1)S(1)} all-to-all(bf16[32,104,256]{2,1,0:T(8,128)(2,1)S(1)} %add_partner.1), channel_id=1, replica_groups=mesh['zl'=2,'y'=4,'x'=4,'zh'=2,'c'=2] {'zl','y','x'}, dimensions={0} | all-to-all | bytes 3407872 | tf_op jit(solution)/shard_map/all_to_all | solution.py:294
  129.1 1.0 unpack_heads.1
  130.1 0.9 collective-permute-start.3
  131.0 5.8 %all-to-all-start.3 = ((bf16[2,3,64,640]{3,2,1,0:T(8,128)(2,1)}), bf16[2,3,64,640]{3,2,1,0:T(8,128)(2,1)S(1)}, u32[]{:S(2)}, u32[]{:S(2)}) async-start(bf16[2,3,64,640]{3,2,1,0:T(8,128)(2,1)} %get-tuple-element.11), calls=%async_computation.3 | async-start | bytes 983040 | tf_op jit(solution)/shard_map/all_to_all | solution.py:300
  136.8 0.0 collective-permute-done.3
  136.8 1.3 all-to-all-done.3.f_ref
  138.1 0.9 finish.1
  (9 shorter events, 0.1 us)
Async XLA Ops:
  0.6 16.5 %copy-start.6 = (bf16[32,2560]{1,0:T(8,128)(2,1)S(1)}, bf16[32,2560]{1,0:T(8,128)(2,1)}, u32[]{:S(2)}) copy-start(bf16[32,2560]{1,0:T(8,128)(2,1)} %param.13) | copy-start | bytes 491524
  1.6 15.5 %collective-permute-start = (bf16[32,1280]{1,0:T(8,128)(2,1)S(1)}, bf16[32,1280]{1,0:T(8,128)(2,1)S(1)}, u32[]{:S(2)}, u32[]{:S(2)}) collective-permute-start(bf16[32,1280]{1,0:T(8,128)(2,1)S(1)} %broadcast_select_fusion.1), channel_id=1, source_target_pairs={{0,2},{2,0},{1,3},{3,1},{4,6},{6,4},{5,7},{7,5},{8,10},{10,8},{9,1... | collective-permute-start | bytes 245768 | tf_op jit(solution)/shard_map/ppermute | solution.py:279
  6.1 0.9 copy-start
  7.0 0.9 copy-start.1
  8.0 0.9 copy-start.2
  8.9 0.9 copy-start.3
  9.8 0.9 copy-start.4
  10.7 0.9 copy-start.5
  12.7 6.2 %all-to-all-start = ((bf16[2,6,64,640]{3,2,1,0:T(8,128)(2,1)}), bf16[2,6,64,640]{3,2,1,0:T(8,128)(2,1)S(1)}, u32[]{:S(2)}, u32[]{:S(2)}) async-start(bf16[2,6,64,640]{3,2,1,0:T(8,128)(2,1)} %split_tokens.1), calls=%async_computation | async-start | bytes 1966080 | tf_op jit(solution)/shard_map/all_to_all | solution.py:281
  60.5 6.9 %collective-permute-start.1 = (bf16[32,168,256]{2,1,0:T(8,128)(2,1)S(1)}, bf16[32,168,256]{2,1,0:T(8,128)(2,1)}, u32[]{:S(2)}, u32[]{:S(2)}) collective-permute-start(bf16[32,168,256]{2,1,0:T(8,128)(2,1)S(1)} %all_to_all.20.mine), channel_id=1, source_target_pairs={{0,1},{1,0},{2,3},{3,2},{4,5},{5,4},{6,7},{7,6},{8,9},{9,8},{10,11... | collective-permute-start | bytes 8257544 | tf_op jit(solution)/shard_map/ppermute | solution.py:286
  98.7 2.7 %collective-permute-start.2 = (bf16[32,64,256]{2,1,0:T(8,128)(2,1)S(1)}, bf16[32,64,256]{2,1,0:T(8,128)(2,1)S(1)}, u32[]{:S(2)}, u32[]{:S(2)}) collective-permute-start(bf16[32,64,256]{2,1,0:T(8,128)(2,1)S(1)} %get-tuple-element.10), channel_id=1, source_target_pairs={{0,1},{1,0},{2,3},{3,2},{4,5},{5,4},{6,7},{7,6},{8,9},{9,8},{10,11... | collective-permute-start | bytes 3145736 | tf_op jit(solution)/shard_map/ppermute | solution.py:292
  130.1 6.7 %collective-permute-start.3 = (bf16[2,32,1280]{2,1,0:T(8,128)(2,1)S(1)}, bf16[2,32,1280]{2,1,0:T(8,128)(2,1)S(1)}, u32[]{:S(2)}, u32[]{:S(2)}) collective-permute-start(bf16[2,32,1280]{2,1,0:T(8,128)(2,1)S(1)} %select_bitcast_fusion), channel_id=1, source_target_pairs={{0,2},{2,0},{1,3},{3,1},{4,6},{6,4},{5,7},{7,5},{8,10},{10,8},{9,1... | collective-permute-start | bytes 491528 | tf_op jit(solution)/shard_map/ppermute | solution.py:299
  131.0 7.1 %all-to-all-start.3 = ((bf16[2,3,64,640]{3,2,1,0:T(8,128)(2,1)}), bf16[2,3,64,640]{3,2,1,0:T(8,128)(2,1)S(1)}, u32[]{:S(2)}, u32[]{:S(2)}) async-start(bf16[2,3,64,640]{3,2,1,0:T(8,128)(2,1)} %get-tuple-element.11), calls=%async_computation.3 | async-start | bytes 983040 | tf_op jit(solution)/shard_map/all_to_all | solution.py:300

commit v2 on v1

--- a/solution.py
+++ b/solution.py
@@ -21,12 +21,15 @@
 VMEM = pl.BlockSpec(memory_space=pltpu.VMEM)
 
 
-def call(body, outs, ins, name, limit, scratch=(), aliases=None, cost=None):
+HBM = pl.BlockSpec(memory_space=pltpu.HBM)
+
+
+def call(body, outs, ins, name, limit, scratch=(), cost=None, aliases=None):
     return pl.pallas_call(
         body,
-        out_shape=outs,
-        in_specs=[VMEM] * ins,
-        out_specs=jax.tree.map(lambda _: VMEM, outs),
+        out_shape=[one for one, _ in outs],
+        in_specs=ins,
+        out_specs=[place for _, place in outs],
         scratch_shapes=list(scratch),
         input_output_aliases=aliases or {},
         compiler_params=pltpu.CompilerParams(vmem_limit_bytes=limit * 1024 * 1024),
@@ -43,15 +46,43 @@
     return lax.dot_general(a, b, (((1,), (0,)), ((), ())), preferred_element_type=F32)
 
 
+def core():
+    return lax.axis_index("c")
+
+
+def group():
+    return lax.axis_index("zh")
+
+
 def split_tokens(*refs):
-    ins, out = refs[:-1], refs[-1]
-    for at, ref in enumerate(ins):
-        for core in range(2):
-            out[core, at, 0:32, :] = ref[32 * core : 32 * core + 32, :]
-            out[core, at, 32:64, :] = ref[64 + 32 * core : 96 + 32 * core, :]
-
-
-def pack_heads(e_ref, g_ref, out):
+    *arrays, gap, sent, kept, gap_sent, gap_kept, sems, gap_sems = refs
+    wide = gap_sent.shape[1]
+    copies = []
+    for at, (dst, who) in enumerate(((gap_sent, 1 - group()), (gap_kept, group()))):
+        lanes = pl.ds(pl.multiple_of(who * wide, HD), wide)
+        copies.append(pltpu.make_async_copy(gap.at[:, lanes], dst, gap_sems.at[at]))
+    for at, ref in enumerate(arrays):
+        for half in range(2):
+            for side, (dst, who) in enumerate(((sent, 1 - core()), (kept, core()))):
+                low = pl.multiple_of(64 * half + 32 * who, 32)
+                copies.append(
+                    pltpu.make_async_copy(
+                        ref.at[pl.ds(low, 32), :],
+                        dst.at[at, 32 * half : 32 * half + 32, :],
+                        sems.at[at, half, side],
+                    )
+                )
+    for copy in copies:
+        copy.start()
+    for copy in copies:
+        copy.wait()
+
+
+def pack_heads(kept, got, gap, got_gap, out, e_ref, g_ref):
+    e_ref[core()] = kept[...]
+    e_ref[1 - core()] = got[...]
+    g_ref[group()] = gap[...]
+    g_ref[1 - group()] = got_gap[...]
     heads = 2 * (e_ref.shape[3] // HD)
     half = heads // 2
     for chip in range(out.shape[0]):
@@ -59,16 +90,16 @@
         if head >= heads:
             out[chip] = jnp.zeros(out.shape[1:], BF)
             continue
-        core, cols = head // half, slice((head % half) * HD, (head % half + 1) * HD)
-        out[chip, 0:64, 0:HD] = e_ref[core, 1, :, cols]
-        out[chip, 0:64, HD:] = e_ref[core, 4, :, cols]
-        out[chip, 64:128, 0:HD] = e_ref[core, 2, :, cols]
-        out[chip, 64:128, HD:] = e_ref[core, 5, :, cols]
+        at_core, cols = head // half, slice((head % half) * HD, (head % half + 1) * HD)
+        out[chip, 0:64, 0:HD] = e_ref[at_core, 1, :, cols]
+        out[chip, 0:64, HD:] = e_ref[at_core, 4, :, cols]
+        out[chip, 64:128, 0:HD] = e_ref[at_core, 2, :, cols]
+        out[chip, 64:128, HD:] = e_ref[at_core, 5, :, cols]
         low = PIECE * part
         rows = min(PIECE, KROWS - low)
         for side, at in ((0, 0), (1, 3)):
             lanes = slice(side * HD, side * HD + HD)
-            out[chip, 128 : 128 + rows, lanes] = e_ref[core, at, low : low + rows, cols]
+            out[chip, 128 : 128 + rows, lanes] = e_ref[at_core, at, low : low + rows, cols]
             if rows < PIECE:
                 out[chip, 128 + rows : 128 + PIECE, lanes] = jnp.zeros((PIECE - rows, HD), BF)
         gcols = slice(head * HD, head * HD + HD)
@@ -204,35 +235,41 @@
         ).astype(BF)
 
 
-def unpack_heads(r_ref, f_ref, o_ref):
+def unpack_heads(r_ref, sent, kept, o_sent, o_kept, f_ref, o_ref):
     half = f_ref.shape[3] // HD
     for head in range(2 * half):
-        core, cols = head // half, slice((head % half) * HD, (head % half + 1) * HD)
+        at_core, cols = head // half, slice((head % half) * HD, (head % half + 1) * HD)
         first = PARTS * head
         both = sum(r_ref[first + part, 0:KROWS, :].astype(F32) for part in range(PARTS))
-        f_ref[core, 1, :, cols] = both[:, 0:HD].astype(BF)
-        f_ref[core, 2, :, cols] = both[:, HD:].astype(BF)
+        f_ref[at_core, 1, :, cols] = both[:, 0:HD].astype(BF)
+        f_ref[at_core, 2, :, cols] = both[:, HD:].astype(BF)
         ocols = slice(head * HD, head * HD + HD)
         for eight in range(KROWS // 8):
             chip, low = first + eight // 3, 8 * (eight % 3)
             row = 8 * eight
             lanes = slice(0, HD) if low < 16 else slice(HD, 2 * HD)
-            f_ref[core, 0, row : row + 8, cols] = r_ref[chip, 88 + low % 16 : 96 + low % 16, lanes]
+            f_ref[at_core, 0, row : row + 8, cols] = r_ref[chip, 88 + low % 16 : 96 + low % 16, lanes]
             for side in range(2):
                 o_ref[row // 32, side, row % 32 : row % 32 + 8, ocols] = r_ref[
                     chip, 64 + low : 72 + low, side * HD : side * HD + HD
                 ]
-
-
-def finish(f_ref, o_ref, primal, tangent, dq, dk, dv):
-    for core in range(2):
-        for at, ref in enumerate((dq, dk, dv)):
-            ref[32 * core : 32 * core + 32, :] = f_ref[core, at, 0:32, :]
-            ref[64 + 32 * core : 96 + 32 * core, :] = f_ref[core, at, 32:64, :]
-    wide = o_ref.shape[3]
+    sent[...] = f_ref[1 - core()]
+    kept[...] = f_ref[core()]
+    o_sent[...] = o_ref[1 - group()]
+    o_kept[...] = o_ref[group()]
+
+
+def finish(kept, got, o_kept, o_got, primal, tangent, dq, dk, dv):
+    for at, ref in enumerate((dq, dk, dv)):
+        for half in range(2):
+            rows = slice(32 * half, 32 * half + 32)
+            for piece, who in ((kept, core()), (got, 1 - core())):
+                low = pl.multiple_of(64 * half + 32 * who, 32)
+                ref[pl.ds(low, 32), :] = piece[at, rows, :]
+    wide = o_kept.shape[2]
     for side, ref in enumerate((primal, tangent)):
-        for group in range(2):
-            ref[:, group * wide : group * wide + wide] = o_ref[group, side]
+        for piece, who in ((o_kept, group()), (o_got, 1 - group())):
+            ref[:, pl.ds(pl.multiple_of(wide * who, HD), wide)] = piece[side]
 
 
 def shape(*dims, dtype=BF):
@@ -250,10 +287,10 @@
     flops = 2 * 8 * rows * keys * HD
     return call(
         partial(attention, kc=kc, qt=qt),
-        (shape(chips, 104, 2 * HD), shape(chips, KROWS, 2 * HD)),
-        3,
+        ((shape(chips, 104, 2 * HD), VMEM), (shape(chips, KROWS, 2 * HD), VMEM)),
+        [VMEM] * 3,
         "attention",
-        48,
+        34,
         scratch=(
             pltpu.VMEM((keys, rows), F32),
             pltpu.VMEM((rows, 3 * HD), F32),
@@ -274,34 +311,59 @@
     chips = lax.axis_size(BLOCK_AXES)
     local, feat = q.shape
     wide = gap.shape[1] // 2
-    group = lax.axis_index("zh")
-    low, high = gap[:, :wide], gap[:, wide:]
-    got = lax.ppermute(jnp.where(group == 0, high, low), "zh", SWAP)
-    sent = call(split_tokens, shape(2, 6, KROWS, feat), 6, "split_tokens", 8)(q, k, v, tq, tk, tv)
-    here = lax.all_to_all(sent, "c", 0, 0, tiled=True)
-    own = jnp.where(group == 0, low, high)
-    gaps = jnp.stack([jnp.where(group == 0, own, got), jnp.where(group == 0, got, own)])
-    packed = call(pack_heads, shape(chips, 168, 2 * HD), 2, "pack_heads", 12)(here, gaps)
+    piece = shape(6, KROWS, feat)
+    arrays = (q, k, v, tq, tk, tv, gap)
+    sent, kept, gap_sent, gap_kept = call(
+        split_tokens,
+        ((piece, VMEM), (piece, VMEM), (shape(32, wide), VMEM), (shape(32, wide), VMEM)),
+        [HBM] * 7,
+        "split_tokens",
+        6,
+        scratch=(pltpu.SemaphoreType.DMA((6, 2, 2)), pltpu.SemaphoreType.DMA((2,))),
+    )(*(pltpu.with_memory_space_constraint(one, pltpu.HBM) for one in arrays))
+    got_gap = lax.ppermute(gap_sent, "zh", SWAP)
+    got = lax.ppermute(sent, "c", SWAP)
+    packed = call(
+        pack_heads,
+        ((shape(chips, 168, 2 * HD), VMEM),),
+        [VMEM] * 4,
+        "pack_heads",
+        12,
+        scratch=(pltpu.VMEM((2, 6, KROWS, feat), BF), pltpu.VMEM((2, 32, wide), BF)),
+    )(kept, got, gap_kept, got_gap)[0]
     mine = lax.all_to_all(packed, BLOCK_AXES, 0, 0, tiled=True)
     theirs = lax.ppermute(mine, "c", SWAP)
     rows = chips * PIECE
     part = lax.axis_index(BLOCK_AXES) % PARTS
     short = (jnp.arange(rows) % PIECE >= KROWS - PIECE * (PARTS - 1)) & (part == PARTS - 1)
     mask = jnp.where(short, 0.0, 1.0).astype(F32)[None]
-    out, out_theirs = main_kernel(chips, 256, 256)(mine, theirs, mask)
+    out, out_theirs = main_kernel(chips, 1024, 256)(mine, theirs, mask)
     partner = lax.ppermute(out_theirs, "c", SWAP)
-    back = call(add_partner, shape(chips, 104, 2 * HD), 2, "add_partner", 8, aliases={0: 0})(out, partner)
+    back = call(
+        add_partner, ((shape(chips, 104, 2 * HD), VMEM),), [VMEM] * 2, "add_partner", 8, aliases={0: 0}
+    )(out, partner)[0]
     back = lax.all_to_all(back, BLOCK_AXES, 0, 0, tiled=True)
-    grads, outs = call(
-        unpack_heads, (shape(2, 3, KROWS, feat), shape(2, 2, 32, wide)), 1, "unpack_heads", 12
+    piece, opiece = shape(3, KROWS, feat), shape(2, 32, wide)
+    sent, kept, o_sent, o_kept = call(
+        unpack_heads,
+        ((piece, VMEM), (piece, VMEM), (opiece, VMEM), (opiece, VMEM)),
+        [VMEM],
+        "unpack_heads",
+        12,
+        scratch=(pltpu.VMEM((2, 3, KROWS, feat), BF), pltpu.VMEM((2, 2, 32, wide), BF)),
     )(back)
-    other = jnp.where(group == 0, outs[1], outs[0])
-    got = lax.ppermute(other, "zh", SWAP)
-    grads = lax.all_to_all(grads, "c", 0, 0, tiled=True)
-    own = jnp.where(group == 0, outs[0], outs[1])
-    outs = jnp.stack([jnp.where(group == 0, own, got), jnp.where(group == 0, got, own)])
+    o_got = lax.ppermute(o_sent, "zh", SWAP)
+    got = lax.ppermute(sent, "c", SWAP)
     small, large = shape(32, 2 * wide), shape(local, feat)
-    return call(finish, (small, small, large, large, large), 2, "finish", 8)(grads, outs)
+    return tuple(
+        call(
+            finish,
+            ((small, VMEM), (small, VMEM), (large, VMEM), (large, VMEM), (large, VMEM)),
+            [VMEM] * 4,
+            "finish",
+            8,
+        )(kept, got, o_kept, o_got)
+    )
 
 
 def solution(mesh):

time: 140 us -> 118 us (0.84)
  Pallas kernels: 35.4 us -> 21.5 us
  local copies, waits for them, and re-layouts: 5.5 us -> 0 us
  starting transfers between devices: 18.2 us -> 13.6 us
  waiting for transfers between devices: 10.1 us -> 14.3 us
    pallas_call x6, Pallas kernels: 35.4 us -> 21.5 us  [the longest x1 17.4 us: per_device(): out, out_theirs = main_kernel(chips, 1024, 256)(mine, theirs, mask)]
    all_to_all x2 -> x0, starting transfers between devices: 10.3 us -> none  [the longest x1 5.78 us: per_device(): grads = lax.all_to_all(grads, 'c', 0, 0, tiled=True)]
    ppermute x2 -> x4, waiting for transfers between devices: 0.01 us -> 7.2 us  [the longest x1 4.48 us: per_device(): o_got = lax.ppermute(o_sent, 'zh', SWAP)]
    unnamed x14 -> x0, local copies, waits for them, and re-layouts: 5.5 us -> none
    ppermute x2 -> x4, starting transfers between devices: 5.41 us -> 10.6 us  [the longest x1 3.71 us: per_device(): got_gap = lax.ppermute(gap_sent, 'zh', SWAP)]
    all_to_all x2 -> x0, waiting for transfers between devices: 2.92 us -> none  [the longest x1 1.65 us: per_device(): here = lax.all_to_all(sent, 'c', 0, 0, tiled=True)]
  transfers between devices with their start and end apart: 6 -> 6, of which waited for: 4 -> 4; matrix products, arithmetic and copies ran while one was open for 0% -> 0% of each run, Pallas kernels for 1% -> 0%
where the time goes in v2:
time: 118 us
  blocking collectives  67.6 us (57%)
  Pallas kernels  21.5 us (18%)
  waiting for transfers between devices  14.3 us (12%)
  starting transfers between devices  13.6 us (12%)
    all_to_all x1, blocking collectives, per_device(): mine = lax.all_to_all(packed, BLOCK_AXES, 0, 0, tiled=True)  40.8 us
    all_to_all x1, blocking collectives, per_device(): back = lax.all_to_all(back, BLOCK_AXES, 0, 0, tiled=True)  26.8 us
    pallas_call x1, Pallas kernels, per_device(): out, out_theirs = main_kernel(chips, 1024, 256)(mine, theirs, mask)  17.4 us
    ppermute x1, waiting for transfers between devices, per_device(): theirs = lax.ppermute(mine, 'c', SWAP)  4.83 us
    ppermute x1, waiting for transfers between devices, per_device(): o_got = lax.ppermute(o_sent, 'zh', SWAP)  4.48 us
    ppermute x1, starting transfers between devices, per_device(): got_gap = lax.ppermute(gap_sent, 'zh', SWAP)  3.71 us
    ppermute x2, starting transfers between devices, per_device(): got = lax.ppermute(sent, 'c', SWAP)  3.57 us
    ppermute x1, starting transfers between devices, per_device(): o_got = lax.ppermute(o_sent, 'zh', SWAP)  3.3 us
  transfers between devices with their start and end apart: 6, of which 4 were waited for; matrix products, arithmetic and copies ran while one was open for 0% of the time, Pallas kernels for 0%

profile of v2, /device:TPU:1, one launch (start us, length us, event | category | flops | bytes accessed | tf_op | source)
XLA Modules:
  0.0 117.6 jit_solution(13402406684543014620)
XLA Ops:
  0.6 1.6 %split_tokens.1 = (bf16[6,64,640]{2,1,0:T(8,128)(2,1)S(1)}, bf16[6,64,640]{2,1,0:T(8,128)(2,1)S(1)}, bf16[32,1280]{1,0:T(8,128)(2,1)S(1)}, bf16[32,1280]{1,0:T(8,128)(2,1)S(1)}) custom-call(bf16[128,640]{1,0:T(8,128)(2,1)} %refs_0_.1, bf16[128,640]{1,0:T(8,128)(2,1)} %refs_1_.1, bf16[128,640]{1,0:T(8,128)(2,1)} %refs_2_.1, bf16[128,640]{1,0:T(8,128)(2,1)} %refs_3_.1, ...), custom_call_target="tpu_custom_call" | custom-call | tf_op jit(solution)/shard_map/split_tokens/pallas_call | solution.py:316
  2.2 1.5 %collective-permute-start = (bf16[6,64,640]{2,1,0:T(8,128)(2,1)S(1)}, bf16[6,64,640]{2,1,0:T(8,128)(2,1)S(1)}, u32[]{:S(2)}, u32[]{:S(2)}) collective-permute-start(bf16[6,64,640]{2,1,0:T(8,128)(2,1)S(1)} %get-tuple-element.16), channel_id=1, source_target_pairs={{0,1},{1,0},{2,3},{3,2},{4,5},{5,4},{6,7},{7,6},{8,9},{9,8},{10,11... | collective-permute-start | bytes 1474568 | tf_op jit(solution)/shard_map/ppermute | solution.py:325
  3.7 3.7 %collective-permute-start.1 = (bf16[32,1280]{1,0:T(8,128)(2,1)S(1)}, bf16[32,1280]{1,0:T(8,128)(2,1)S(1)}, u32[]{:S(2)}, u32[]{:S(2)}) collective-permute-start(bf16[32,1280]{1,0:T(8,128)(2,1)S(1)} %get-tuple-element.18), channel_id=1, source_target_pairs={{0,2},{2,0},{1,3},{3,1},{4,6},{6,4},{5,7},{7,5},{8,10},{10,8},{9,1... | collective-permute-start | bytes 245768 | tf_op jit(solution)/shard_map/ppermute | solution.py:324
  7.4 2.7 %collective-permute-done.1.got_gap = bf16[32,1280]{1,0:T(8,128)(2,1)S(1)} collective-permute-done((bf16[32,1280]{1,0:T(8,128)(2,1)S(1)}, bf16[32,1280]{1,0:T(8,128)(2,1)S(1)}, u32[]{:S(2)}, u32[]{:S(2)}) %collective-permute-start.1) | collective-permute-done | bytes 81952 | tf_op jit(solution)/shard_map/ppermute | solution.py:324
  10.1 0.0 collective-permute-done.got
  10.1 0.4 pack_heads.1
  10.6 40.8 %all_to_all.10.mine = bf16[32,168,256]{2,1,0:T(8,128)(2,1)S(1)} all-to-all(bf16[32,168,256]{2,1,0:T(8,128)(2,1)S(1)} %pack_heads.1), channel_id=1, replica_groups=mesh['zl'=2,'y'=4,'x'=4,'zh'=2,'c'=2] {'zl','y','x'}, dimensions={0} | all-to-all | bytes 5505024 | tf_op jit(solution)/shard_map/all_to_all | solution.py:334
  51.3 2.5 %collective-permute-start.2 = (bf16[32,168,256]{2,1,0:T(8,128)(2,1)S(1)}, bf16[32,168,256]{2,1,0:T(8,128)(2,1)}, u32[]{:S(2)}, u32[]{:S(2)}) collective-permute-start(bf16[32,168,256]{2,1,0:T(8,128)(2,1)S(1)} %all_to_all.10.mine), channel_id=1, source_target_pairs={{0,1},{1,0},{2,3},{3,2},{4,5},{5,4},{6,7},{7,6},{8,9},{9,8},{10,11... | collective-permute-start | bytes 8257544 | tf_op jit(solution)/shard_map/ppermute | solution.py:335
  53.9 4.8 %collective-permute-done.2.theirs = bf16[32,168,256]{2,1,0:T(8,128)(2,1)} collective-permute-done((bf16[32,168,256]{2,1,0:T(8,128)(2,1)S(1)}, bf16[32,168,256]{2,1,0:T(8,128)(2,1)}, u32[]{:S(2)}, u32[]{:S(2)}) %collective-permute-start.2) | collective-permute-done | bytes 2752544 | tf_op jit(solution)/shard_map/ppermute | solution.py:335
  58.7 17.4 %attention.1 = (bf16[32,104,256]{2,1,0:T(8,128)(2,1)S(1)}, bf16[32,64,256]{2,1,0:T(8,128)(2,1)S(1)}) custom-call(bf16[32,168,256]{2,1,0:T(8,128)(2,1)S(1)} %all_to_all.10.mine, bf16[32,168,256]{2,1,0:T(8,128)(2,1)} %collective-permute-done.2.theirs, f32[1,768]{1,0:T(1,128)S(1)} %and_select_fusion.mask), custom_call_target="tpu_custom_call" | custom-call | flops 6442450944 | bytes 9000000 | tf_op jit(solution)/shard_map/attention/pallas_call | solution.py:340
  76.1 0.5 collective-permute-start.3
  76.6 2.3 %collective-permute-done.3.d_ref = bf16[32,64,256]{2,1,0:T(8,128)(2,1)S(1)} collective-permute-done((bf16[32,64,256]{2,1,0:T(8,128)(2,1)S(1)}, bf16[32,64,256]{2,1,0:T(8,128)(2,1)S(1)}, u32[]{:S(2)}, u32[]{:S(2)}) %collective-permute-start.3) | collective-permute-done | bytes 1048608 | tf_op jit(solution)/shard_map/ppermute | solution.py:341
  78.9 0.8 add_partner.1
  79.7 26.8 %all_to_all.11.r_ref = bf16[32,104,256]{2,1,0:T(8,128)(2,1)S(1)} all-to-all(bf16[32,104,256]{2,1,0:T(8,128)(2,1)S(1)} %add_partner.1), channel_id=1, replica_groups=mesh['zl'=2,'y'=4,'x'=4,'zh'=2,'c'=2] {'zl','y','x'}, dimensions={0} | all-to-all | bytes 3407872 | tf_op jit(solution)/shard_map/all_to_all | solution.py:345
  106.6 0.2 unpack_heads.1
  106.8 2.1 %collective-permute-start.4 = (bf16[3,64,640]{2,1,0:T(8,128)(2,1)S(1)}, bf16[3,64,640]{2,1,0:T(8,128)(2,1)S(1)}, u32[]{:S(2)}, u32[]{:S(2)}) collective-permute-start(bf16[3,64,640]{2,1,0:T(8,128)(2,1)S(1)} %get-tuple-element.22), channel_id=1, source_target_pairs={{0,1},{1,0},{2,3},{3,2},{4,5},{5,4},{6,7},{7,6},{8,9},{9,8},{10,11... | collective-permute-start | bytes 737288 | tf_op jit(solution)/shard_map/ppermute | solution.py:356
  108.9 3.3 %collective-permute-start.5 = (bf16[2,32,1280]{2,1,0:T(8,128)(2,1)S(1)}, bf16[2,32,1280]{2,1,0:T(8,128)(2,1)S(1)}, u32[]{:S(2)}, u32[]{:S(2)}) collective-permute-start(bf16[2,32,1280]{2,1,0:T(8,128)(2,1)S(1)} %get-tuple-element.24), channel_id=1, source_target_pairs={{0,2},{2,0},{1,3},{3,1},{4,6},{6,4},{5,7},{7,5},{8,10},{10,8},{9,1... | collective-permute-start | bytes 491528 | tf_op jit(solution)/shard_map/ppermute | solution.py:355
  112.2 4.5 %collective-permute-done.5.o_got = bf16[2,32,1280]{2,1,0:T(8,128)(2,1)S(1)} collective-permute-done((bf16[2,32,1280]{2,1,0:T(8,128)(2,1)S(1)}, bf16[2,32,1280]{2,1,0:T(8,128)(2,1)S(1)}, u32[]{:S(2)}, u32[]{:S(2)}) %collective-permute-start.5) | collective-permute-done | bytes 163872 | tf_op jit(solution)/shard_map/ppermute | solution.py:355
  116.7 0.0 collective-permute-done.4.got
  116.7 1.0 finish.1
  (1 shorter events, 0.0 us)
Async XLA Ops:
  2.2 7.9 %collective-permute-start = (bf16[6,64,640]{2,1,0:T(8,128)(2,1)S(1)}, bf16[6,64,640]{2,1,0:T(8,128)(2,1)S(1)}, u32[]{:S(2)}, u32[]{:S(2)}) collective-permute-start(bf16[6,64,640]{2,1,0:T(8,128)(2,1)S(1)} %get-tuple-element.16), channel_id=1, source_target_pairs={{0,1},{1,0},{2,3},{3,2},{4,5},{5,4},{6,7},{7,6},{8,9},{9,8},{10,11... | collective-permute-start | bytes 1474568 | tf_op jit(solution)/shard_map/ppermute | solution.py:325
  3.7 6.4 %collective-permute-start.1 = (bf16[32,1280]{1,0:T(8,128)(2,1)S(1)}, bf16[32,1280]{1,0:T(8,128)(2,1)S(1)}, u32[]{:S(2)}, u32[]{:S(2)}) collective-permute-start(bf16[32,1280]{1,0:T(8,128)(2,1)S(1)} %get-tuple-element.18), channel_id=1, source_target_pairs={{0,2},{2,0},{1,3},{3,1},{4,6},{6,4},{5,7},{7,5},{8,10},{10,8},{9,1... | collective-permute-start | bytes 245768 | tf_op jit(solution)/shard_map/ppermute | solution.py:324
  51.3 7.4 %collective-permute-start.2 = (bf16[32,168,256]{2,1,0:T(8,128)(2,1)S(1)}, bf16[32,168,256]{2,1,0:T(8,128)(2,1)}, u32[]{:S(2)}, u32[]{:S(2)}) collective-permute-start(bf16[32,168,256]{2,1,0:T(8,128)(2,1)S(1)} %all_to_all.10.mine), channel_id=1, source_target_pairs={{0,1},{1,0},{2,3},{3,2},{4,5},{5,4},{6,7},{7,6},{8,9},{9,8},{10,11... | collective-permute-start | bytes 8257544 | tf_op jit(solution)/shard_map/ppermute | solution.py:335
  76.1 2.7 %collective-permute-start.3 = (bf16[32,64,256]{2,1,0:T(8,128)(2,1)S(1)}, bf16[32,64,256]{2,1,0:T(8,128)(2,1)S(1)}, u32[]{:S(2)}, u32[]{:S(2)}) collective-permute-start(bf16[32,64,256]{2,1,0:T(8,128)(2,1)S(1)} %get-tuple-element.20), channel_id=1, source_target_pairs={{0,1},{1,0},{2,3},{3,2},{4,5},{5,4},{6,7},{7,6},{8,9},{9,8},{10,11... | collective-permute-start | bytes 3145736 | tf_op jit(solution)/shard_map/ppermute | solution.py:341
  106.8 9.9 %collective-permute-start.4 = (bf16[3,64,640]{2,1,0:T(8,128)(2,1)S(1)}, bf16[3,64,640]{2,1,0:T(8,128)(2,1)S(1)}, u32[]{:S(2)}, u32[]{:S(2)}) collective-permute-start(bf16[3,64,640]{2,1,0:T(8,128)(2,1)S(1)} %get-tuple-element.22), channel_id=1, source_target_pairs={{0,1},{1,0},{2,3},{3,2},{4,5},{5,4},{6,7},{7,6},{8,9},{9,8},{10,11... | collective-permute-start | bytes 737288 | tf_op jit(solution)/shard_map/ppermute | solution.py:356
  108.9 7.8 %collective-permute-start.5 = (bf16[2,32,1280]{2,1,0:T(8,128)(2,1)S(1)}, bf16[2,32,1280]{2,1,0:T(8,128)(2,1)S(1)}, u32[]{:S(2)}, u32[]{:S(2)}) collective-permute-start(bf16[2,32,1280]{2,1,0:T(8,128)(2,1)S(1)} %get-tuple-element.24), channel_id=1, source_target_pairs={{0,2},{2,0},{1,3},{3,1},{4,6},{6,4},{5,7},{7,5},{8,10},{10,8},{9,1... | collective-permute-start | bytes 491528 | tf_op jit(solution)/shard_map/ppermute | solution.py:355

commit v3 on v2

v3 whole, which is shorter than its diff:
```python
import math

import jax
import jax.numpy as jnp
from jax import lax
from jax.experimental import pallas as pl
from jax.experimental.pallas import tpu as pltpu
from jax.sharding import Mesh, PartitionSpec as P


BF = jnp.bfloat16
F32 = jnp.float32
HD = 128
LOSS = 64.0
PARTS = 3
PIECE = 24
KROWS = 64
QT = 256
SUB = 512
INV = 1.0 / math.sqrt(HD)
EXP_SCALE = INV * math.log2(math.e)
VMEM = pl.BlockSpec(memory_space=pltpu.VMEM)
HBM = pl.BlockSpec(memory_space=pltpu.HBM)


def call(body, outs, ins, limit, scratch=(), flops=0, exps=0, moved=1_000_000):
    return pl.pallas_call(
        body,
        out_shape=[
            pltpu.HBM(one.shape, one.dtype) if place is HBM else one for one, place in outs
        ],
        in_specs=ins,
        out_specs=[place for _, place in outs],
        scratch_shapes=list(scratch),
        compiler_params=pltpu.CompilerParams(vmem_limit_bytes=limit * 1024 * 1024),
        cost_estimate=pl.CostEstimate(flops=flops, bytes_accessed=moved, transcendentals=exps),
    )


def nt(a, b):
    return lax.dot_general(a, b, (((1,), (1,)), ((), ())), preferred_element_type=F32)


def nn(a, b):
    return lax.dot_general(a, b, (((1,), (0,)), ((), ())), preferred_element_type=F32)


def core():
    return lax.axis_index("c")


def group():
    return lax.axis_index("zh")


def split_tokens(*refs):
    *arrays, gap, sent, kept, gap_sent, gap_kept, sems, gap_sems = refs
    wide = gap_sent.shape[1]
    copies = []
    for at, (dst, who) in enumerate(((gap_sent, 1 - group()), (gap_kept, group()))):
        lanes = pl.ds(pl.multiple_of(who * wide, HD), wide)
        copies.append(pltpu.make_async_copy(gap.at[:, lanes], dst, gap_sems.at[at]))
    for at, ref in enumerate(arrays):
        for half in range(2):
            for side, (dst, who) in enumerate(((sent, 1 - core()), (kept, core()))):
                low = pl.multiple_of(64 * half + 32 * who, 32)
                copies.append(
                    pltpu.make_async_copy(
                        ref.at[pl.ds(low, 32), :],
                        dst.at[at, 32 * half : 32 * half + 32, :],
                        sems.at[at, half, side],
                    )
                )
    for copy in copies:
        copy.start()
    for copy in copies:
        copy.wait()


def spread(out, stage, sems, fill):
    lot = out.shape[0] // sems.shape[0]
    copies = []
    for at in range(sems.shape[0]):
        for chip in range(lot * at, lot * at + lot):
            fill(chip)
        rows = pl.ds(lot * at, lot)
        copies.append(pltpu.make_async_copy(stage.at[rows], out.at[rows], sems.at[at]))
        copies[-1].start()
    for copy in copies:
        copy.wait()


def pack_heads(kept, got, out, e_ref, stage, sems):
    e_ref[core()] = kept[...]
    e_ref[1 - core()] = got[...]
    half = e_ref.shape[3] // HD

    def fill(chip):
        head, part = chip // PARTS, chip % PARTS
        if head >= 2 * half:
            stage[chip] = jnp.zeros(stage.shape[1:], BF)
            return
        at, cols = head // half, slice((head % half) * HD, (head % half + 1) * HD)
        stage[chip, 0:64, 0:HD] = e_ref[at, 1, :, cols]
        stage[chip, 0:64, HD:] = e_ref[at, 4, :, cols]
        stage[chip, 64:128, 0:HD] = e_ref[at, 2, :, cols]
        stage[chip, 64:128, HD:] = e_ref[at, 5, :, cols]
        low = PIECE * part
        rows = min(PIECE, KROWS - low)
        for side, array in ((0, 0), (1, 3)):
            lanes = slice(side * HD, side * HD + HD)
            stage[chip, 128 : 128 + rows, lanes] = e_ref[at, array, low : low + rows, cols]
            if rows < PIECE:
                stage[chip, 128 + rows : 152, lanes] = jnp.zeros((PIECE - rows, HD), BF)

    spread(out, stage, sems, fill)


def pack_gaps(gap, got_gap, out, g_ref, stage, sems):
    g_ref[group()] = gap[...]
    g_ref[1 - group()] = got_gap[...]
    heads = gap.shape[1] // HD

    def fill(chip):
        head, low = chip // PARTS, PIECE * (chip % PARTS)
        stage[chip] = jnp.zeros(stage.shape[1:], BF)
        if head >= heads:
            return
        gcols = slice(head * HD, head * HD + HD)
        for eight in range(PIECE // 8):
            lanes = slice(0, HD) if eight < 2 else slice(HD, 2 * HD)
            to, row = 8 * (eight % 2), low + 8 * eight
            if row < KROWS:
                stage[chip, to : to + 8, lanes] = g_ref[row // 32, row % 32 : row % 32 + 8, gcols]

    spread(out, stage, sems, fill)


def fold(x, op):
    return op(x.reshape(x.shape[0] // 8, 8, x.shape[1]), axis=0)


def rows_of(ref, slot, count, low):
    return ref[slot : slot + count, low : low + KROWS, :].reshape(count * KROWS, 2 * HD)


def forward(keys, q_ref, qq_ref, w_ref, m_ref, sums_ref, acc_ref, s_ref, wt_ref, kk_ref, vt_ref):
    tiles = q_ref.shape[0]
    length = kk_ref.shape[0]
    per = SUB // KROWS
    subs = length // SUB
    for i in range(subs):
        at = slice(SUB * i, SUB * i + SUB)
        kk_ref[at, :] = rows_of(keys, per * i, per, 0)
        vt_ref[:, at] = rows_of(keys, per * i, per, KROWS).astype(F32).T.astype(BF)

    def tile(t, carry):
        q, qq = q_ref[t], qq_ref[t]
        peak = jnp.full((8, QT), -jnp.inf, F32)
        for i in range(subs):
            at = slice(SUB * i, SUB * i + SUB)
            s = nt(kk_ref[at, 0:HD], q)
            s_ref[at, :] = s
            peak = jnp.maximum(peak, fold(s, jnp.max))
        peak = jnp.max(peak, axis=0, keepdims=True)
        total = jnp.zeros((8, QT), F32)
        tan_total = jnp.zeros((8, QT), F32)
        for i in range(subs):
            at = slice(SUB * i, SUB * i + SUB)
            w = jnp.exp2((s_ref[at, :] - peak) * EXP_SCALE)
            wt = w * nt(kk_ref[at, :], qq)
            total = total + fold(w, jnp.sum)
            tan_total = tan_total + fold(wt, jnp.sum)
            w_ref[t, at, :] = w.astype(BF)
            wt_ref[at, :] = wt.astype(BF)
        m_ref[t] = peak
        sums_ref[t, 0:1, :] = jnp.sum(total, axis=0, keepdims=True)
        sums_ref[t, 1:2, :] = jnp.sum(tan_total, axis=0, keepdims=True) * INV
        both = nn(vt_ref[...], w_ref[t])
        acc_ref[t, 0:HD, :] = both[0:HD, :]
        acc_ref[t, HD:, :] = both[HD:, :] + nn(vt_ref[0:HD, :], wt_ref[...]) * INV
        return carry

    lax.fori_loop(0, tiles, tile, 0)


def forward_mine(mine, q_ref, qq_ref, w_ref, m_ref, sums_ref, acc_ref, stage, *scratch):
    for s in range(mine.shape[0]):
        stage[PIECE * s : PIECE * s + PIECE, :] = mine[s, 2 * KROWS :, :].astype(F32)
    for t in range(q_ref.shape[0]):
        rows = slice(QT * t, QT * t + QT)
        q_ref[t] = stage[rows, 0:HD].astype(BF)
        qq_ref[t, :, 0:HD] = stage[rows, HD:].astype(BF)
        qq_ref[t, :, HD:] = stage[rows, 0:HD].astype(BF)
    forward(mine, q_ref, qq_ref, w_ref, m_ref, sums_ref, acc_ref, *scratch)


def forward_theirs(
    theirs, q_ref, qq_ref, m1_ref, sums1_ref, acc1_ref,
    out, w_ref, o_ref, share_ref,
    m_ref, sums_ref, acc_ref, stage, pieces, sem, *scratch
):
    forward(theirs, q_ref, qq_ref, w_ref, m_ref, sums_ref, acc_ref, *scratch)
    for t in range(q_ref.shape[0]):
        top = jnp.maximum(m1_ref[t], m_ref[t])
        f1 = jnp.exp2((m1_ref[t] - top) * EXP_SCALE)
        f2 = jnp.exp2((m_ref[t] - top) * EXP_SCALE)
        sums = sums1_ref[t] * f1 + sums_ref[t] * f2
        inverse = 1.0 / sums[0:1]
        s1, s2 = f1 * inverse, f2 * inverse
        share_ref[0, t] = s1
        share_ref[1, t] = s2
        both = acc1_ref[t] * s1 + acc_ref[t] * s2
        primal = both[0:HD]
        tangent = both[HD:] - (sums[1:2] * inverse) * primal
        o_ref[t, 0:HD, :] = primal.astype(BF).astype(F32)
        o_ref[t, HD:, :] = tangent.astype(BF).astype(F32)
        stage[QT * t : QT * t + QT, :] = o_ref[t].T
    for s in range(out.shape[0]):
        pieces[s] = stage[PIECE * s : PIECE * s + PIECE, :].astype(BF)
    copy = pltpu.make_async_copy(pieces, out, sem)
    copy.start()
    copy.wait()


def backward(keys, q_ref, cot_ref, inner_ref, w_ref, share_ref, side, dst, dq_ref, kt_ref, ds_ref, p_ref):
    tiles = q_ref.shape[0]
    per = SUB // KROWS
    subs = keys.shape[0] // per

    def some(i, carry):
        at = pl.ds(pl.multiple_of(SUB * i, SUB), SUB)
        slots = pl.ds(per * i, per)
        k = keys[slots, 0:KROWS, 0:HD].reshape(SUB, HD)
        v = keys[slots, KROWS : 2 * KROWS, 0:HD].reshape(SUB, HD)
        kt_ref[i] = k.astype(F32).T.astype(BF)
        for t in range(tiles):
            cols = slice(QT * t, QT * t + QT)
            p = w_ref[t, at, :].astype(F32) * share_ref[side, t]
            ds = p * (nt(v, cot_ref[cols, :]) - inner_ref[t])
            p_ref[:, cols] = p.astype(BF)
            ds_ref[i, :, cols] = ds.astype(BF)
        dk = nn(ds_ref[i], q_ref[...].reshape(tiles * QT, HD)) * INV
        dv = nn(p_ref[...], cot_ref[...])
        dst[slots, 0:KROWS, 0:HD] = dk.astype(BF).reshape(per, KROWS, HD)
        dst[slots, 0:KROWS, HD:] = dv.astype(BF).reshape(per, KROWS, HD)
        return carry

    lax.fori_loop(0, subs, some, 0)
    dq = dq_ref[...]
    for i in range(subs):
        dq = dq + nn(kt_ref[i], ds_ref[i])
    dq_ref[...] = dq


def backward_theirs(
    theirs, gaps, mask, q_ref, o_ref, w_ref, share_ref, dst, cot_ref, inner_ref, dq_ref, stage, *scratch
):
    for s in range(gaps.shape[0]):
        stage[PIECE * s : PIECE * s + 16, :] = gaps[s, :, 0:HD].astype(F32)
        stage[PIECE * s + 16 : PIECE * s + 24, :] = gaps[s, 0:8, HD:].astype(F32)
    for t in range(q_ref.shape[0]):
        rows = slice(QT * t, QT * t + QT)
        cot = (LOSS * (stage[rows, :].T + o_ref[t, HD:, :])) * mask[:, rows]
        cot = cot.astype(BF).astype(F32)
        inner_ref[t] = jnp.sum(cot * o_ref[t, 0:HD, :], axis=0, keepdims=True)
        cot_ref[rows, :] = cot.T.astype(BF)
    dq_ref[...] = jnp.zeros_like(dq_ref)
    backward(theirs, q_ref, cot_ref, inner_ref, w_ref, share_ref, 1, dst, dq_ref, *scratch)


def backward_mine(
    mine, q_ref, cot_ref, inner_ref, w_ref, share_ref, dq1_ref, out, dq_ref, stage, *scratch
):
    dq_ref[...] = dq1_ref[...]
    backward(mine, q_ref, cot_ref, inner_ref, w_ref, share_ref, 0, out, dq_ref, *scratch)
    stage[...] = (dq_ref[...] * INV).T
    for s in range(out.shape[0]):
        low = PIECE * s
        out[s, 64:80, 0:HD] = stage[low : low + 16, :].astype(BF)
        out[s, 64:72, HD:] = stage[low + 16 : low + 24, :].astype(BF)
        out[s, 72:80, HD:] = jnp.zeros((8, HD), BF)


def add_partner(mine, theirs, out, stage, sems):
    def fill(chip):
        stage[chip, 0:KROWS, :] = (
            mine[chip, 0:KROWS, :].astype(F32) + theirs[chip].astype(F32)
        ).astype(BF)
        stage[chip, KROWS:, :] = mine[chip, KROWS:, :]

    spread(out, stage, sems, fill)


def unpack_outs(r_ref, sent, kept, o_ref):
    heads = o_ref.shape[3] // HD
    for head in range(heads):
        cols = slice(head * HD, head * HD + HD)
        for eight in range(KROWS // 8):
            chip, low = PARTS * head + eight // 3, 8 * (eight % 3)
            row = 8 * eight
            for side in range(2):
                o_ref[row // 32, side, row % 32 : row % 32 + 8, cols] = r_ref[
                    chip, low : low + 8, side * HD : side * HD + HD
                ]
    sent[...] = o_ref[1 - group()]
    kept[...] = o_ref[group()]


def unpack_grads(r_ref, sent, kept, f_ref):
    half = f_ref.shape[3] // HD
    for head in range(2 * half):
        at, cols = head // half, slice((head % half) * HD, (head % half + 1) * HD)
        first = PARTS * head
        both = sum(r_ref[first + part, 0:KROWS, :].astype(F32) for part in range(PARTS))
        f_ref[at, 1, :, cols] = both[:, 0:HD].astype(BF)
        f_ref[at, 2, :, cols] = both[:, HD:].astype(BF)
        for eight in range(KROWS // 8):
            chip, low = first + eight // 3, 8 * (eight % 3)
            row = 8 * eight
            lanes = slice(0, HD) if low < 16 else slice(HD, 2 * HD)
            f_ref[at, 0, row : row + 8, cols] = r_ref[chip, 64 + low % 16 : 72 + low % 16, lanes]
    sent[...] = f_ref[1 - core()]
    kept[...] = f_ref[core()]


def finish_outs(kept, got, primal, tangent):
    wide = kept.shape[2]
    for side, ref in enumerate((primal, tangent)):
        for piece, who in ((kept, group()), (got, 1 - group())):
            ref[:, pl.ds(pl.multiple_of(wide * who, HD), wide)] = piece[side]


def finish_grads(kept, got, dq, dk, dv):
    for at, ref in enumerate((dq, dk, dv)):
        for half in range(2):
            rows = slice(32 * half, 32 * half + 32)
            for piece, who in ((kept, core()), (got, 1 - core())):
                low = pl.multiple_of(64 * half + 32 * who, 32)
                ref[pl.ds(low, 32), :] = piece[at, rows, :]


def shape(*dims, dtype=BF):
    return jax.ShapeDtypeStruct(dims, dtype)


SWAP = [(0, 1), (1, 0)]
BLOCK_AXES = ("zl", "y", "x")


def exchange(array):
    return lax.all_to_all(array, BLOCK_AXES, 0, 0, tiled=True)


def swap(array, axis):
    return lax.ppermute(array, axis, SWAP)


def out_stage(chips, rows):
    return (pltpu.VMEM((chips, rows, 2 * HD), BF), pltpu.SemaphoreType.DMA((4,)))


def attention(chips, mine, theirs, gaps, mask):
    length, tiles = chips * KROWS, chips * PIECE // QT
    rows = tiles * QT
    flops = 2 * length * rows * HD
    q, qq = shape(tiles, QT, HD), shape(tiles, QT, 2 * HD)
    w = shape(tiles, length, QT)
    stats, sums, acc = (shape(tiles, n, QT, dtype=F32) for n in (1, 2, 2 * HD))
    scratch = (
        pltpu.VMEM((length, QT), F32),
        pltpu.VMEM((length, QT), BF),
        pltpu.VMEM((length, 2 * HD), BF),
        pltpu.VMEM((2 * HD, length), BF),
    )
    stage = pltpu.VMEM((rows, 2 * HD), F32)
    q, qq, w1, m1, sums1, acc1 = call(
        forward_mine,
        [(one, VMEM) for one in (q, qq, w, stats, sums, acc)],
        [VMEM],
        24,
        (stage,) + scratch,
        6 * flops, length * rows, 7_000_000,
    )(mine)
    out, w2, o, share = call(
        forward_theirs,
        [
            (shape(chips, PIECE, 2 * HD), HBM),
            (w, VMEM), (acc, VMEM), (shape(2, tiles, 1, QT, dtype=F32), VMEM),
        ],
        [VMEM] * 6,
        28,
        (
            pltpu.VMEM(stats.shape, F32), pltpu.VMEM(sums.shape, F32), pltpu.VMEM(acc.shape, F32),
            stage, pltpu.VMEM((chips, PIECE, 2 * HD), BF), pltpu.SemaphoreType.DMA,
        ) + scratch,
        6 * flops, length * rows, 7_000_000,
    )(theirs, q, qq, m1, sums1, acc1)
    outs = exchange(out)
    subs = length // SUB
    scratch = (
        pltpu.VMEM((rows, HD), F32),
        pltpu.VMEM((subs, HD, SUB), BF),
        pltpu.VMEM((subs, SUB, rows), BF),
        pltpu.VMEM((SUB, rows), BF),
    )
    out_theirs, cot, inner, dq = call(
        backward_theirs,
        [
            (shape(chips, KROWS, 2 * HD), VMEM), (shape(rows, HD), VMEM),
            (stats, VMEM), (shape(HD, rows, dtype=F32), VMEM),
        ],
        [VMEM] * 7,
        24,
        scratch,
        8 * flops, 0, 7_000_000,
    )(theirs, gaps, mask, q, o, w2, share)
    partner = swap(out_theirs, "c")
    out = call(
        backward_mine,
        [(shape(chips, KROWS + 16, 2 * HD), VMEM)],
        [VMEM] * 7,
        24,
        (pltpu.VMEM((HD, rows), F32),) + scratch,
        8 * flops, 0, 7_000_000,
    )(mine, q, cot, inner, w1, share, dq)[0]
    back = call(
        add_partner, [(shape(chips, KROWS + 16, 2 * HD), HBM)], [VMEM] * 2, 8,
        out_stage(chips, KROWS + 16),
    )(out, partner)[0]
    return outs, exchange(back)


def per_device(q, k, v, tq, tk, tv, gap):
    chips = lax.axis_size(BLOCK_AXES)
    local, feat = q.shape
    wide = gap.shape[1] // 2
    piece, gpiece = shape(6, KROWS, feat), shape(32, wide)
    arrays = (q, k, v, tq, tk, tv, gap)
    sent, kept, gap_sent, gap_kept = call(
        split_tokens,
        [(piece, VMEM), (piece, VMEM), (gpiece, VMEM), (gpiece, VMEM)],
        [HBM] * 7,
        4,
        (pltpu.SemaphoreType.DMA((6, 2, 2)), pltpu.SemaphoreType.DMA((2,))),
    )(*(pltpu.with_memory_space_constraint(one, pltpu.HBM) for one in arrays))
    got = swap(sent, "c")
    packed = call(
        pack_heads,
        [(shape(chips, 152, 2 * HD), HBM)],
        [VMEM] * 2,
        8,
        (pltpu.VMEM((2,) + piece.shape, BF),) + out_stage(chips, 152),
    )(kept, got)[0]
    mine = exchange(packed)

    got_gap = swap(gap_sent, "zh")
    packed = call(
        pack_gaps,
        [(shape(chips, 16, 2 * HD), HBM)],
        [VMEM] * 2,
        4,
        (pltpu.VMEM((2,) + gpiece.shape, BF),) + out_stage(chips, 16),
    )(gap_kept, got_gap)[0]
    gaps = exchange(packed)
    theirs = swap(mine, "c")

    rows = chips * PIECE
    part = lax.axis_index(BLOCK_AXES) % PARTS
    short = (jnp.arange(rows) % PIECE >= KROWS - PIECE * (PARTS - 1)) & (part == PARTS - 1)
    mask = jnp.where(short, 0.0, 1.0).astype(F32)[None]
    outs, back = attention(chips, mine, theirs, gaps, mask)

    opiece, fpiece = shape(2, 32, wide), shape(3, KROWS, feat)
    sent, kept = call(
        unpack_outs, [(opiece, VMEM), (opiece, VMEM)], [VMEM], 4,
        (pltpu.VMEM((2,) + opiece.shape, BF),),
    )(outs)
    got = swap(sent, "zh")
    small, large = shape(32, 2 * wide), shape(local, feat)
    primal, tangent = call(finish_outs, [(small, VMEM), (small, VMEM)], [VMEM] * 2, 4)(kept, got)
    sent, kept = call(
        unpack_grads, [(fpiece, VMEM), (fpiece, VMEM)], [VMEM], 6,
        (pltpu.VMEM((2,) + fpiece.shape, BF),),
    )(back)
    got = swap(sent, "c")
    dq, dk, dv = call(finish_grads, [(large, VMEM)] * 3, [VMEM] * 2, 4)(kept, got)
    return primal, tangent, dq, dk, dv


def solution(mesh):
    sizes = (2, 4, 4, 2, 2)
    inner = Mesh(mesh.devices.reshape(sizes), BLOCK_AXES + ("zh", "c"))
    both = P(BLOCK_AXES, ("zh", "c"))
    rows = P(BLOCK_AXES + ("zh", "c"), None)

    return jax.shard_map(
        per_device,
        mesh=inner,
        in_specs=(both,) * 6 + (rows,),
        out_specs=(rows, rows, both, both, both),
        check_vma=False,
    )
```

time: 118 us -> 144 us (1.22)
  the two profiles are of different devices: /device:TPU:1 before, /device:TPU:0 now
where the time goes in v3:
time: 144 us; the launch traced here: 143 us
  blocking collectives  70.7 us (49%)
  Pallas kernels  31.7 us (22%)
  waiting for transfers between devices  17.6 us (12%)
  starting transfers between devices  15.6 us (11%)
  local copies, waits for them, and re-layouts  6.81 us (5%)
    all_to_all x2, blocking collectives, exchange(): return lax.all_to_all(array, BLOCK_AXES, 0, 0, tiled=True)  70.7 us
    all_to_all x2, waiting for transfers between devices, exchange(): return lax.all_to_all(array, BLOCK_AXES, 0, 0, tiled=True)  9.09 us
    pallas_call x1, Pallas kernels, attention(): call(forward_theirs, [(shape(chips, PIECE, 2 * HD), HBM), (w, VMEM), (acc...  8.93 us
    ppermute x6, waiting for transfers between devices, swap(): return lax.ppermute(array, axis, SWAP)  8.53 us
    all_to_all x2, starting transfers between devices, exchange(): return lax.all_to_all(array, BLOCK_AXES, 0, 0, tiled=True)  8.44 us
    ppermute x6, starting transfers between devices, swap(): return lax.ppermute(array, axis, SWAP)  7.16 us
    unnamed x14, local copies, waits for them, and re-layouts  6.81 us
    pallas_call x1, Pallas kernels, attention(): call(forward_mine, [(one, VMEM) for one in (q, qq, w, stats, sums, acc)],...  6.07 us
  transfers between devices with their start and end apart: 8, of which 4 were waited for; matrix products, arithmetic and copies ran while one was open for 0% of the time, Pallas kernels for 14%

profile of v3, /device:TPU:0, one launch (start us, length us, event | category | flops | bytes accessed | tf_op | source)
XLA Modules:
  0.0 143.3 jit_solution(3258815931991432696)
XLA Ops:
  0.6 1.6 %shard_map.110 = (bf16[6,64,640]{2,1,0:T(8,128)(2,1)S(1)}, bf16[6,64,640]{2,1,0:T(8,128)(2,1)S(1)}, bf16[32,1280]{1,0:T(8,128)(2,1)S(1)}, bf16[32,1280]{1,0:T(8,128)(2,1)S(1)}) custom-call(bf16[128,640]{1,0:T(8,128)(2,1)} %refs_0_.1, bf16[128,640]{1,0:T(8,128)(2,1)} %refs_1_.1, bf16[128,640]{1,0:T(8,128)(2,1)} %refs_2_.1, bf16[128,640]{1,0:T(8,128)(2,1)} %refs_3_.1, ...), custom_call_target="tpu_custom_call" | custom-call | bytes 1000000 | tf_op jit(solution)/shard_map/pallas_call | solution.py:440
  2.2 0.1 collective-permute-start
  2.3 1.9 %collective-permute-done.got = bf16[6,64,640]{2,1,0:T(8,128)(2,1)S(1)} collective-permute-done((bf16[6,64,640]{2,1,0:T(8,128)(2,1)S(1)}, bf16[6,64,640]{2,1,0:T(8,128)(2,1)S(1)}, u32[]{:S(2)}, u32[]{:S(2)}) %collective-permute-start) | collective-permute-done | bytes 491552 | tf_op jit(solution)/shard_map/ppermute | solution.py:356
  4.2 1.7 %shard_map.111 = bf16[32,152,256]{2,1,0:T(8,128)(2,1)} custom-call(bf16[6,64,640]{2,1,0:T(8,128)(2,1)S(1)} %get-tuple-element.32.kept, bf16[6,64,640]{2,1,0:T(8,128)(2,1)S(1)} %collective-permute-done.got), custom_call_target="tpu_custom_call" | custom-call | bytes 1000000 | tf_op jit(solution)/shard_map/pallas_call | solution.py:448
  5.8 41.6 %all_to_all.20.mine = bf16[32,152,256]{2,1,0:T(8,128)(2,1)S(1)} all-to-all(bf16[32,152,256]{2,1,0:T(8,128)(2,1)} %shard_map.111), channel_id=1, replica_groups=mesh['zl'=2,'y'=4,'x'=4,'zh'=2,'c'=2] {'zl','y','x'}, dimensions={0} | all-to-all | bytes 4980736 | tf_op jit(solution)/shard_map/all_to_all | solution.py:352
  47.5 0.0 collective-permute-start.1
  47.5 3.6 %collective-permute-start.3 = (bf16[32,1280]{1,0:T(8,128)(2,1)S(1)}, bf16[32,1280]{1,0:T(8,128)(2,1)S(1)}, u32[]{:S(2)}, u32[]{:S(2)}) collective-permute-start(bf16[32,1280]{1,0:T(8,128)(2,1)S(1)} %get-tuple-element.45), channel_id=1, source_target_pairs={{0,2},{2,0},{1,3},{3,1},{4,6},{6,4},{5,7},{7,5},{8,10},{10,8},{9,1... | collective-permute-start | bytes 245768 | tf_op jit(solution)/shard_map/ppermute | solution.py:356
  51.1 3.1 %collective-permute-done.3.got_gap = bf16[32,1280]{1,0:T(8,128)(2,1)S(1)} collective-permute-done((bf16[32,1280]{1,0:T(8,128)(2,1)S(1)}, bf16[32,1280]{1,0:T(8,128)(2,1)S(1)}, u32[]{:S(2)}, u32[]{:S(2)}) %collective-permute-start.3) | collective-permute-done | bytes 81952 | tf_op jit(solution)/shard_map/ppermute | solution.py:356
  54.2 0.8 shard_map.116
  54.9 4.3 %all-to-all-start.2 = ((bf16[32,16,256]{2,1,0:T(8,128)(2,1)}), bf16[32,16,256]{2,1,0:T(8,128)(2,1)S(1)}, u32[]{:S(2)}, u32[]{:S(2)}) async-start(bf16[32,16,256]{2,1,0:T(8,128)(2,1)} %shard_map.116), calls=%async_computation.2 | async-start | bytes 524288 | tf_op jit(solution)/shard_map/all_to_all | solution.py:352
  59.3 6.1 %shard_map.112 = (bf16[3,256,128]{2,1,0:T(8,128)(2,1)S(1)}, bf16[3,256,256]{2,1,0:T(8,128)(2,1)S(1)}, bf16[3,2048,256]{2,1,0:T(8,128)(2,1)S(1)}, f32[3,1,256]{2,...) custom-call(bf16[32,152,256]{2,1,0:T(8,128)(2,1)S(1)} %all_to_all.20.mine), custom_call_target="tpu_custom_call" | custom-call | flops 2415919104 | bytes 7000000 | tf_op jit(solution)/shard_map/pallas_call | solution.py:377
  65.4 1.6 %copy-done = bf16[3,2048,256]{2,1,0:T(8,128)(2,1)} copy-done((bf16[3,2048,256]{2,1,0:T(8,128)(2,1)}, bf16[3,2048,256]{2,1,0:T(8,128)(2,1)S(1)}, u32[]{:S(2)}) %copy-start) | copy-done | bytes 3145752
  67.0 0.0 collective-permute-done.1.theirs
  67.0 8.9 %shard_map.113 = (bf16[32,24,256]{2,1,0:T(8,128)(2,1)}, bf16[3,2048,256]{2,1,0:T(8,128)(2,1)S(1)}, f32[3,256,256]{2,1,0:T(8,128)S(1)}, f32[2,3,1,256]{3,2,1,0:T(1,128)S(1)}) custom-call(bf16[32,152,256]{2,1,0:T(8,128)(2,1)} %collective-permute-done.1.theirs, bf16[3,256,128]{2,1,0:T(8,128)(2,1)S(1)} %get-tuple-element.34.q_ref, ...), custom_call_target="tpu_custom_call" | custom-call | flops 2415919104 | bytes 7000000 | tf_op jit(solution)/shard_map/pallas_call | solution.py:385
  75.9 1.7 %copy-done.2 = bf16[3,2048,256]{2,1,0:T(8,128)(2,1)} copy-done((bf16[3,2048,256]{2,1,0:T(8,128)(2,1)}, bf16[3,2048,256]{2,1,0:T(8,128)(2,1)S(1)}, u32[]{:S(2)}) %copy-start.2) | copy-done | bytes 3145752
  77.6 0.7 copy-done.4
  78.3 1.9 %copy-done.3 = bf16[3,2048,256]{2,1,0:T(8,128)(2,1)S(1)} copy-done((bf16[3,2048,256]{2,1,0:T(8,128)(2,1)S(1)}, bf16[3,2048,256]{2,1,0:T(8,128)(2,1)}, u32[]{:S(2)}) %copy-start.3) | copy-done | bytes 3145752
  80.2 0.9 copy-done.5
  81.1 5.9 %shard_map.117 = (bf16[32,64,256]{2,1,0:T(8,128)(2,1)S(1)}, bf16[768,128]{1,0:T(8,128)(2,1)S(1)}, f32[3,1,256]{2,1,0:T(1,128)S(1)}, f32[128,768]{1,0:T(8,128)S(1)}) custom-call(bf16[32,152,256]{2,1,0:T(8,128)(2,1)} %collective-permute-done.1.theirs, bf16[32,16,256]{2,1,0:T(8,128)(2,1)S(1)} %all-to-all-done.2.gaps, f32[1,768]{1,0:T(1,128)S(1)} %and_select_fusion.mask, ...), custom_call_target="tpu_custom_call" | custom-call | flops 3221225472 | bytes 7000000 | tf_op jit(solution)/shard_map/pallas_call | solution.py:407
  87.0 0.1 collective-permute-start.4
  87.1 3.9 %shard_map.118.mine = bf16[32,80,256]{2,1,0:T(8,128)(2,1)S(1)} custom-call(bf16[32,152,256]{2,1,0:T(8,128)(2,1)S(1)} %all_to_all.20.mine, bf16[3,256,128]{2,1,0:T(8,128)(2,1)S(1)} %copy-done.6, bf16[768,128]{1,0:T(8,128)(2,1)S(1)} %get-tuple-element.49.cot_ref, f32[3,1,256]{2,1,0:T(1,128)S(1)} %get-tuple-element.50.inner_ref, ...), custom_call_target="tpu_custom_call" | custom-call | flops 3221225472 | bytes 7000000 | tf_op jit(solution)/shard_map/pallas_call | solution.py:419
  91.0 1.2 shard_map.119
  92.2 29.1 %all_to_all.21.r_ref = bf16[32,80,256]{2,1,0:T(8,128)(2,1)S(1)} all-to-all(bf16[32,80,256]{2,1,0:T(8,128)(2,1)} %shard_map.119), channel_id=1, replica_groups=mesh['zl'=2,'y'=4,'x'=4,'zh'=2,'c'=2] {'zl','y','x'}, dimensions={0} | all-to-all | bytes 2621440 | tf_op jit(solution)/shard_map/all_to_all | solution.py:352
  121.3 4.1 %all-to-all-start.1 = ((bf16[32,24,256]{2,1,0:T(8,128)(2,1)}), bf16[32,24,256]{2,1,0:T(8,128)(2,1)S(1)}, u32[]{:S(2)}, u32[]{:S(2)}) async-start(bf16[32,24,256]{2,1,0:T(8,128)(2,1)} %get-tuple-element.39), calls=%async_computation.1 | async-start | bytes 786432 | tf_op jit(solution)/shard_map/all_to_all | solution.py:352
  125.4 0.2 shard_map.120
  125.6 0.1 collective-permute-start.5
  125.7 9.1 %all-to-all-done.1.r_ref = bf16[32,24,256]{2,1,0:T(8,128)(2,1)S(1)} async-done(((bf16[32,24,256]{2,1,0:T(8,128)(2,1)}), bf16[32,24,256]{2,1,0:T(8,128)(2,1)S(1)}, u32[]{:S(2)}, u32[]{:S(2)}) %all-to-all-start.1) | async-done | bytes 393248 | tf_op jit(solution)/shard_map/all_to_all | solution.py:352
  134.7 0.1 shard_map.114
  134.8 3.3 %collective-permute-start.2 = (bf16[2,32,1280]{2,1,0:T(8,128)(2,1)S(1)}, bf16[2,32,1280]{2,1,0:T(8,128)(2,1)S(1)}, u32[]{:S(2)}, u32[]{:S(2)}) collective-permute-start(bf16[2,32,1280]{2,1,0:T(8,128)(2,1)S(1)} %get-tuple-element.41), channel_id=1, source_target_pairs={{0,2},{2,0},{1,3},{3,1},{4,6},{6,4},{5,7},{7,5},{8,10},{10,8},{9,1... | collective-permute-start | bytes 491528 | tf_op jit(solution)/shard_map/ppermute | solution.py:356
  138.1 3.6 %collective-permute-done.2.got = bf16[2,32,1280]{2,1,0:T(8,128)(2,1)S(1)} collective-permute-done((bf16[2,32,1280]{2,1,0:T(8,128)(2,1)S(1)}, bf16[2,32,1280]{2,1,0:T(8,128)(2,1)S(1)}, u32[]{:S(2)}, u32[]{:S(2)}) %collective-permute-start.2) | collective-permute-done | bytes 163872 | tf_op jit(solution)/shard_map/ppermute | solution.py:356
  141.7 0.8 shard_map.115
  142.5 0.8 shard_map.121
  (13 shorter events, 0.0 us)
Async XLA Ops:
  2.2 1.9 %collective-permute-start = (bf16[6,64,640]{2,1,0:T(8,128)(2,1)S(1)}, bf16[6,64,640]{2,1,0:T(8,128)(2,1)S(1)}, u32[]{:S(2)}, u32[]{:S(2)}) collective-permute-start(bf16[6,64,640]{2,1,0:T(8,128)(2,1)S(1)} %get-tuple-element.33), channel_id=1, source_target_pairs={{0,1},{1,0},{2,3},{3,2},{4,5},{5,4},{6,7},{7,6},{8,9},{9,8},{10,11... | collective-permute-start | bytes 1474568 | tf_op jit(solution)/shard_map/ppermute | solution.py:356
  47.5 19.5 %collective-permute-start.1 = (bf16[32,152,256]{2,1,0:T(8,128)(2,1)S(1)}, bf16[32,152,256]{2,1,0:T(8,128)(2,1)}, u32[]{:S(2)}, u32[]{:S(2)}) collective-permute-start(bf16[32,152,256]{2,1,0:T(8,128)(2,1)S(1)} %all_to_all.20.mine), channel_id=1, source_target_pairs={{0,1},{1,0},{2,3},{3,2},{4,5},{5,4},{6,7},{7,6},{8,9},{9,8},{10,11... | collective-permute-start | bytes 7471112 | tf_op jit(solution)/shard_map/ppermute | solution.py:356
  47.5 6.7 %collective-permute-start.3 = (bf16[32,1280]{1,0:T(8,128)(2,1)S(1)}, bf16[32,1280]{1,0:T(8,128)(2,1)S(1)}, u32[]{:S(2)}, u32[]{:S(2)}) collective-permute-start(bf16[32,1280]{1,0:T(8,128)(2,1)S(1)} %get-tuple-element.45), channel_id=1, source_target_pairs={{0,2},{2,0},{1,3},{3,1},{4,6},{6,4},{5,7},{7,5},{8,10},{10,8},{9,1... | collective-permute-start | bytes 245768 | tf_op jit(solution)/shard_map/ppermute | solution.py:356
  54.9 23.4 %all-to-all-start.2 = ((bf16[32,16,256]{2,1,0:T(8,128)(2,1)}), bf16[32,16,256]{2,1,0:T(8,128)(2,1)S(1)}, u32[]{:S(2)}, u32[]{:S(2)}) async-start(bf16[32,16,256]{2,1,0:T(8,128)(2,1)} %shard_map.116), calls=%async_computation.2 | async-start | bytes 524288 | tf_op jit(solution)/shard_map/all_to_all | solution.py:352
  65.3 1.6 %copy-start = (bf16[3,2048,256]{2,1,0:T(8,128)(2,1)}, bf16[3,2048,256]{2,1,0:T(8,128)(2,1)S(1)}, u32[]{:S(2)}) copy-start(bf16[3,2048,256]{2,1,0:T(8,128)(2,1)S(1)} %get-tuple-element.51.w_ref) | copy-start | bytes 9437188
  75.9 1.7 %copy-start.2 = (bf16[3,2048,256]{2,1,0:T(8,128)(2,1)}, bf16[3,2048,256]{2,1,0:T(8,128)(2,1)S(1)}, u32[]{:S(2)}) copy-start(bf16[3,2048,256]{2,1,0:T(8,128)(2,1)S(1)} %get-tuple-element.47.w_ref) | copy-start | bytes 9437188
  77.6 0.7 copy-start.4
  78.3 1.9 %copy-start.3 = (bf16[3,2048,256]{2,1,0:T(8,128)(2,1)S(1)}, bf16[3,2048,256]{2,1,0:T(8,128)(2,1)}, u32[]{:S(2)}) copy-start(bf16[3,2048,256]{2,1,0:T(8,128)(2,1)} %copy-done.2) | copy-start | bytes 9437188
  80.2 0.9 copy-start.5
  81.1 6.0 %copy-start.1 = (bf16[3,2048,256]{2,1,0:T(8,128)(2,1)S(1)}, bf16[3,2048,256]{2,1,0:T(8,128)(2,1)}, u32[]{:S(2)}) copy-start(bf16[3,2048,256]{2,1,0:T(8,128)(2,1)} %copy-done) | copy-start | bytes 9437188
  81.1 6.0 %copy-start.6 = (bf16[3,256,128]{2,1,0:T(8,128)(2,1)S(1)}, bf16[3,256,128]{2,1,0:T(8,128)(2,1)}, u32[]{:S(2)}) copy-start(bf16[3,256,128]{2,1,0:T(8,128)(2,1)} %copy-done.4) | copy-start | bytes 589828
  87.0 4.0 %collective-permute-start.4 = (bf16[32,64,256]{2,1,0:T(8,128)(2,1)S(1)}, bf16[32,64,256]{2,1,0:T(8,128)(2,1)S(1)}, u32[]{:S(2)}, u32[]{:S(2)}) collective-permute-start(bf16[32,64,256]{2,1,0:T(8,128)(2,1)S(1)} %get-tuple-element.53), channel_id=1, source_target_pairs={{0,1},{1,0},{2,3},{3,2},{4,5},{5,4},{6,7},{7,6},{8,9},{9,8},{10,11... | collective-permute-start | bytes 3145736 | tf_op jit(solution)/shard_map/ppermute | solution.py:356
  121.3 13.5 %all-to-all-start.1 = ((bf16[32,24,256]{2,1,0:T(8,128)(2,1)}), bf16[32,24,256]{2,1,0:T(8,128)(2,1)S(1)}, u32[]{:S(2)}, u32[]{:S(2)}) async-start(bf16[32,24,256]{2,1,0:T(8,128)(2,1)} %get-tuple-element.39), calls=%async_computation.1 | async-start | bytes 786432 | tf_op jit(solution)/shard_map/all_to_all | solution.py:352
  125.6 16.9 %collective-permute-start.5 = (bf16[3,64,640]{2,1,0:T(8,128)(2,1)S(1)}, bf16[3,64,640]{2,1,0:T(8,128)(2,1)S(1)}, u32[]{:S(2)}, u32[]{:S(2)}) collective-permute-start(bf16[3,64,640]{2,1,0:T(8,128)(2,1)S(1)} %get-tuple-element.55), channel_id=1, source_target_pairs={{0,1},{1,0},{2,3},{3,2},{4,5},{5,4},{6,7},{7,6},{8,9},{9,8},{10,11... | collective-permute-start | bytes 737288 | tf_op jit(solution)/shard_map/ppermute | solution.py:356
  134.8 6.9 %collective-permute-start.2 = (bf16[2,32,1280]{2,1,0:T(8,128)(2,1)S(1)}, bf16[2,32,1280]{2,1,0:T(8,128)(2,1)S(1)}, u32[]{:S(2)}, u32[]{:S(2)}) collective-permute-start(bf16[2,32,1280]{2,1,0:T(8,128)(2,1)S(1)} %get-tuple-element.41), channel_id=1, source_target_pairs={{0,2},{2,0},{1,3},{3,1},{4,6},{6,4},{5,7},{7,5},{8,10},{10,8},{9,1... | collective-permute-start | bytes 491528 | tf_op jit(solution)/shard_map/ppermute | solution.py:356

commit v4 on v3

v4 whole, which is shorter than its diff:
```python
import math

import jax
import jax.numpy as jnp
from jax import lax
from jax.experimental import pallas as pl
from jax.experimental.pallas import tpu as pltpu
from jax.sharding import Mesh, PartitionSpec as P


BF = jnp.bfloat16
F32 = jnp.float32
HD = 128
LOSS = 64.0
PARTS = 3
PIECE = 24
EIGHTS = ((0, 1, 4), (2, 5, None), (3, 6, 7))
KROWS = 64
QT = 256
SUB = 512
INV = 1.0 / math.sqrt(HD)
EXP_SCALE = INV * math.log2(math.e)
VMEM = pl.BlockSpec(memory_space=pltpu.VMEM)
HBM = pl.BlockSpec(memory_space=pltpu.HBM)
ANY = pl.BlockSpec(memory_space=pl.ANY)


def call(body, outs, ins, limit, scratch=(), flops=0, exps=0, moved=1_000_000):
    return pl.pallas_call(
        body,
        out_shape=[
            pltpu.HBM(one.shape, one.dtype) if place is HBM else one for one, place in outs
        ],
        in_specs=ins,
        out_specs=[place for _, place in outs],
        scratch_shapes=list(scratch),
        compiler_params=pltpu.CompilerParams(vmem_limit_bytes=limit * 1024 * 1024),
        cost_estimate=pl.CostEstimate(flops=flops, bytes_accessed=moved, transcendentals=exps),
    )


def nt(a, b):
    return lax.dot_general(a, b, (((1,), (1,)), ((), ())), preferred_element_type=F32)


def nn(a, b):
    return lax.dot_general(a, b, (((1,), (0,)), ((), ())), preferred_element_type=F32)


def core():
    return lax.axis_index("c")


def group():
    return lax.axis_index("zh")


def split_tokens(*refs):
    *arrays, gap, sent, kept, gap_here, sems, gap_sem = refs
    copies = []
    for at, ref in enumerate(arrays):
        for half in range(2):
            for side, (dst, who) in enumerate(((sent, 1 - core()), (kept, core()))):
                low = pl.multiple_of(64 * half + 32 * who, 32)
                copies.append(
                    pltpu.make_async_copy(
                        ref.at[pl.ds(low, 32), :],
                        dst.at[at, 32 * half : 32 * half + 32, :],
                        sems.at[at, half, side],
                    )
                )
    copies.append(pltpu.make_async_copy(gap, gap_here, gap_sem))
    for copy in copies:
        copy.start()
    for copy in copies:
        copy.wait()


def pack_heads(kept, got, gap, out, e_ref):
    e_ref[core()] = kept[...]
    e_ref[1 - core()] = got[...]
    half = e_ref.shape[3] // HD
    zero = jnp.zeros((8, HD), BF)
    for chip in range(out.shape[0]):
        head, part = chip // PARTS, chip % PARTS
        if head >= 2 * half:
            out[chip] = jnp.zeros(out.shape[1:], BF)
            continue
        at, cols = head // half, slice((head % half) * HD, (head % half + 1) * HD)
        out[chip, 0:64, 0:HD] = e_ref[at, 1, :, cols]
        out[chip, 0:64, HD:] = e_ref[at, 4, :, cols]
        out[chip, 64:128, 0:HD] = e_ref[at, 2, :, cols]
        out[chip, 64:128, HD:] = e_ref[at, 5, :, cols]
        for to, eight in enumerate(EIGHTS[part]):
            rows = slice(128 + 8 * to, 136 + 8 * to)
            for side, array in ((0, 0), (1, 3)):
                lanes = slice(side * HD, side * HD + HD)
                if eight is None:
                    out[chip, rows, lanes] = zero
                else:
                    out[chip, rows, lanes] = e_ref[at, array, 8 * eight : 8 * eight + 8, cols]
    for mine in range(2):

        @pl.when(group() == mine)
        def _():
            for chip in range(2 * half * PARTS):
                head, part = chip // PARTS, chip % PARTS
                for place in range(2):
                    eight = EIGHTS[part][mine + place]
                    rows = slice(152 + 8 * place, 160 + 8 * place)
                    for other in range(2):
                        lanes = slice(other * HD, other * HD + HD)
                        low = (2 * half * other + head) * HD
                        if eight is None or eight // 4 != mine:
                            out[chip, rows, lanes] = zero
                        else:
                            at = 8 * (eight % 4)
                            out[chip, rows, lanes] = gap[at : at + 8, low : low + HD]


def split_gaps(mine, sent, kept, sems):
    copies = []
    for at, (dst, who) in enumerate(((sent, 1 - group()), (kept, group()))):
        lanes = pl.ds(pl.multiple_of(who * HD, HD), HD)
        copies.append(pltpu.make_async_copy(mine.at[:, 152:168, lanes], dst, sems.at[at]))
    for copy in copies:
        copy.start()
    for copy in copies:
        copy.wait()


def fold(x, op):
    return op(x.reshape(x.shape[0] // 8, 8, x.shape[1]), axis=0)


def forward(keys, q_ref, qq_ref, w_ref, m_ref, sums_ref, acc_ref, s_ref, wt_ref, kk_ref, vt_ref,
            ready=None, done=None):
    tiles = q_ref.shape[0]
    per = SUB // KROWS
    subs = kk_ref.shape[0] // SUB
    ats = [slice(SUB * i, SUB * i + SUB) for i in range(subs)]

    def scores(t, i, peak):
        s = nt(kk_ref[ats[i], 0:HD], q_ref[t])
        s_ref[t % 2, ats[i], :] = s
        return jnp.maximum(peak, fold(s, jnp.max))

    def values(t, i):
        both = nn(vt_ref[:, ats[i]], w_ref[t, ats[i], :])
        tan = nn(vt_ref[0:HD, ats[i]], wt_ref[t % 2, ats[i], :]) * INV
        if i == 0:
            acc_ref[t, 0:HD, :] = both[0:HD]
            acc_ref[t, HD:, :] = both[HD:] + tan
        else:
            acc_ref[t, 0:HD, :] += both[0:HD]
            acc_ref[t, HD:, :] += both[HD:] + tan

    lowest = jnp.full((8, QT), -jnp.inf, F32)
    peak = lowest
    for i in range(subs):
        if ready is not None:
            ready(i)
        slots = slice(per * i, per * i + per)
        kk_ref[ats[i], :] = keys[slots, 0:KROWS, :].reshape(SUB, 2 * HD)
        v = keys[slots, KROWS : 2 * KROWS, :].reshape(SUB, 2 * HD)
        vt_ref[:, ats[i]] = v.astype(F32).T.astype(BF)
        peak = scores(0, i, peak)
    for t in range(tiles):
        top = jnp.max(peak, axis=0, keepdims=True)
        m_ref[t] = top
        peak = lowest
        total = jnp.zeros((8, QT), F32)
        tan_total = jnp.zeros((8, QT), F32)
        for i in range(subs):
            w = jnp.exp2((s_ref[t % 2, ats[i], :] - top) * EXP_SCALE)
            wt = w * nt(kk_ref[ats[i], :], qq_ref[t])
            total = total + fold(w, jnp.sum)
            tan_total = tan_total + fold(wt, jnp.sum)
            w_ref[t, ats[i], :] = w.astype(BF)
            wt_ref[t % 2, ats[i], :] = wt.astype(BF)
            if t + 1 < tiles:
                peak = scores(t + 1, i, peak)
            if t > 0:
                values(t - 1, i)
        sums_ref[t, 0:1, :] = jnp.sum(total, axis=0, keepdims=True)
        sums_ref[t, 1:2, :] = jnp.sum(tan_total, axis=0, keepdims=True) * INV
        if done is not None:
            done(t)
    for i in range(subs):
        values(tiles - 1, i)


def forward_mine(mine, q_ref, qq_ref, w_hbm, m_ref, sums_ref, acc_ref, stage, w_ref, sems, *scratch):
    for s in range(mine.shape[0]):
        stage[PIECE * s : PIECE * s + PIECE, :] = mine[s, 128:152, :].astype(F32)
    tiles = q_ref.shape[0]
    for t in range(tiles):
        rows = slice(QT * t, QT * t + QT)
        q_ref[t] = stage[rows, 0:HD].astype(BF)
        qq_ref[t, :, 0:HD] = stage[rows, HD:].astype(BF)
        qq_ref[t, :, HD:] = stage[rows, 0:HD].astype(BF)
    copies = [pltpu.make_async_copy(w_ref.at[t], w_hbm.at[t], sems.at[t]) for t in range(tiles)]
    forward(
        mine, q_ref, qq_ref, w_ref, m_ref, sums_ref, acc_ref, *scratch,
        done=lambda t: copies[t].start(),
    )
    for copy in copies:
        copy.wait()


def backward(keys, q_ref, cot_ref, inner_ref, w_ref, share_ref, side, dst, dq, kt_ref, ds_ref, p_ref,
             ready=None):
    tiles = q_ref.shape[0]
    per = SUB // KROWS
    subs = ds_ref.shape[0]
    q_all = q_ref[...].reshape(tiles * QT, HD)
    for i in range(subs):
        if ready is not None:
            ready(i)
        at, slots = slice(SUB * i, SUB * i + SUB), slice(per * i, per * i + per)
        k = keys[slots, 0:KROWS, 0:HD].reshape(SUB, HD)
        v = keys[slots, KROWS : 2 * KROWS, 0:HD].reshape(SUB, HD)
        kt_ref[i] = k.astype(F32).T.astype(BF)
        for t in range(tiles):
            cols = slice(QT * t, QT * t + QT)
            p = w_ref[t, at, :].astype(F32) * share_ref[side, t]
            ds = p * (nt(v, cot_ref[cols, :]) - inner_ref[t])
            p_ref[:, cols] = p.astype(BF)
            ds_ref[i, :, cols] = ds.astype(BF)
        dk = nn(ds_ref[i], q_all) * INV
        dv = nn(p_ref[...], cot_ref[...])
        dst[slots, 0:KROWS, 0:HD] = dk.astype(BF).reshape(per, KROWS, HD)
        dst[slots, 0:KROWS, HD:] = dv.astype(BF).reshape(per, KROWS, HD)
    for i in range(subs):
        dq = dq + nn(kt_ref[i], ds_ref[i])
    return dq


def theirs_both_ways(
    theirs_hbm, q_ref, qq_ref, m1_ref, sums1_ref, acc1_ref, gap_kept, gap_got, mask,
    dst, pieces, cot_ref, inner_ref, dq_ref, share_ref,
    theirs, sems, w_ref, m_ref, sums_ref, acc_ref, g_ref, stage, kt_ref, ds_ref, p_ref, *scratch
):
    per = SUB // KROWS
    copies = [
        pltpu.make_async_copy(
            theirs_hbm.at[per * i : per * i + per, 0:128, :],
            theirs.at[per * i : per * i + per],
            sems.at[i],
        )
        for i in range(ds_ref.shape[0])
    ]
    for copy in copies:
        copy.start()
    forward(
        theirs, q_ref, qq_ref, w_ref, m_ref, sums_ref, acc_ref, *scratch,
        ready=lambda i: copies[i].wait(),
    )
    g_ref[group()] = gap_kept[...]
    g_ref[1 - group()] = gap_got[...]
    for s in range(gap_kept.shape[0]):
        low = PIECE * s
        first, second = g_ref[0, s].astype(F32), g_ref[1, s].astype(F32)
        stage[low : low + 8, 0:HD] = first[0:8]
        stage[low + 8 : low + 16, 0:HD] = first[8:16] + second[0:8]
        stage[low + 16 : low + 24, 0:HD] = second[8:16]
    for t in range(q_ref.shape[0]):
        rows = slice(QT * t, QT * t + QT)
        top = jnp.maximum(m1_ref[t], m_ref[t])
        f1 = jnp.exp2((m1_ref[t] - top) * EXP_SCALE)
        f2 = jnp.exp2((m_ref[t] - top) * EXP_SCALE)
        sums = sums1_ref[t] * f1 + sums_ref[t] * f2
        inverse = 1.0 / sums[0:1]
        s1, s2 = f1 * inverse, f2 * inverse
        share_ref[0, t] = s1
        share_ref[1, t] = s2
        both = acc1_ref[t] * s1 + acc_ref[t] * s2
        tangent = both[HD:] - (sums[1:2] * inverse) * both[0:HD]
        primal = both[0:HD].astype(BF).astype(F32)
        tangent = tangent.astype(BF).astype(F32)
        cot = (LOSS * (stage[rows, 0:HD].T + tangent)) * mask[:, rows]
        cot = cot.astype(BF).astype(F32)
        inner_ref[t] = jnp.sum(cot * primal, axis=0, keepdims=True)
        cot_ref[rows, :] = cot.T.astype(BF)
        stage[rows, 0:HD] = primal.T
        stage[rows, HD:] = tangent.T
    for s in range(pieces.shape[0]):
        pieces[s] = stage[PIECE * s : PIECE * s + PIECE, :].astype(BF)
    dq_ref[...] = backward(
        theirs, q_ref, cot_ref, inner_ref, w_ref, share_ref, 1, dst, jnp.zeros(dq_ref.shape, F32),
        kt_ref, ds_ref, p_ref,
    )


def backward_mine(
    mine, q_ref, cot_ref, inner_ref, w_hbm, share_ref, dq_ref, out, w_ref, sems, stage, *scratch
):
    ats = [slice(SUB * i, SUB * i + SUB) for i in range(w_ref.shape[1] // SUB)]
    copies = [
        pltpu.make_async_copy(w_hbm.at[:, at, :], w_ref.at[:, at, :], sems.at[i])
        for i, at in enumerate(ats)
    ]
    for copy in copies:
        copy.start()
    dq = backward(
        mine, q_ref, cot_ref, inner_ref, w_ref, share_ref, 0, out, dq_ref[...], *scratch,
        ready=lambda i: copies[i].wait(),
    )
    stage[...] = (dq * INV).T
    for s in range(out.shape[0]):
        low = PIECE * s
        out[s, 64:80, 0:HD] = stage[low : low + 16, :].astype(BF)
        out[s, 64:72, HD:] = stage[low + 16 : low + 24, :].astype(BF)
        out[s, 72:80, HD:] = jnp.zeros((8, HD), BF)


def gather_out(mine, pieces, theirs, out):
    for s in range(out.shape[0]):
        out[s, 0:KROWS, :] = (
            mine[s, 0:KROWS, :].astype(F32) + theirs[s].astype(F32)
        ).astype(BF)
        out[s, 64:88, :] = pieces[s]
        out[s, 88:104, :] = mine[s, 64:80, :]


def unpack_heads(r_ref, sent, kept, o_sent, o_kept, f_ref, o_ref):
    half = f_ref.shape[3] // HD
    for head in range(2 * half):
        at, cols = head // half, slice((head % half) * HD, (head % half + 1) * HD)
        first = PARTS * head
        both = sum(r_ref[first + part, 0:KROWS, :].astype(F32) for part in range(PARTS))
        f_ref[at, 1, :, cols] = both[:, 0:HD].astype(BF)
        f_ref[at, 2, :, cols] = both[:, HD:].astype(BF)
        ocols = slice(head * HD, head * HD + HD)
        for part in range(PARTS):
            for place, eight in enumerate(EIGHTS[part]):
                if eight is None:
                    continue
                row, low = 8 * eight, 8 * place
                lanes = slice(0, HD) if place < 2 else slice(HD, 2 * HD)
                from_row = 88 + low % 16
                f_ref[at, 0, row : row + 8, cols] = r_ref[first + part, from_row : from_row + 8, lanes]
                for side in range(2):
                    o_ref[row // 32, side, row % 32 : row % 32 + 8, ocols] = r_ref[
                        first + part, 64 + low : 72 + low, side * HD : side * HD + HD
                    ]
    sent[...] = f_ref[1 - core()]
    kept[...] = f_ref[core()]
    o_sent[...] = o_ref[1 - group()]
    o_kept[...] = o_ref[group()]


def finish(kept, got, o_kept, o_got, primal, tangent, dq, dk, dv):
    for at, ref in enumerate((dq, dk, dv)):
        for half in range(2):
            rows = slice(32 * half, 32 * half + 32)
            for piece, who in ((kept, core()), (got, 1 - core())):
                low = pl.multiple_of(64 * half + 32 * who, 32)
                ref[pl.ds(low, 32), :] = piece[at, rows, :]
    wide = o_kept.shape[2]
    for side, ref in enumerate((primal, tangent)):
        for piece, who in ((o_kept, group()), (o_got, 1 - group())):
            ref[:, pl.ds(pl.multiple_of(wide * who, HD), wide)] = piece[side]


def shape(*dims, dtype=BF):
    return jax.ShapeDtypeStruct(dims, dtype)


SWAP = [(0, 1), (1, 0)]
BLOCK_AXES = ("zl", "y", "x")


def exchange(array):
    return lax.all_to_all(array, BLOCK_AXES, 0, 0, tiled=True)


def swap(array, axis):
    return lax.ppermute(array, axis, SWAP)


def attention(chips, mine, mask):
    length, tiles = chips * KROWS, chips * PIECE // QT
    rows, subs = tiles * QT, length // SUB
    flops = 2 * length * rows * HD
    gpiece = shape(chips, 16, HD)
    gap_sent, gap_kept = call(
        split_gaps, [(gpiece, VMEM), (gpiece, VMEM)], [ANY], 2, (pltpu.SemaphoreType.DMA((2,)),),
        moved=500_000,
    )(mine)
    gap_got = swap(gap_sent, "zh")
    theirs = swap(mine, "c")
    q, qq = shape(tiles, QT, HD), shape(tiles, QT, 2 * HD)
    w = shape(tiles, length, QT)
    stats, sums, acc = (shape(tiles, n, QT, dtype=F32) for n in (1, 2, 2 * HD))
    tiles_of = (pltpu.VMEM(w.shape, BF), pltpu.SemaphoreType.DMA((tiles,)))
    scratch = (
        pltpu.VMEM((2, length, QT), F32),
        pltpu.VMEM((2, length, QT), BF),
        pltpu.VMEM((length, 2 * HD), BF),
        pltpu.VMEM((2 * HD, length), BF),
    )
    back_scratch = (
        pltpu.VMEM((subs, HD, SUB), BF),
        pltpu.VMEM((subs, SUB, rows), BF),
        pltpu.VMEM((SUB, rows), BF),
    )
    stage = pltpu.VMEM((rows, 2 * HD), F32)
    q, qq, w1, m1, sums1, acc1 = call(
        forward_mine,
        [(q, VMEM), (qq, VMEM), (w, HBM), (stats, VMEM), (sums, VMEM), (acc, VMEM)],
        [VMEM],
        30,
        (stage,) + tiles_of + scratch,
        6 * flops, length * rows, 7_000_000,
    )(mine)
    key_piece = shape(chips, KROWS, 2 * HD)
    dst, pieces, cot, inner, dq, share = call(
        theirs_both_ways,
        [
            (key_piece, VMEM), (shape(chips, PIECE, 2 * HD), VMEM), (shape(rows, HD), VMEM),
            (stats, VMEM), (shape(HD, rows, dtype=F32), VMEM),
            (shape(2, tiles, 1, QT, dtype=F32), VMEM),
        ],
        [ANY] + [VMEM] * 8,
        30,
        (
            pltpu.VMEM((chips, 2 * KROWS, 2 * HD), BF), pltpu.SemaphoreType.DMA((subs,)),
            pltpu.VMEM(w.shape, BF), pltpu.VMEM(stats.shape, F32), pltpu.VMEM(sums.shape, F32),
            pltpu.VMEM(acc.shape, F32), pltpu.VMEM((2,) + gpiece.shape, BF), stage,
        ) + back_scratch + scratch,
        14 * flops, length * rows, 7_000_000,
    )(theirs, q, qq, m1, sums1, acc1, gap_kept, gap_got, mask)
    partner = swap(dst, "c")
    out = call(
        backward_mine,
        [(shape(chips, KROWS + 16, 2 * HD), VMEM)],
        [VMEM] * 4 + [HBM] + [VMEM] * 2,
        30,
        (
            pltpu.VMEM(w.shape, BF), pltpu.SemaphoreType.DMA((subs,)), pltpu.VMEM((rows, HD), F32),
        ) + back_scratch,
        8 * flops, 0, 7_000_000,
    )(mine, q, cot, inner, w1, share, dq)[0]
    return call(gather_out, [(shape(chips, 104, 2 * HD), VMEM)], [VMEM] * 3, 8)(out, pieces, partner)[0]


def per_device(q, k, v, tq, tk, tv, gap):
    chips = lax.axis_size(BLOCK_AXES)
    local, feat = q.shape
    wide = gap.shape[1] // 2
    piece = shape(6, KROWS, feat)
    arrays = (q, k, v, tq, tk, tv, gap)
    sent, kept, gap_here = call(
        split_tokens,
        [(piece, VMEM), (piece, VMEM), (shape(*gap.shape), VMEM)],
        [HBM] * 7,
        4,
        (pltpu.SemaphoreType.DMA((6, 2, 2)), pltpu.SemaphoreType.DMA),
    )(*(pltpu.with_memory_space_constraint(one, pltpu.HBM) for one in arrays))
    got = swap(sent, "c")
    packed = call(
        pack_heads,
        [(shape(chips, 168, 2 * HD), VMEM)],
        [VMEM] * 3,
        8,
        (pltpu.VMEM((2,) + piece.shape, BF),),
    )(kept, got, gap_here)[0]
    mine = exchange(packed)

    rows = chips * PIECE
    part = lax.axis_index(BLOCK_AXES) % PARTS
    short = (jnp.arange(rows) % PIECE >= 16) & (part == 1)
    mask = jnp.where(short, 0.0, 1.0).astype(F32)[None]
    back = exchange(attention(chips, mine, mask))

    opiece, fpiece = shape(2, 32, wide), shape(3, KROWS, feat)
    sent, kept, o_sent, o_kept = call(
        unpack_heads,
        [(fpiece, VMEM), (fpiece, VMEM), (opiece, VMEM), (opiece, VMEM)],
        [VMEM],
        8,
        (pltpu.VMEM((2,) + fpiece.shape, BF), pltpu.VMEM((2,) + opiece.shape, BF)),
    )(back)
    o_got = swap(o_sent, "zh")
    got = swap(sent, "c")
    small, large = shape(32, 2 * wide), shape(local, feat)
    return tuple(
        call(finish, [(small, VMEM)] * 2 + [(large, VMEM)] * 3, [VMEM] * 4, 8)(
            kept, got, o_kept, o_got
        )
    )


def solution(mesh):
    sizes = (2, 4, 4, 2, 2)
    inner = Mesh(mesh.devices.reshape(sizes), BLOCK_AXES + ("zh", "c"))
    both = P(BLOCK_AXES, ("zh", "c"))
    rows = P(BLOCK_AXES + ("zh", "c"), None)

    return jax.shard_map(
        per_device,
        mesh=inner,
        in_specs=(both,) * 6 + (rows,),
        out_specs=(rows, rows, both, both, both),
        check_vma=False,
    )
```

time: 144 us -> 111 us (0.77)
  the two profiles are of different devices: /device:TPU:0 before, /device:TPU:1 now
where the time goes in v4:
time: 111 us; the launch traced here: 110 us
  blocking collectives  69.2 us (62%)
  Pallas kernels  22.4 us (20%)
  starting transfers between devices  11.8 us (11%)
  waiting for transfers between devices  6.14 us (6%)
    all_to_all x2, blocking collectives, exchange(): return lax.all_to_all(array, BLOCK_AXES, 0, 0, tiled=True)  69.2 us
    ppermute x6, starting transfers between devices, swap(): return lax.ppermute(array, axis, SWAP)  11.8 us
    pallas_call x1, Pallas kernels, attention(): call(theirs_both_ways, [(key_piece, VMEM), (shape(chips, PIECE, 2 * HD),...  9.67 us
    ppermute x6, waiting for transfers between devices, swap(): return lax.ppermute(array, axis, SWAP)  6.14 us
    pallas_call x1, Pallas kernels, attention(): call(backward_mine, [(shape(chips, KROWS + 16, 2 * HD), VMEM)], [VMEM] *...  4.61 us
    pallas_call x1, Pallas kernels, attention(): call(forward_mine, [(q, VMEM), (qq, VMEM), (w, HBM), (stats, VMEM), (sums...  4.59 us
  transfers between devices with their start and end apart: 6, of which 2 were waited for; matrix products, arithmetic and copies ran while one was open for 0% of the time, Pallas kernels for 8%

profile of v4, /device:TPU:1, one launch (start us, length us, event | category | flops | bytes accessed | tf_op | source)
XLA Modules:
  0.0 110.3 jit_solution(7909853203857329105)
XLA Ops:
  0.6 1.6 %shard_map.110 = (bf16[6,64,640]{2,1,0:T(8,128)(2,1)S(1)}, bf16[6,64,640]{2,1,0:T(8,128)(2,1)S(1)}, bf16[32,2560]{1,0:T(8,128)(2,1)S(1)}) custom-call(bf16[128,640]{1,0:T(8,128)(2,1)} %refs_0_.1, bf16[128,640]{1,0:T(8,128)(2,1)} %refs_1_.1, bf16[128,640]{1,0:T(8,128)(2,1)} %refs_2_.1, bf16[128,640]{1,0:T(8,128)(2,1)} %refs_3_.1, bf16[128,640]{1,0:T(8,128)(2,1)} %refs_4_.1, ...), custom_call_target="tpu_custom_call" | custom-call | bytes 1000000 | tf_op jit(solution)/shard_map/pallas_call | solution.py:454
  2.2 1.5 %collective-permute-start = (bf16[6,64,640]{2,1,0:T(8,128)(2,1)S(1)}, bf16[6,64,640]{2,1,0:T(8,128)(2,1)S(1)}, u32[]{:S(2)}, u32[]{:S(2)}) collective-permute-start(bf16[6,64,640]{2,1,0:T(8,128)(2,1)S(1)} %get-tuple-element.27), channel_id=1, source_target_pairs={{0,1},{1,0},{2,3},{3,2},{4,5},{5,4},{6,7},{7,6},{8,9},{9,8},{10,11... | collective-permute-start | bytes 1474568 | tf_op jit(solution)/shard_map/ppermute | solution.py:379
  3.7 1.5 %collective-permute-done.got = bf16[6,64,640]{2,1,0:T(8,128)(2,1)S(1)} collective-permute-done((bf16[6,64,640]{2,1,0:T(8,128)(2,1)S(1)}, bf16[6,64,640]{2,1,0:T(8,128)(2,1)S(1)}, u32[]{:S(2)}, u32[]{:S(2)}) %collective-permute-start) | collective-permute-done | bytes 491552 | tf_op jit(solution)/shard_map/ppermute | solution.py:379
  5.2 0.4 shard_map.111
  5.6 42.3 %all_to_all.10.mine = bf16[32,168,256]{2,1,0:T(8,128)(2,1)S(1)} all-to-all(bf16[32,168,256]{2,1,0:T(8,128)(2,1)S(1)} %shard_map.111), channel_id=1, replica_groups=mesh['zl'=2,'y'=4,'x'=4,'zh'=2,'c'=2] {'zl','y','x'}, dimensions={0} | all-to-all | bytes 5505024 | tf_op jit(solution)/shard_map/all_to_all | solution.py:375
  47.9 2.0 %collective-permute-start.1 = (bf16[32,168,256]{2,1,0:T(8,128)(2,1)S(1)}, bf16[32,168,256]{2,1,0:T(8,128)(2,1)}, u32[]{:S(2)}, u32[]{:S(2)}) collective-permute-start(bf16[32,168,256]{2,1,0:T(8,128)(2,1)S(1)} %all_to_all.10.mine), channel_id=1, source_target_pairs={{0,1},{1,0},{2,3},{3,2},{4,5},{5,4},{6,7},{7,6},{8,9},{9,8},{10,11... | collective-permute-start | bytes 8257544 | tf_op jit(solution)/shard_map/ppermute | solution.py:379
  50.0 0.1 shard_map.113
  50.1 3.4 %collective-permute-start.2 = (bf16[32,16,128]{2,1,0:T(8,128)(2,1)S(1)}, bf16[32,16,128]{2,1,0:T(8,128)(2,1)S(1)}, u32[]{:S(2)}, u32[]{:S(2)}) collective-permute-start(bf16[32,16,128]{2,1,0:T(8,128)(2,1)S(1)} %get-tuple-element.35), channel_id=1, source_target_pairs={{0,2},{2,0},{1,3},{3,1},{4,6},{6,4},{5,7},{7,5},{8,10},{10,8},{9,1... | collective-permute-start | bytes 393224 | tf_op jit(solution)/shard_map/ppermute | solution.py:379
  53.5 4.6 %shard_map.112 = (bf16[3,256,128]{2,1,0:T(8,128)(2,1)S(1)}, bf16[3,256,256]{2,1,0:T(8,128)(2,1)S(1)}, bf16[3,2048,256]{2,1,0:T(8,128)(2,1)}, f32[3,1,256]{2,1,0:...) custom-call(bf16[32,168,256]{2,1,0:T(8,128)(2,1)S(1)} %all_to_all.10.mine), custom_call_target="tpu_custom_call" | custom-call | flops 2415919104 | bytes 7000000 | tf_op jit(solution)/shard_map/pallas_call | solution.py:409
  58.1 0.0 collective-permute-done.2.gap_got
  58.1 0.0 collective-permute-done.1.theirs_hbm
  58.1 0.0 copy-start
  58.1 9.7 %shard_map.114 = (bf16[32,64,256]{2,1,0:T(8,128)(2,1)S(1)}, bf16[32,24,256]{2,1,0:T(8,128)(2,1)S(1)}, bf16[768,128]{1,0:T(8,128)(2,1)S(1)}, f32[3,1,256]{2,1,0:T...) custom-call(bf16[32,168,256]{2,1,0:T(8,128)(2,1)} %collective-permute-done.1.theirs_hbm, ...), custom_call_target="tpu_custom_call" | custom-call | flops 5637144576 | bytes 7000000 | tf_op jit(solution)/shard_map/pallas_call | solution.py:418
  67.8 0.4 collective-permute-start.3
  68.1 0.0 copy-done
  68.1 4.6 %shard_map.115.mine = bf16[32,80,256]{2,1,0:T(8,128)(2,1)S(1)} custom-call(bf16[32,168,256]{2,1,0:T(8,128)(2,1)S(1)} %all_to_all.10.mine, bf16[3,256,128]{2,1,0:T(8,128)(2,1)S(1)} %get-tuple-element.29.q_ref, bf16[768,128]{1,0:T(8,128)(2,1)S(1)} %get-tuple-element.36.cot_ref, f32[3,1,256]{2,1,0:T(1,128)S(1)} %get-tuple-element.37.inner_ref, ...), custom_call_target="tpu_custom_call" | custom-call | flops 3221225472 | bytes 7000000 | tf_op jit(solution)/shard_map/pallas_call | solution.py:435
  72.7 0.0 collective-permute-done.3.theirs
  72.8 0.3 shard_map.116
  73.0 26.9 %all_to_all.11.r_ref = bf16[32,104,256]{2,1,0:T(8,128)(2,1)S(1)} all-to-all(bf16[32,104,256]{2,1,0:T(8,128)(2,1)S(1)} %shard_map.116), channel_id=1, replica_groups=mesh['zl'=2,'y'=4,'x'=4,'zh'=2,'c'=2] {'zl','y','x'}, dimensions={0} | all-to-all | bytes 3407872 | tf_op jit(solution)/shard_map/all_to_all | solution.py:375
  99.9 0.2 shard_map.117
  100.1 2.1 %collective-permute-start.4 = (bf16[3,64,640]{2,1,0:T(8,128)(2,1)S(1)}, bf16[3,64,640]{2,1,0:T(8,128)(2,1)S(1)}, u32[]{:S(2)}, u32[]{:S(2)}) collective-permute-start(bf16[3,64,640]{2,1,0:T(8,128)(2,1)S(1)} %get-tuple-element.44), channel_id=1, source_target_pairs={{0,1},{1,0},{2,3},{3,2},{4,5},{5,4},{6,7},{7,6},{8,9},{9,8},{10,11... | collective-permute-start | bytes 737288 | tf_op jit(solution)/shard_map/ppermute | solution.py:379
  102.2 2.5 %collective-permute-start.5 = (bf16[2,32,1280]{2,1,0:T(8,128)(2,1)S(1)}, bf16[2,32,1280]{2,1,0:T(8,128)(2,1)S(1)}, u32[]{:S(2)}, u32[]{:S(2)}) collective-permute-start(bf16[2,32,1280]{2,1,0:T(8,128)(2,1)S(1)} %get-tuple-element.46), channel_id=1, source_target_pairs={{0,2},{2,0},{1,3},{3,1},{4,6},{6,4},{5,7},{7,5},{8,10},{10,8},{9,1... | collective-permute-start | bytes 491528 | tf_op jit(solution)/shard_map/ppermute | solution.py:379
  104.7 4.6 %collective-permute-done.5.o_got = bf16[2,32,1280]{2,1,0:T(8,128)(2,1)S(1)} collective-permute-done((bf16[2,32,1280]{2,1,0:T(8,128)(2,1)S(1)}, bf16[2,32,1280]{2,1,0:T(8,128)(2,1)S(1)}, u32[]{:S(2)}, u32[]{:S(2)}) %collective-permute-start.5) | collective-permute-done | bytes 163872 | tf_op jit(solution)/shard_map/ppermute | solution.py:379
  109.4 0.0 collective-permute-done.4.got
  109.4 1.0 shard_map.118
  (1 shorter events, 0.0 us)
Async XLA Ops:
  2.2 3.0 %collective-permute-start = (bf16[6,64,640]{2,1,0:T(8,128)(2,1)S(1)}, bf16[6,64,640]{2,1,0:T(8,128)(2,1)S(1)}, u32[]{:S(2)}, u32[]{:S(2)}) collective-permute-start(bf16[6,64,640]{2,1,0:T(8,128)(2,1)S(1)} %get-tuple-element.27), channel_id=1, source_target_pairs={{0,1},{1,0},{2,3},{3,2},{4,5},{5,4},{6,7},{7,6},{8,9},{9,8},{10,11... | collective-permute-start | bytes 1474568 | tf_op jit(solution)/shard_map/ppermute | solution.py:379
  47.9 10.1 %collective-permute-start.1 = (bf16[32,168,256]{2,1,0:T(8,128)(2,1)S(1)}, bf16[32,168,256]{2,1,0:T(8,128)(2,1)}, u32[]{:S(2)}, u32[]{:S(2)}) collective-permute-start(bf16[32,168,256]{2,1,0:T(8,128)(2,1)S(1)} %all_to_all.10.mine), channel_id=1, source_target_pairs={{0,1},{1,0},{2,3},{3,2},{4,5},{5,4},{6,7},{7,6},{8,9},{9,8},{10,11... | collective-permute-start | bytes 8257544 | tf_op jit(solution)/shard_map/ppermute | solution.py:379
  50.1 8.0 %collective-permute-start.2 = (bf16[32,16,128]{2,1,0:T(8,128)(2,1)S(1)}, bf16[32,16,128]{2,1,0:T(8,128)(2,1)S(1)}, u32[]{:S(2)}, u32[]{:S(2)}) collective-permute-start(bf16[32,16,128]{2,1,0:T(8,128)(2,1)S(1)} %get-tuple-element.35), channel_id=1, source_target_pairs={{0,2},{2,0},{1,3},{3,1},{4,6},{6,4},{5,7},{7,5},{8,10},{10,8},{9,1... | collective-permute-start | bytes 393224 | tf_op jit(solution)/shard_map/ppermute | solution.py:379
  58.1 10.1 %copy-start = (bf16[3,2048,256]{2,1,0:T(8,128)(2,1)S(1)}, bf16[3,2048,256]{2,1,0:T(8,128)(2,1)}, u32[]{:S(2)}) copy-start(bf16[3,2048,256]{2,1,0:T(8,128)(2,1)} %get-tuple-element.38.w_hbm) | copy-start | bytes 9437188
  67.8 5.0 %collective-permute-start.3 = (bf16[32,64,256]{2,1,0:T(8,128)(2,1)S(1)}, bf16[32,64,256]{2,1,0:T(8,128)(2,1)S(1)}, u32[]{:S(2)}, u32[]{:S(2)}) collective-permute-start(bf16[32,64,256]{2,1,0:T(8,128)(2,1)S(1)} %get-tuple-element.42), channel_id=1, source_target_pairs={{0,1},{1,0},{2,3},{3,2},{4,5},{5,4},{6,7},{7,6},{8,9},{9,8},{10,11... | collective-permute-start | bytes 3145736 | tf_op jit(solution)/shard_map/ppermute | solution.py:379
  100.1 9.2 %collective-permute-start.4 = (bf16[3,64,640]{2,1,0:T(8,128)(2,1)S(1)}, bf16[3,64,640]{2,1,0:T(8,128)(2,1)S(1)}, u32[]{:S(2)}, u32[]{:S(2)}) collective-permute-start(bf16[3,64,640]{2,1,0:T(8,128)(2,1)S(1)} %get-tuple-element.44), channel_id=1, source_target_pairs={{0,1},{1,0},{2,3},{3,2},{4,5},{5,4},{6,7},{7,6},{8,9},{9,8},{10,11... | collective-permute-start | bytes 737288 | tf_op jit(solution)/shard_map/ppermute | solution.py:379
  102.2 7.2 %collective-permute-start.5 = (bf16[2,32,1280]{2,1,0:T(8,128)(2,1)S(1)}, bf16[2,32,1280]{2,1,0:T(8,128)(2,1)S(1)}, u32[]{:S(2)}, u32[]{:S(2)}) collective-permute-start(bf16[2,32,1280]{2,1,0:T(8,128)(2,1)S(1)} %get-tuple-element.46), channel_id=1, source_target_pairs={{0,2},{2,0},{1,3},{3,1},{4,6},{6,4},{5,7},{7,5},{8,10},{10,8},{9,1... | collective-permute-start | bytes 491528 | tf_op jit(solution)/shard_map/ppermute | solution.py:379

commit v5 on v4

--- a/solution.py
+++ b/solution.py
@@ -293,34 +293,24 @@
 
 
 def backward_mine(
-    mine, q_ref, cot_ref, inner_ref, w_hbm, share_ref, dq_ref, out, w_ref, sems, stage, *scratch
+    mine, q_ref, cot_ref, inner_ref, w_ref, share_ref, dq_ref, out, dq_out, stage, *scratch
 ):
-    ats = [slice(SUB * i, SUB * i + SUB) for i in range(w_ref.shape[1] // SUB)]
-    copies = [
-        pltpu.make_async_copy(w_hbm.at[:, at, :], w_ref.at[:, at, :], sems.at[i])
-        for i, at in enumerate(ats)
-    ]
-    for copy in copies:
-        copy.start()
     dq = backward(
-        mine, q_ref, cot_ref, inner_ref, w_ref, share_ref, 0, out, dq_ref[...], *scratch,
-        ready=lambda i: copies[i].wait(),
+        mine, q_ref, cot_ref, inner_ref, w_ref, share_ref, 0, out, dq_ref[...], *scratch
     )
     stage[...] = (dq * INV).T
     for s in range(out.shape[0]):
-        low = PIECE * s
-        out[s, 64:80, 0:HD] = stage[low : low + 16, :].astype(BF)
-        out[s, 64:72, HD:] = stage[low + 16 : low + 24, :].astype(BF)
-        out[s, 72:80, HD:] = jnp.zeros((8, HD), BF)
-
-
-def gather_out(mine, pieces, theirs, out):
+        dq_out[s] = stage[PIECE * s : PIECE * s + PIECE, :].astype(BF)
+
+
+def gather_out(mine, dq, pieces, theirs, out):
     for s in range(out.shape[0]):
-        out[s, 0:KROWS, :] = (
-            mine[s, 0:KROWS, :].astype(F32) + theirs[s].astype(F32)
-        ).astype(BF)
-        out[s, 64:88, :] = pieces[s]
-        out[s, 88:104, :] = mine[s, 64:80, :]
+        both = (mine[s].astype(F32) + theirs[s].astype(F32)).astype(BF)
+        out[s, 0:64, :] = both[:, 0:HD]
+        out[s, 64:128, :] = both[:, HD:]
+        out[s, 128:152, :] = pieces[s, :, 0:HD]
+        out[s, 152:176, :] = pieces[s, :, HD:]
+        out[s, 176:200, :] = dq[s]
 
 
 def unpack_heads(r_ref, sent, kept, o_sent, o_kept, f_ref, o_ref):
@@ -328,21 +318,21 @@
     for head in range(2 * half):
         at, cols = head // half, slice((head % half) * HD, (head % half + 1) * HD)
         first = PARTS * head
-        both = sum(r_ref[first + part, 0:KROWS, :].astype(F32) for part in range(PARTS))
-        f_ref[at, 1, :, cols] = both[:, 0:HD].astype(BF)
-        f_ref[at, 2, :, cols] = both[:, HD:].astype(BF)
+        for array, low in ((1, 0), (2, KROWS)):
+            rows = slice(low, low + KROWS)
+            both = sum(r_ref[first + part, rows, :].astype(F32) for part in range(PARTS))
+            f_ref[at, array, :, cols] = both.astype(BF)
         ocols = slice(head * HD, head * HD + HD)
         for part in range(PARTS):
             for place, eight in enumerate(EIGHTS[part]):
                 if eight is None:
                     continue
                 row, low = 8 * eight, 8 * place
-                lanes = slice(0, HD) if place < 2 else slice(HD, 2 * HD)
-                from_row = 88 + low % 16
-                f_ref[at, 0, row : row + 8, cols] = r_ref[first + part, from_row : from_row + 8, lanes]
+                f_ref[at, 0, row : row + 8, cols] = r_ref[first + part, 176 + low : 184 + low, :]
                 for side in range(2):
+                    from_row = 128 + PIECE * side + low
                     o_ref[row // 32, side, row % 32 : row % 32 + 8, ocols] = r_ref[
-                        first + part, 64 + low : 72 + low, side * HD : side * HD + HD
+                        first + part, from_row : from_row + 8, :
                     ]
     sent[...] = f_ref[1 - core()]
     kept[...] = f_ref[core()]
@@ -432,17 +422,17 @@
         14 * flops, length * rows, 7_000_000,
     )(theirs, q, qq, m1, sums1, acc1, gap_kept, gap_got, mask)
     partner = swap(dst, "c")
-    out = call(
+    out, dq = call(
         backward_mine,
-        [(shape(chips, KROWS + 16, 2 * HD), VMEM)],
-        [VMEM] * 4 + [HBM] + [VMEM] * 2,
-        30,
-        (
-            pltpu.VMEM(w.shape, BF), pltpu.SemaphoreType.DMA((subs,)), pltpu.VMEM((rows, HD), F32),
-        ) + back_scratch,
+        [(key_piece, VMEM), (shape(chips, PIECE, HD), VMEM)],
+        [VMEM] * 7,
+        26,
+        (pltpu.VMEM((rows, HD), F32),) + back_scratch,
         8 * flops, 0, 7_000_000,
-    )(mine, q, cot, inner, w1, share, dq)[0]
-    return call(gather_out, [(shape(chips, 104, 2 * HD), VMEM)], [VMEM] * 3, 8)(out, pieces, partner)[0]
+    )(mine, q, cot, inner, w1, share, dq)
+    return call(gather_out, [(shape(chips, 200, HD), VMEM)], [VMEM] * 4, 8)(
+        out, dq, pieces, partner
+    )[0]
 
 
 def per_device(q, k, v, tq, tk, tv, gap):

time: 111 us -> 109 us (0.982)
  Pallas kernels: 22.4 us -> 21.1 us
    pallas_call x2, Pallas kernels: 4.86 us -> 3.66 us  [the longest x1 3.36 us: attention(): call(backward_mine, [(key_piece, VMEM), (shape(chips, PIECE, HD), VMEM)],...]
  transfers between devices with their start and end apart: 6 -> 6, of which waited for: 2 -> 2; matrix products, arithmetic and copies ran while one was open for 0% -> 0% of each run, Pallas kernels for 8% -> 7%
where the time goes in v5:
time: 109 us; the launch traced here: 108 us
  blocking collectives  68.5 us (63%)
  Pallas kernels  21.1 us (19%)
  starting transfers between devices  11.9 us (11%)
  waiting for transfers between devices  6.07 us (6%)
    all_to_all x2, blocking collectives, exchange(): return lax.all_to_all(array, BLOCK_AXES, 0, 0, tiled=True)  68.5 us
    ppermute x6, starting transfers between devices, swap(): return lax.ppermute(array, axis, SWAP)  11.9 us
    pallas_call x1, Pallas kernels, attention(): call(theirs_both_ways, [(key_piece, VMEM), (shape(chips, PIECE, 2 * HD),...  9.63 us
    ppermute x6, waiting for transfers between devices, swap(): return lax.ppermute(array, axis, SWAP)  6.07 us
    pallas_call x1, Pallas kernels, attention(): call(forward_mine, [(q, VMEM), (qq, VMEM), (w, HBM), (stats, VMEM), (sums...  4.57 us
    pallas_call x1, Pallas kernels, attention(): call(backward_mine, [(key_piece, VMEM), (shape(chips, PIECE, HD), VMEM)],...  3.36 us
  transfers between devices with their start and end apart: 6, of which 2 were waited for; matrix products, arithmetic and copies ran while one was open for 0% of the time, Pallas kernels for 7%

profile of v5, /device:TPU:1, one launch (start us, length us, event | category | flops | bytes accessed | tf_op | source)
XLA Modules:
  0.0 108.4 jit_solution(710017321563549430)
XLA Ops:
  0.6 1.6 %shard_map.110 = (bf16[6,64,640]{2,1,0:T(8,128)(2,1)S(1)}, bf16[6,64,640]{2,1,0:T(8,128)(2,1)S(1)}, bf16[32,2560]{1,0:T(8,128)(2,1)S(1)}) custom-call(bf16[128,640]{1,0:T(8,128)(2,1)} %refs_0_.1, bf16[128,640]{1,0:T(8,128)(2,1)} %refs_1_.1, bf16[128,640]{1,0:T(8,128)(2,1)} %refs_2_.1, bf16[128,640]{1,0:T(8,128)(2,1)} %refs_3_.1, bf16[128,640]{1,0:T(8,128)(2,1)} %refs_4_.1, ...), custom_call_target="tpu_custom_call" | custom-call | bytes 1000000 | tf_op jit(solution)/shard_map/pallas_call | solution.py:444
  2.2 1.5 %collective-permute-start = (bf16[6,64,640]{2,1,0:T(8,128)(2,1)S(1)}, bf16[6,64,640]{2,1,0:T(8,128)(2,1)S(1)}, u32[]{:S(2)}, u32[]{:S(2)}) collective-permute-start(bf16[6,64,640]{2,1,0:T(8,128)(2,1)S(1)} %get-tuple-element.29), channel_id=1, source_target_pairs={{0,1},{1,0},{2,3},{3,2},{4,5},{5,4},{6,7},{7,6},{8,9},{9,8},{10,11... | collective-permute-start | bytes 1474568 | tf_op jit(solution)/shard_map/ppermute | solution.py:369
  3.7 1.5 %collective-permute-done.got = bf16[6,64,640]{2,1,0:T(8,128)(2,1)S(1)} collective-permute-done((bf16[6,64,640]{2,1,0:T(8,128)(2,1)S(1)}, bf16[6,64,640]{2,1,0:T(8,128)(2,1)S(1)}, u32[]{:S(2)}, u32[]{:S(2)}) %collective-permute-start) | collective-permute-done | bytes 491552 | tf_op jit(solution)/shard_map/ppermute | solution.py:369
  5.2 0.4 shard_map.111
  5.6 42.3 %all_to_all.10.mine = bf16[32,168,256]{2,1,0:T(8,128)(2,1)S(1)} all-to-all(bf16[32,168,256]{2,1,0:T(8,128)(2,1)S(1)} %shard_map.111), channel_id=1, replica_groups=mesh['zl'=2,'y'=4,'x'=4,'zh'=2,'c'=2] {'zl','y','x'}, dimensions={0} | all-to-all | bytes 5505024 | tf_op jit(solution)/shard_map/all_to_all | solution.py:365
  47.9 2.0 %collective-permute-start.1 = (bf16[32,168,256]{2,1,0:T(8,128)(2,1)S(1)}, bf16[32,168,256]{2,1,0:T(8,128)(2,1)}, u32[]{:S(2)}, u32[]{:S(2)}) collective-permute-start(bf16[32,168,256]{2,1,0:T(8,128)(2,1)S(1)} %all_to_all.10.mine), channel_id=1, source_target_pairs={{0,1},{1,0},{2,3},{3,2},{4,5},{5,4},{6,7},{7,6},{8,9},{9,8},{10,11... | collective-permute-start | bytes 8257544 | tf_op jit(solution)/shard_map/ppermute | solution.py:369
  50.0 0.1 shard_map.113
  50.1 3.4 %collective-permute-start.2 = (bf16[32,16,128]{2,1,0:T(8,128)(2,1)S(1)}, bf16[32,16,128]{2,1,0:T(8,128)(2,1)S(1)}, u32[]{:S(2)}, u32[]{:S(2)}) collective-permute-start(bf16[32,16,128]{2,1,0:T(8,128)(2,1)S(1)} %get-tuple-element.37), channel_id=1, source_target_pairs={{0,2},{2,0},{1,3},{3,1},{4,6},{6,4},{5,7},{7,5},{8,10},{10,8},{9,1... | collective-permute-start | bytes 393224 | tf_op jit(solution)/shard_map/ppermute | solution.py:369
  53.5 4.6 %shard_map.112 = (bf16[3,256,128]{2,1,0:T(8,128)(2,1)S(1)}, bf16[3,256,256]{2,1,0:T(8,128)(2,1)S(1)}, bf16[3,2048,256]{2,1,0:T(8,128)(2,1)}, f32[3,1,256]{2,1,0:...) custom-call(bf16[32,168,256]{2,1,0:T(8,128)(2,1)S(1)} %all_to_all.10.mine), custom_call_target="tpu_custom_call" | custom-call | flops 2415919104 | bytes 7000000 | tf_op jit(solution)/shard_map/pallas_call | solution.py:399
  58.0 0.0 collective-permute-done.2.gap_got
  58.1 0.0 collective-permute-done.1.theirs_hbm
  58.1 0.0 copy-start
  58.1 9.6 %shard_map.114 = (bf16[32,64,256]{2,1,0:T(8,128)(2,1)S(1)}, bf16[32,24,256]{2,1,0:T(8,128)(2,1)S(1)}, bf16[768,128]{1,0:T(8,128)(2,1)S(1)}, f32[3,1,256]{2,1,0:T...) custom-call(bf16[32,168,256]{2,1,0:T(8,128)(2,1)} %collective-permute-done.1.theirs_hbm, ...), custom_call_target="tpu_custom_call" | custom-call | flops 5637144576 | bytes 7000000 | tf_op jit(solution)/shard_map/pallas_call | solution.py:408
  67.7 0.4 collective-permute-start.3
  68.1 0.0 copy-done
  68.1 3.4 %shard_map.115 = (bf16[32,64,256]{2,1,0:T(8,128)(2,1)S(1)}, bf16[32,24,128]{2,1,0:T(8,128)(2,1)S(1)}) custom-call(bf16[32,168,256]{2,1,0:T(8,128)(2,1)S(1)} %all_to_all.10.mine, bf16[3,256,128]{2,1,0:T(8,128)(2,1)S(1)} %get-tuple-element.31.q_ref, bf16[768,128]{1,0:T(8,128)(2,1)S(1)} %get-tuple-element.38.cot_ref, ...), custom_call_target="tpu_custom_call" | custom-call | flops 3221225472 | bytes 7000000 | tf_op jit(solution)/shard_map/pallas_call | solution.py:425
  71.4 0.0 collective-permute-done.3.theirs
  71.5 0.3 shard_map.116
  71.8 26.2 %all_to_all.11.r_ref = bf16[32,200,128]{2,1,0:T(8,128)(2,1)S(1)} all-to-all(bf16[32,200,128]{2,1,0:T(8,128)(2,1)S(1)} %shard_map.116), channel_id=1, replica_groups=mesh['zl'=2,'y'=4,'x'=4,'zh'=2,'c'=2] {'zl','y','x'}, dimensions={0} | all-to-all | bytes 3276800 | tf_op jit(solution)/shard_map/all_to_all | solution.py:365
  98.0 0.2 shard_map.117
  98.2 2.1 %collective-permute-start.4 = (bf16[3,64,640]{2,1,0:T(8,128)(2,1)S(1)}, bf16[3,64,640]{2,1,0:T(8,128)(2,1)S(1)}, u32[]{:S(2)}, u32[]{:S(2)}) collective-permute-start(bf16[3,64,640]{2,1,0:T(8,128)(2,1)S(1)} %get-tuple-element.48), channel_id=1, source_target_pairs={{0,1},{1,0},{2,3},{3,2},{4,5},{5,4},{6,7},{7,6},{8,9},{9,8},{10,11... | collective-permute-start | bytes 737288 | tf_op jit(solution)/shard_map/ppermute | solution.py:369
  100.3 2.6 %collective-permute-start.5 = (bf16[2,32,1280]{2,1,0:T(8,128)(2,1)S(1)}, bf16[2,32,1280]{2,1,0:T(8,128)(2,1)S(1)}, u32[]{:S(2)}, u32[]{:S(2)}) collective-permute-start(bf16[2,32,1280]{2,1,0:T(8,128)(2,1)S(1)} %get-tuple-element.50), channel_id=1, source_target_pairs={{0,2},{2,0},{1,3},{3,1},{4,6},{6,4},{5,7},{7,5},{8,10},{10,8},{9,1... | collective-permute-start | bytes 491528 | tf_op jit(solution)/shard_map/ppermute | solution.py:369
  102.9 4.6 %collective-permute-done.5.o_got = bf16[2,32,1280]{2,1,0:T(8,128)(2,1)S(1)} collective-permute-done((bf16[2,32,1280]{2,1,0:T(8,128)(2,1)S(1)}, bf16[2,32,1280]{2,1,0:T(8,128)(2,1)S(1)}, u32[]{:S(2)}, u32[]{:S(2)}) %collective-permute-start.5) | collective-permute-done | bytes 163872 | tf_op jit(solution)/shard_map/ppermute | solution.py:369
  107.4 0.0 collective-permute-done.4.got
  107.4 1.0 shard_map.118
  (1 shorter events, 0.0 us)
Async XLA Ops:
  2.2 3.0 %collective-permute-start = (bf16[6,64,640]{2,1,0:T(8,128)(2,1)S(1)}, bf16[6,64,640]{2,1,0:T(8,128)(2,1)S(1)}, u32[]{:S(2)}, u32[]{:S(2)}) collective-permute-start(bf16[6,64,640]{2,1,0:T(8,128)(2,1)S(1)} %get-tuple-element.29), channel_id=1, source_target_pairs={{0,1},{1,0},{2,3},{3,2},{4,5},{5,4},{6,7},{7,6},{8,9},{9,8},{10,11... | collective-permute-start | bytes 1474568 | tf_op jit(solution)/shard_map/ppermute | solution.py:369
  47.9 10.1 %collective-permute-start.1 = (bf16[32,168,256]{2,1,0:T(8,128)(2,1)S(1)}, bf16[32,168,256]{2,1,0:T(8,128)(2,1)}, u32[]{:S(2)}, u32[]{:S(2)}) collective-permute-start(bf16[32,168,256]{2,1,0:T(8,128)(2,1)S(1)} %all_to_all.10.mine), channel_id=1, source_target_pairs={{0,1},{1,0},{2,3},{3,2},{4,5},{5,4},{6,7},{7,6},{8,9},{9,8},{10,11... | collective-permute-start | bytes 8257544 | tf_op jit(solution)/shard_map/ppermute | solution.py:369
  50.1 8.0 %collective-permute-start.2 = (bf16[32,16,128]{2,1,0:T(8,128)(2,1)S(1)}, bf16[32,16,128]{2,1,0:T(8,128)(2,1)S(1)}, u32[]{:S(2)}, u32[]{:S(2)}) collective-permute-start(bf16[32,16,128]{2,1,0:T(8,128)(2,1)S(1)} %get-tuple-element.37), channel_id=1, source_target_pairs={{0,2},{2,0},{1,3},{3,1},{4,6},{6,4},{5,7},{7,5},{8,10},{10,8},{9,1... | collective-permute-start | bytes 393224 | tf_op jit(solution)/shard_map/ppermute | solution.py:369
  58.1 10.0 %copy-start = (bf16[3,2048,256]{2,1,0:T(8,128)(2,1)S(1)}, bf16[3,2048,256]{2,1,0:T(8,128)(2,1)}, u32[]{:S(2)}) copy-start(bf16[3,2048,256]{2,1,0:T(8,128)(2,1)} %get-tuple-element.40.w_ref) | copy-start | bytes 9437188
  67.7 3.7 %collective-permute-start.3 = (bf16[32,64,256]{2,1,0:T(8,128)(2,1)S(1)}, bf16[32,64,256]{2,1,0:T(8,128)(2,1)S(1)}, u32[]{:S(2)}, u32[]{:S(2)}) collective-permute-start(bf16[32,64,256]{2,1,0:T(8,128)(2,1)S(1)} %get-tuple-element.46), channel_id=1, source_target_pairs={{0,1},{1,0},{2,3},{3,2},{4,5},{5,4},{6,7},{7,6},{8,9},{9,8},{10,11... | collective-permute-start | bytes 3145736 | tf_op jit(solution)/shard_map/ppermute | solution.py:369
  98.2 9.2 %collective-permute-start.4 = (bf16[3,64,640]{2,1,0:T(8,128)(2,1)S(1)}, bf16[3,64,640]{2,1,0:T(8,128)(2,1)S(1)}, u32[]{:S(2)}, u32[]{:S(2)}) collective-permute-start(bf16[3,64,640]{2,1,0:T(8,128)(2,1)S(1)} %get-tuple-element.48), channel_id=1, source_target_pairs={{0,1},{1,0},{2,3},{3,2},{4,5},{5,4},{6,7},{7,6},{8,9},{9,8},{10,11... | collective-permute-start | bytes 737288 | tf_op jit(solution)/shard_map/ppermute | solution.py:369
  100.3 7.2 %collective-permute-start.5 = (bf16[2,32,1280]{2,1,0:T(8,128)(2,1)S(1)}, bf16[2,32,1280]{2,1,0:T(8,128)(2,1)S(1)}, u32[]{:S(2)}, u32[]{:S(2)}) collective-permute-start(bf16[2,32,1280]{2,1,0:T(8,128)(2,1)S(1)} %get-tuple-element.50), channel_id=1, source_target_pairs={{0,2},{2,0},{1,3},{3,1},{4,6},{6,4},{5,7},{7,5},{8,10},{10,8},{9,1... | collective-permute-start | bytes 491528 | tf_op jit(solution)/shard_map/ppermute | solution.py:369

commit v6 on v5

v6 whole, which is shorter than its diff:
```python
import math

import jax
import jax.numpy as jnp
from jax import lax
from jax.experimental import pallas as pl
from jax.experimental.pallas import tpu as pltpu
from jax.sharding import Mesh, PartitionSpec as P


BF = jnp.bfloat16
F32 = jnp.float32
HD = 128
LOSS = 64.0
PARTS = 3
PIECE = 24
EIGHTS = ((0, 1, 4), (2, 5, None), (3, 6, 7))
GAPS = (((0, 0), (0, 1), (1, 0)), ((0, 2), (1, 1), None), ((0, 3), (1, 2), (1, 3)))
SLOT = 328
KROWS = 64
QT = 256
SUB = 512
INV = 1.0 / math.sqrt(HD)
EXP_SCALE = INV * math.log2(math.e)
VMEM = pl.BlockSpec(memory_space=pltpu.VMEM)
HBM = pl.BlockSpec(memory_space=pltpu.HBM)
ANY = pl.BlockSpec(memory_space=pl.ANY)


def call(body, outs, ins, limit, scratch=(), flops=0, exps=0, moved=1_000_000):
    return pl.pallas_call(
        body,
        out_shape=[
            pltpu.HBM(one.shape, one.dtype) if place is HBM else one for one, place in outs
        ],
        in_specs=ins,
        out_specs=[place for _, place in outs],
        scratch_shapes=list(scratch),
        compiler_params=pltpu.CompilerParams(vmem_limit_bytes=limit * 1024 * 1024),
        cost_estimate=pl.CostEstimate(flops=flops, bytes_accessed=moved, transcendentals=exps),
    )


def nt(a, b):
    return lax.dot_general(a, b, (((1,), (1,)), ((), ())), preferred_element_type=F32)


def nn(a, b):
    return lax.dot_general(a, b, (((1,), (0,)), ((), ())), preferred_element_type=F32)


def core():
    return lax.axis_index("c")


def group():
    return lax.axis_index("zh")


def half_row(half, who):
    return pl.multiple_of(64 * lax.rem(group() + half, 2) + 32 * who, 32)


def part_here():
    place = lax.axis_index("zl") * 16 + lax.axis_index("y") * 4 + lax.axis_index("x")
    return lax.rem(place, PARTS)


def split_tokens(*refs):
    *arrays, gap, sent, kept, gap_here, sems, gap_sems = refs
    copies = []
    for at, ref in enumerate(arrays):
        for half in range(2):
            for side, (dst, who) in enumerate(((sent, 1 - core()), (kept, core()))):
                copies.append(
                    pltpu.make_async_copy(
                        ref.at[pl.ds(half_row(half, who), 32), :],
                        dst.at[at, 32 * half : 32 * half + 32, :],
                        sems.at[at, half, side],
                    )
                )
    wide = gap_here.shape[2]
    for at, who in enumerate((group(), 1 - group())):
        lanes = pl.ds(pl.multiple_of(who * wide, HD), wide)
        copies.append(pltpu.make_async_copy(gap.at[:, lanes], gap_here.at[at], gap_sems.at[at]))
    for copy in copies:
        copy.start()
    for copy in copies:
        copy.wait()


def pack_heads(kept, got, gap, out, e_ref):
    e_ref[core()] = kept[...]
    e_ref[1 - core()] = got[...]
    half = e_ref.shape[3] // HD
    zero = jnp.zeros((8, HD), BF)
    for chip in range(out.shape[0]):
        head, part = chip // PARTS, chip % PARTS
        if head >= 2 * half:
            out[chip] = jnp.zeros(out.shape[1:], BF)
            continue
        at, cols = head // half, slice((head % half) * HD, (head % half + 1) * HD)
        for to, array in enumerate((1, 4, 2, 5)):
            out[chip, KROWS * to : KROWS * to + KROWS, :] = e_ref[at, array, :, cols]
        gcols = slice(head * HD, head * HD + HD)
        for to in range(3):
            eight = EIGHTS[part][to]
            for low, array in ((256, 0), (280, 3)):
                rows = slice(low + 8 * to, low + 8 * to + 8)
                if eight is None:
                    out[chip, rows, :] = zero
                else:
                    out[chip, rows, :] = e_ref[at, array, 8 * eight : 8 * eight + 8, cols]
            rows = slice(304 + 8 * to, 312 + 8 * to)
            if GAPS[part][to] is None:
                out[chip, rows, :] = zero
            else:
                which, eight = GAPS[part][to]
                out[chip, rows, :] = gap[which, 8 * eight : 8 * eight + 8, gcols]


def split_gaps(mine, sent, kept, sems):
    copies = [
        pltpu.make_async_copy(mine.at[:, low : low + 16, :], dst, sems.at[at])
        for at, (dst, low) in enumerate(((sent, 312), (kept, 304)))
    ]
    for copy in copies:
        copy.start()
    for copy in copies:
        copy.wait()


def fold(x, op):
    return op(x.reshape(x.shape[0] // 8, 8, x.shape[1]), axis=0)


def forward(keys, q_ref, qq_ref, w_ref, m_ref, sums_ref, acc_ref, s_ref, wt_ref, kk_ref, vt_ref,
            ready=None, done=None, close=None):
    tiles = q_ref.shape[0]
    per = SUB // KROWS
    subs = kk_ref.shape[0] // SUB
    ats = [slice(SUB * i, SUB * i + SUB) for i in range(subs)]

    def scores(t, i, peak):
        s = nt(kk_ref[ats[i], 0:HD], q_ref[t])
        s_ref[t % 2, ats[i], :] = s
        return jnp.maximum(peak, fold(s, jnp.max))

    def values(t, i):
        both = nn(vt_ref[:, ats[i]], w_ref[t, ats[i], :])
        tan = nn(vt_ref[0:HD, ats[i]], wt_ref[t % 2, ats[i], :]) * INV
        if i == 0:
            acc_ref[t, 0:HD, :] = both[0:HD]
            acc_ref[t, HD:, :] = both[HD:] + tan
        else:
            acc_ref[t, 0:HD, :] += both[0:HD]
            acc_ref[t, HD:, :] += both[HD:] + tan

    lowest = jnp.full((8, QT), -jnp.inf, F32)
    peak = lowest
    for i in range(subs):
        if ready is not None:
            ready(i)
        slots = slice(per * i, per * i + per)
        for half in range(2):
            lanes = slice(HD * half, HD * half + HD)
            kk_ref[ats[i], lanes] = keys[slots, KROWS * half : KROWS * half + KROWS, :].reshape(SUB, HD)
            v = keys[slots, KROWS * (2 + half) : KROWS * (3 + half), :].reshape(SUB, HD)
            vt_ref[lanes, ats[i]] = v.astype(F32).T.astype(BF)
        peak = scores(0, i, peak)
    for t in range(tiles):
        top = jnp.max(peak, axis=0, keepdims=True)
        m_ref[t] = top
        peak = lowest
        total = jnp.zeros((8, QT), F32)
        tan_total = jnp.zeros((8, QT), F32)
        for i in range(subs):
            w = jnp.exp2((s_ref[t % 2, ats[i], :] - top) * EXP_SCALE)
            wt = w * nt(kk_ref[ats[i], :], qq_ref[t])
            total = total + fold(w, jnp.sum)
            tan_total = tan_total + fold(wt, jnp.sum)
            w_ref[t, ats[i], :] = w.astype(BF)
            wt_ref[t % 2, ats[i], :] = wt.astype(BF)
            if t + 1 < tiles:
                peak = scores(t + 1, i, peak)
            if t > 0:
                values(t - 1, i)
        sums_ref[t, 0:1, :] = jnp.sum(total, axis=0, keepdims=True)
        sums_ref[t, 1:2, :] = jnp.sum(tan_total, axis=0, keepdims=True) * INV
        if done is not None:
            done(t)
        if close is not None and t > 0:
            close(t - 1)
    for i in range(subs):
        values(tiles - 1, i)
    if close is not None:
        close(tiles - 1)


def forward_mine(mine, q_ref, qq_ref, w_hbm, m_ref, sums_ref, acc_ref, stage, w_ref, sems, *scratch):
    for s in range(mine.shape[0]):
        stage[PIECE * s : PIECE * s + PIECE, 0:HD] = mine[s, 256:280, :].astype(F32)
        stage[PIECE * s : PIECE * s + PIECE, HD:] = mine[s, 280:304, :].astype(F32)
    tiles = q_ref.shape[0]
    for t in range(tiles):
        rows = slice(QT * t, QT * t + QT)
        q_ref[t] = stage[rows, 0:HD].astype(BF)
        qq_ref[t, :, 0:HD] = stage[rows, HD:].astype(BF)
        qq_ref[t, :, HD:] = stage[rows, 0:HD].astype(BF)
    copies = [pltpu.make_async_copy(w_ref.at[t], w_hbm.at[t], sems.at[t]) for t in range(tiles)]
    forward(
        mine, q_ref, qq_ref, w_ref, m_ref, sums_ref, acc_ref, *scratch,
        done=lambda t: copies[t].start(),
    )
    for copy in copies:
        copy.wait()


def backward(key, value, q_ref, cot_ref, inner_ref, w_ref, share_ref, side, dst, dq, kt_ref, ds_ref, p_ref):
    tiles = q_ref.shape[0]
    per = SUB // KROWS
    subs = ds_ref.shape[0]
    q_all = q_ref[...].reshape(tiles * QT, HD)
    for i in range(subs):
        at, slots = slice(SUB * i, SUB * i + SUB), slice(per * i, per * i + per)
        v = value(at, slots)
        kt_ref[i] = key(at, slots).astype(F32).T.astype(BF)
        for t in range(tiles):
            cols = slice(QT * t, QT * t + QT)
            p = w_ref[t, at, :].astype(F32) * share_ref[side, t]
            ds = p * (nt(v, cot_ref[cols, :]) - inner_ref[t])
            p_ref[:, cols] = p.astype(BF)
            ds_ref[i, :, cols] = ds.astype(BF)
        dk = nn(ds_ref[i], q_all) * INV
        dv = nn(p_ref[...], cot_ref[...])
        dst[slots, 0:KROWS, 0:HD] = dk.astype(BF).reshape(per, KROWS, HD)
        dst[slots, 0:KROWS, HD:] = dv.astype(BF).reshape(per, KROWS, HD)
    for i in range(subs):
        dq = dq + nn(kt_ref[i], ds_ref[i])
    return dq


def forward_theirs(
    theirs_hbm, q_ref, qq_ref, m1_ref, sums1_ref, acc1_ref,
    w_ref, pieces, cross, o_ref, share_ref, kv_ref,
    theirs, sems, m_ref, sums_ref, acc_ref, stage, *scratch
):
    per = SUB // KROWS
    copies = [
        pltpu.make_async_copy(
            theirs_hbm.at[per * i : per * i + per, 0 : 4 * KROWS, :],
            theirs.at[per * i : per * i + per],
            sems.at[i],
        )
        for i in range(theirs.shape[0] // per)
    ]
    for copy in copies:
        copy.start()

    def close(t):
        rows = slice(QT * t, QT * t + QT)
        top = jnp.maximum(m1_ref[t], m_ref[t])
        f1 = jnp.exp2((m1_ref[t] - top) * EXP_SCALE)
        f2 = jnp.exp2((m_ref[t] - top) * EXP_SCALE)
        sums = sums1_ref[t] * f1 + sums_ref[t] * f2
        inverse = 1.0 / sums[0:1]
        s1, s2 = f1 * inverse, f2 * inverse
        share_ref[0, t] = s1
        share_ref[1, t] = s2
        both = acc1_ref[t] * s1 + acc_ref[t] * s2
        tangent = both[HD:] - (sums[1:2] * inverse) * both[0:HD]
        o_ref[t, 0:HD, :] = both[0:HD].astype(BF).astype(F32)
        o_ref[t, HD:, :] = tangent.astype(BF).astype(F32)
        stage[rows, :] = o_ref[t].T

    forward(
        theirs, q_ref, qq_ref, w_ref, m_ref, sums_ref, acc_ref, *scratch,
        ready=lambda i: copies[i].wait(), close=close,
    )
    for i in range(len(copies)):
        at, slots = slice(SUB * i, SUB * i + SUB), slice(per * i, per * i + per)
        kv_ref[at, 0:HD] = theirs[slots, 0:KROWS, :].reshape(SUB, HD)
        kv_ref[at, HD:] = theirs[slots, 2 * KROWS : 3 * KROWS, :].reshape(SUB, HD)
    for s in range(pieces.shape[0]):
        low = PIECE * s
        pieces[s] = stage[low : low + PIECE, :].astype(BF)
        cross[s] = stage[low + 8 : low + PIECE, :].astype(BF)


def backward_theirs(
    kv, gap_kept, gap_got, mask, q_ref, o_ref, w_ref, share_ref,
    dst, cot_ref, inner_ref, dq_ref, stage, *scratch
):
    first = part_here() == 0
    for s in range(gap_kept.shape[0]):
        low = PIECE * s
        own, got = gap_kept[s].astype(F32), gap_got[s].astype(F32)
        stage[low : low + 8, :] = own[0:8]
        stage[low + 8 : low + 16, :] = jnp.where(first, own[8:16], got[0:8])
        stage[low + 16 : low + 24, :] = got[8:16]
    for t in range(q_ref.shape[0]):
        rows = slice(QT * t, QT * t + QT)
        cot = (LOSS * (stage[rows, :].T + o_ref[t, HD:, :])) * mask[:, rows]
        cot = cot.astype(BF).astype(F32)
        inner_ref[t] = jnp.sum(cot * o_ref[t, 0:HD, :], axis=0, keepdims=True)
        cot_ref[rows, :] = cot.T.astype(BF)
    dq_ref[...] = backward(
        lambda at, slots: kv[at, 0:HD], lambda at, slots: kv[at, HD:],
        q_ref, cot_ref, inner_ref, w_ref, share_ref, 1, dst, jnp.zeros(dq_ref.shape, F32), *scratch,
    )


def backward_mine(
    mine, q_ref, cot_ref, inner_ref, w_ref, share_ref, dq_ref, out, dq_out, stage, *scratch
):
    def rows_of(low):
        return lambda at, slots: mine[slots, low : low + KROWS, :].reshape(SUB, HD)

    dq = backward(
        rows_of(0), rows_of(2 * KROWS),
        q_ref, cot_ref, inner_ref, w_ref, share_ref, 0, out, dq_ref[...], *scratch,
    )
    stage[...] = (dq * INV).T
    for s in range(out.shape[0]):
        dq_out[s] = stage[PIECE * s : PIECE * s + PIECE, :].astype(BF)


def gather_out(mine, dq, pieces, got, theirs, out):
    first = part_here() == 0
    for s in range(out.shape[0]):
        both = (mine[s].astype(F32) + theirs[s].astype(F32)).astype(BF)
        out[s, 0:64, :] = both[:, 0:HD]
        out[s, 64:128, :] = both[:, HD:]
        second = jnp.where(first, pieces[s, 8:16, :].astype(F32), got[s, 0:8, :].astype(F32)).astype(BF)
        for low, lanes in ((128, slice(0, HD)), (152, slice(HD, 2 * HD))):
            out[s, low : low + 8, :] = pieces[s, 0:8, lanes]
            out[s, low + 8 : low + 16, :] = second[:, lanes]
            out[s, low + 16 : low + 24, :] = got[s, 8:16, lanes]
        out[s, 176:200, :] = dq[s]


def unpack_grads(r_ref, sent, kept, f_ref):
    half = f_ref.shape[3] // HD
    for head in range(2 * half):
        at, cols = head // half, slice((head % half) * HD, (head % half + 1) * HD)
        first = PARTS * head
        for array, low in ((1, 0), (2, KROWS)):
            rows = slice(low, low + KROWS)
            both = sum(r_ref[first + part, rows, :].astype(F32) for part in range(PARTS))
            f_ref[at, array, :, cols] = both.astype(BF)
        for part in range(PARTS):
            for place, eight in enumerate(EIGHTS[part]):
                if eight is not None:
                    row, low = 8 * eight, 176 + 8 * place
                    f_ref[at, 0, row : row + 8, cols] = r_ref[first + part, low : low + 8, :]
    sent[...] = f_ref[1 - core()]
    kept[...] = f_ref[core()]


def finish_outs(r_ref, primal, tangent, o_ref):
    wide = o_ref.shape[3]
    for head in range(wide // HD):
        cols = slice(head * HD, head * HD + HD)
        for part in range(PARTS):
            for place, unit in enumerate(GAPS[part]):
                if unit is None:
                    continue
                which, eight = unit
                for side in range(2):
                    low = 128 + PIECE * side + 8 * place
                    o_ref[which, side, 8 * eight : 8 * eight + 8, cols] = r_ref[
                        PARTS * head + part, low : low + 8, :
                    ]
    for side, ref in enumerate((primal, tangent)):
        for which, who in enumerate((group(), 1 - group())):
            ref[:, pl.ds(pl.multiple_of(wide * who, HD), wide)] = o_ref[which, side]


def finish_grads(kept, got, dq, dk, dv):
    for at, ref in enumerate((dq, dk, dv)):
        for half in range(2):
            rows = slice(32 * half, 32 * half + 32)
            for piece, who in ((kept, core()), (got, 1 - core())):
                ref[pl.ds(half_row(half, who), 32), :] = piece[at, rows, :]


def shape(*dims, dtype=BF):
    return jax.ShapeDtypeStruct(dims, dtype)


SWAP = [(0, 1), (1, 0)]
BLOCK_AXES = ("zl", "y", "x")


def exchange(array):
    return lax.all_to_all(array, BLOCK_AXES, 0, 0, tiled=True)


def swap(array, axis):
    return lax.ppermute(array, axis, SWAP)


def attention(chips, mine, mask):
    length, tiles = chips * KROWS, chips * PIECE // QT
    rows, subs = tiles * QT, length // SUB
    flops = 2 * length * rows * HD
    gpiece = shape(chips, 16, HD)
    gap_sent, gap_kept = call(
        split_gaps, [(gpiece, VMEM), (gpiece, VMEM)], [ANY], 2, (pltpu.SemaphoreType.DMA((2,)),),
        moved=500_000,
    )(mine)
    gap_got = swap(gap_sent, "zh")
    theirs = swap(mine, "c")
    q, qq = shape(tiles, QT, HD), shape(tiles, QT, 2 * HD)
    w = shape(tiles, length, QT)
    stats, sums, acc = (shape(tiles, n, QT, dtype=F32) for n in (1, 2, 2 * HD))
    tiles_of = (pltpu.VMEM(w.shape, BF), pltpu.SemaphoreType.DMA((tiles,)))
    scratch = (
        pltpu.VMEM((2, length, QT), F32),
        pltpu.VMEM((2, length, QT), BF),
        pltpu.VMEM((length, 2 * HD), BF),
        pltpu.VMEM((2 * HD, length), BF),
    )
    back_scratch = (
        pltpu.VMEM((subs, HD, SUB), BF),
        pltpu.VMEM((subs, SUB, rows), BF),
        pltpu.VMEM((SUB, rows), BF),
    )
    stage = pltpu.VMEM((rows, 2 * HD), F32)
    q, qq, w1, m1, sums1, acc1 = call(
        forward_mine,
        [(q, VMEM), (qq, VMEM), (w, HBM), (stats, VMEM), (sums, VMEM), (acc, VMEM)],
        [VMEM],
        30,
        (stage,) + tiles_of + scratch,
        6 * flops, length * rows, 7_000_000,
    )(mine)
    key_piece = shape(chips, KROWS, 2 * HD)
    w2, pieces, cross, o, share, kv = call(
        forward_theirs,
        [
            (w, VMEM), (shape(chips, PIECE, 2 * HD), VMEM), (shape(chips, 16, 2 * HD), VMEM),
            (acc, VMEM), (shape(2, tiles, 1, QT, dtype=F32), VMEM), (shape(length, 2 * HD), VMEM),
        ],
        [ANY] + [VMEM] * 5,
        30,
        (
            pltpu.VMEM((chips, 4 * KROWS, HD), BF), pltpu.SemaphoreType.DMA((subs,)),
            pltpu.VMEM(stats.shape, F32), pltpu.VMEM(sums.shape, F32), pltpu.VMEM(acc.shape, F32),
            stage,
        ) + scratch,
        6 * flops, length * rows, 7_000_000,
    )(theirs, q, qq, m1, sums1, acc1)
    cross = swap(cross, "zh")
    dst, cot, inner, dq = call(
        backward_theirs,
        [
            (key_piece, VMEM), (shape(rows, HD), VMEM), (stats, VMEM),
            (shape(HD, rows, dtype=F32), VMEM),
        ],
        [VMEM] * 8,
        30,
        (pltpu.VMEM((rows, HD), F32),) + back_scratch,
        8 * flops, 0, 7_000_000,
    )(kv, gap_kept, gap_got, mask, q, o, w2, share)
    partner = swap(dst, "c")
    out, dq = call(
        backward_mine,
        [(key_piece, VMEM), (shape(chips, PIECE, HD), VMEM)],
        [VMEM] * 7,
        30,
        (pltpu.VMEM((rows, HD), F32),) + back_scratch,
        8 * flops, 0, 7_000_000,
    )(mine, q, cot, inner, w1, share, dq)
    return call(gather_out, [(shape(chips, 200, HD), VMEM)], [VMEM] * 5, 8)(
        out, dq, pieces, cross, partner
    )[0]


def per_device(q, k, v, tq, tk, tv, gap):
    chips = lax.axis_size(BLOCK_AXES)
    local, feat = q.shape
    wide = gap.shape[1] // 2
    piece = shape(6, KROWS, feat)
    arrays = (q, k, v, tq, tk, tv, gap)
    sent, kept, gap_here = call(
        split_tokens,
        [(piece, VMEM), (piece, VMEM), (shape(2, 32, wide), VMEM)],
        [HBM] * 7,
        4,
        (pltpu.SemaphoreType.DMA((6, 2, 2)), pltpu.SemaphoreType.DMA((2,))),
    )(*(pltpu.with_memory_space_constraint(one, pltpu.HBM) for one in arrays))
    got = swap(sent, "c")
    packed = call(
        pack_heads,
        [(shape(chips, SLOT, HD), VMEM)],
        [VMEM] * 3,
        8,
        (pltpu.VMEM((2,) + piece.shape, BF),),
    )(kept, got, gap_here)[0]
    mine = exchange(packed)

    rows = chips * PIECE
    part = lax.axis_index(BLOCK_AXES) % PARTS
    short = (jnp.arange(rows) % PIECE >= 16) & (part == 1)
    mask = jnp.where(short, 0.0, 1.0).astype(F32)[None]
    back = exchange(attention(chips, mine, mask))

    fpiece = shape(3, KROWS, feat)
    sent, kept = call(
        unpack_grads, [(fpiece, VMEM), (fpiece, VMEM)], [VMEM], 8,
        (pltpu.VMEM((2,) + fpiece.shape, BF),),
    )(back)
    got = swap(sent, "c")
    small, large = shape(32, 2 * wide), shape(local, feat)
    primal, tangent = call(
        finish_outs, [(small, VMEM)] * 2, [VMEM], 8, (pltpu.VMEM((2, 2, 32, wide), BF),)
    )(back)
    dq, dk, dv = call(finish_grads, [(large, VMEM)] * 3, [VMEM] * 2, 8)(kept, got)
    return primal, tangent, dq, dk, dv


def solution(mesh):
    sizes = (2, 4, 4, 2, 2)
    inner = Mesh(mesh.devices.reshape(sizes), BLOCK_AXES + ("zh", "c"))
    both = P(BLOCK_AXES, ("zh", "c"))
    rows = P(BLOCK_AXES + ("zh", "c"), None)

    return jax.shard_map(
        per_device,
        mesh=inner,
        in_specs=(both,) * 6 + (rows,),
        out_specs=(rows, rows, both, both, both),
        check_vma=False,
    )
```

time: 109 us -> 108 us (level)
  starting transfers between devices: 11.9 us -> 10.1 us
  blocking collectives: 68.5 us -> 66.9 us
  Pallas kernels: 21.1 us -> 22.6 us
  waiting for transfers between devices: 6.07 us -> 7.55 us
    ppermute x6, starting transfers between devices: 11.9 us -> 10.1 us  [swap(): return lax.ppermute(array, axis, SWAP)]
    all_to_all x2, blocking collectives: 68.5 us -> 66.9 us  [exchange(): return lax.all_to_all(array, BLOCK_AXES, 0, 0, tiled=True)]
    pallas_call x6 -> x8, Pallas kernels: 13.1 us -> 14.6 us  [the longest x1 6.65 us: attention(): call(forward_theirs, [(w, VMEM), (shape(chips, PIECE, 2 * HD), VMEM), (sh...]
    ppermute x6, waiting for transfers between devices: 6.07 us -> 7.55 us  [swap(): return lax.ppermute(array, axis, SWAP)]
  transfers between devices with their start and end apart: 6 -> 6, of which waited for: 2 -> 3; matrix products, arithmetic and copies ran while one was open for 0% -> 0% of each run, Pallas kernels for 7% -> 14%
where the time goes in v6:
time: 108 us
  blocking collectives  66.9 us (62%)
  Pallas kernels  22.6 us (21%)
  starting transfers between devices  10.1 us (9%)
  waiting for transfers between devices  7.55 us (7%)
    all_to_all x2, blocking collectives, exchange(): return lax.all_to_all(array, BLOCK_AXES, 0, 0, tiled=True)  66.9 us
    ppermute x6, starting transfers between devices, swap(): return lax.ppermute(array, axis, SWAP)  10.1 us
    ppermute x6, waiting for transfers between devices, swap(): return lax.ppermute(array, axis, SWAP)  7.55 us
    pallas_call x1, Pallas kernels, attention(): call(forward_theirs, [(w, VMEM), (shape(chips, PIECE, 2 * HD), VMEM), (sh...  6.65 us
    pallas_call x1, Pallas kernels, attention(): call(forward_mine, [(q, VMEM), (qq, VMEM), (w, HBM), (stats, VMEM), (sums...  4.64 us
    pallas_call x1, Pallas kernels, attention(): call(backward_theirs, [(key_piece, VMEM), (shape(rows, HD), VMEM), (stats...  3.8 us
    pallas_call x1, Pallas kernels, attention(): call(backward_mine, [(key_piece, VMEM), (shape(chips, PIECE, HD), VMEM)],...  3.38 us
  transfers between devices with their start and end apart: 6, of which 3 were waited for; matrix products, arithmetic and copies ran while one was open for 0% of the time, Pallas kernels for 14%

profile of v6, /device:TPU:1, one launch (start us, length us, event | category | flops | bytes accessed | tf_op | source)
XLA Modules:
  0.0 108.0 jit_solution(2595690990877765074)
XLA Ops:
  0.6 1.6 %shard_map.110 = (bf16[6,64,640]{2,1,0:T(8,128)(2,1)S(1)}, bf16[6,64,640]{2,1,0:T(8,128)(2,1)S(1)}, bf16[2,32,1280]{2,1,0:T(8,128)(2,1)S(1)}) custom-call(bf16[128,640]{1,0:T(8,128)(2,1)} %refs_0_.1, bf16[128,640]{1,0:T(8,128)(2,1)} %refs_1_.1, bf16[128,640]{1,0:T(8,128)(2,1)} %refs_2_.1, bf16[128,640]{1,0:T(8,128)(2,1)} %refs_3_.1, ...), custom_call_target="tpu_custom_call" | custom-call | bytes 1000000 | tf_op jit(solution)/shard_map/pallas_call | solution.py:486
  2.2 1.5 %collective-permute-start = (bf16[6,64,640]{2,1,0:T(8,128)(2,1)S(1)}, bf16[6,64,640]{2,1,0:T(8,128)(2,1)S(1)}, u32[]{:S(2)}, u32[]{:S(2)}) collective-permute-start(bf16[6,64,640]{2,1,0:T(8,128)(2,1)S(1)} %get-tuple-element.36), channel_id=1, source_target_pairs={{0,1},{1,0},{2,3},{3,2},{4,5},{5,4},{6,7},{7,6},{8,9},{9,8},{10,11... | collective-permute-start | bytes 1474568 | tf_op jit(solution)/shard_map/ppermute | solution.py:400
  3.7 1.5 %collective-permute-done.got = bf16[6,64,640]{2,1,0:T(8,128)(2,1)S(1)} collective-permute-done((bf16[6,64,640]{2,1,0:T(8,128)(2,1)S(1)}, bf16[6,64,640]{2,1,0:T(8,128)(2,1)S(1)}, u32[]{:S(2)}, u32[]{:S(2)}) %collective-permute-start) | collective-permute-done | bytes 491552 | tf_op jit(solution)/shard_map/ppermute | solution.py:400
  5.2 0.4 shard_map.111
  5.6 41.6 %all_to_all.10.mine = bf16[32,328,128]{2,1,0:T(8,128)(2,1)S(1)} all-to-all(bf16[32,328,128]{2,1,0:T(8,128)(2,1)S(1)} %shard_map.111), channel_id=1, replica_groups=mesh['zl'=2,'y'=4,'x'=4,'zh'=2,'c'=2] {'zl','y','x'}, dimensions={0} | all-to-all | bytes 5373952 | tf_op jit(solution)/shard_map/all_to_all | solution.py:396
  47.2 2.1 %collective-permute-start.1 = (bf16[32,328,128]{2,1,0:T(8,128)(2,1)S(1)}, bf16[32,328,128]{2,1,0:T(8,128)(2,1)}, u32[]{:S(2)}, u32[]{:S(2)}) collective-permute-start(bf16[32,328,128]{2,1,0:T(8,128)(2,1)S(1)} %all_to_all.10.mine), channel_id=1, source_target_pairs={{0,1},{1,0},{2,3},{3,2},{4,5},{5,4},{6,7},{7,6},{8,9},{9,8},{10,11... | collective-permute-start | bytes 8060936 | tf_op jit(solution)/shard_map/ppermute | solution.py:400
  49.4 3.4 %collective-permute-start.2 = (bf16[32,16,128]{2,1,0:T(8,128)(2,1)S(1)}, bf16[32,16,128]{2,1,0:T(8,128)(2,1)S(1)}, u32[]{:S(2)}, u32[]{:S(2)}) collective-permute-start(bf16[32,16,128]{2,1,0:T(8,128)(2,1)S(1)} %get-tuple-element.45), channel_id=1, source_target_pairs={{0,2},{2,0},{1,3},{3,1},{4,6},{6,4},{5,7},{7,5},{8,10},{10,8},{9,1... | collective-permute-start | bytes 393224 | tf_op jit(solution)/shard_map/ppermute | solution.py:400
  52.8 4.6 %shard_map.112 = (bf16[3,256,128]{2,1,0:T(8,128)(2,1)S(1)}, bf16[3,256,256]{2,1,0:T(8,128)(2,1)S(1)}, bf16[3,2048,256]{2,1,0:T(8,128)(2,1)}, f32[3,1,256]{2,1,0:...) custom-call(bf16[32,328,128]{2,1,0:T(8,128)(2,1)S(1)} %all_to_all.10.mine), custom_call_target="tpu_custom_call" | custom-call | flops 2415919104 | bytes 7000000 | tf_op jit(solution)/shard_map/pallas_call | solution.py:430
  57.4 0.0 collective-permute-done.1.theirs_hbm
  57.4 6.7 %shard_map.113 = (bf16[3,2048,256]{2,1,0:T(8,128)(2,1)S(1)}, bf16[32,24,256]{2,1,0:T(8,128)(2,1)S(1)}, bf16[32,16,256]{2,1,0:T(8,128)(2,1)S(1)}, f32[3,256,256]{...) custom-call(bf16[32,328,128]{2,1,0:T(8,128)(2,1)} %collective-permute-done.1.theirs_hbm, ...), custom_call_target="tpu_custom_call" | custom-call | flops 2415919104 | bytes 7000000 | tf_op jit(solution)/shard_map/pallas_call | solution.py:439
  64.1 0.0 collective-permute-done.2.gap_got
  64.1 0.0 copy-start
  64.1 3.8 %shard_map.115 = (bf16[32,64,256]{2,1,0:T(8,128)(2,1)S(1)}, bf16[768,128]{1,0:T(8,128)(2,1)S(1)}, f32[3,1,256]{2,1,0:T(1,128)S(1)}, f32[128,768]{1,0:T(8,128)S(1)}) custom-call(bf16[2048,256]{1,0:T(8,128)(2,1)S(1)} %get-tuple-element.43.kv, bf16[32,16,128]{2,1,0:T(8,128)(2,1)S(1)} %get-tuple-element.44.gap_kept, ...), custom_call_target="tpu_custom_call" | custom-call | flops 3221225472 | bytes 7000000 | tf_op jit(solution)/shard_map/pallas_call | solution.py:455
  67.9 0.4 collective-permute-start.4
  68.3 0.0 collective-permute-start.3
  68.3 0.0 copy-done
  68.3 3.4 %shard_map.116 = (bf16[32,64,256]{2,1,0:T(8,128)(2,1)S(1)}, bf16[32,24,128]{2,1,0:T(8,128)(2,1)S(1)}) custom-call(bf16[32,328,128]{2,1,0:T(8,128)(2,1)S(1)} %all_to_all.10.mine, bf16[3,256,128]{2,1,0:T(8,128)(2,1)S(1)} %get-tuple-element.38.q_ref, bf16[768,128]{1,0:T(8,128)(2,1)S(1)} %get-tuple-element.49.cot_ref, ...), custom_call_target="tpu_custom_call" | custom-call | flops 3221225472 | bytes 7000000 | tf_op jit(solution)/shard_map/pallas_call | solution.py:467
  71.7 5.7 %collective-permute-done.3.got = bf16[32,16,256]{2,1,0:T(8,128)(2,1)S(1)} collective-permute-done((bf16[32,16,256]{2,1,0:T(8,128)(2,1)S(1)}, bf16[32,16,256]{2,1,0:T(8,128)(2,1)S(1)}, u32[]{:S(2)}, u32[]{:S(2)}) %collective-permute-start.3) | collective-permute-done | bytes 262176 | tf_op jit(solution)/shard_map/ppermute | solution.py:400
  77.4 0.0 collective-permute-done.4.theirs
  77.4 0.3 shard_map.117
  77.8 25.3 %all_to_all.11.r_ref = bf16[32,200,128]{2,1,0:T(8,128)(2,1)S(1)} all-to-all(bf16[32,200,128]{2,1,0:T(8,128)(2,1)S(1)} %shard_map.117), channel_id=1, replica_groups=mesh['zl'=2,'y'=4,'x'=4,'zh'=2,'c'=2] {'zl','y','x'}, dimensions={0} | all-to-all | bytes 3276800 | tf_op jit(solution)/shard_map/all_to_all | solution.py:396
  103.1 0.2 shard_map.119
  103.2 2.7 %collective-permute-start.5 = (bf16[3,64,640]{2,1,0:T(8,128)(2,1)S(1)}, bf16[3,64,640]{2,1,0:T(8,128)(2,1)S(1)}, u32[]{:S(2)}, u32[]{:S(2)}) collective-permute-start(bf16[3,64,640]{2,1,0:T(8,128)(2,1)S(1)} %get-tuple-element.61), channel_id=1, source_target_pairs={{0,1},{1,0},{2,3},{3,2},{4,5},{5,4},{6,7},{7,6},{8,9},{9,8},{10,11... | collective-permute-start | bytes 737288 | tf_op jit(solution)/shard_map/ppermute | solution.py:400
  106.0 0.8 shard_map.118
  106.8 0.3 collective-permute-done.5.got
  107.1 0.8 shard_map.120
  (2 shorter events, 0.1 us)
Async XLA Ops:
  2.2 3.0 %collective-permute-start = (bf16[6,64,640]{2,1,0:T(8,128)(2,1)S(1)}, bf16[6,64,640]{2,1,0:T(8,128)(2,1)S(1)}, u32[]{:S(2)}, u32[]{:S(2)}) collective-permute-start(bf16[6,64,640]{2,1,0:T(8,128)(2,1)S(1)} %get-tuple-element.36), channel_id=1, source_target_pairs={{0,1},{1,0},{2,3},{3,2},{4,5},{5,4},{6,7},{7,6},{8,9},{9,8},{10,11... | collective-permute-start | bytes 1474568 | tf_op jit(solution)/shard_map/ppermute | solution.py:400
  47.2 10.2 %collective-permute-start.1 = (bf16[32,328,128]{2,1,0:T(8,128)(2,1)S(1)}, bf16[32,328,128]{2,1,0:T(8,128)(2,1)}, u32[]{:S(2)}, u32[]{:S(2)}) collective-permute-start(bf16[32,328,128]{2,1,0:T(8,128)(2,1)S(1)} %all_to_all.10.mine), channel_id=1, source_target_pairs={{0,1},{1,0},{2,3},{3,2},{4,5},{5,4},{6,7},{7,6},{8,9},{9,8},{10,11... | collective-permute-start | bytes 8060936 | tf_op jit(solution)/shard_map/ppermute | solution.py:400
  49.4 14.7 %collective-permute-start.2 = (bf16[32,16,128]{2,1,0:T(8,128)(2,1)S(1)}, bf16[32,16,128]{2,1,0:T(8,128)(2,1)S(1)}, u32[]{:S(2)}, u32[]{:S(2)}) collective-permute-start(bf16[32,16,128]{2,1,0:T(8,128)(2,1)S(1)} %get-tuple-element.45), channel_id=1, source_target_pairs={{0,2},{2,0},{1,3},{3,1},{4,6},{6,4},{5,7},{7,5},{8,10},{10,8},{9,1... | collective-permute-start | bytes 393224 | tf_op jit(solution)/shard_map/ppermute | solution.py:400
  64.1 4.2 %copy-start = (bf16[3,2048,256]{2,1,0:T(8,128)(2,1)S(1)}, bf16[3,2048,256]{2,1,0:T(8,128)(2,1)}, u32[]{:S(2)}) copy-start(bf16[3,2048,256]{2,1,0:T(8,128)(2,1)} %get-tuple-element.51.w_ref) | copy-start | bytes 9437188
  67.9 9.5 %collective-permute-start.4 = (bf16[32,64,256]{2,1,0:T(8,128)(2,1)S(1)}, bf16[32,64,256]{2,1,0:T(8,128)(2,1)S(1)}, u32[]{:S(2)}, u32[]{:S(2)}) collective-permute-start(bf16[32,64,256]{2,1,0:T(8,128)(2,1)S(1)} %get-tuple-element.57), channel_id=1, source_target_pairs={{0,1},{1,0},{2,3},{3,2},{4,5},{5,4},{6,7},{7,6},{8,9},{9,8},{10,11... | collective-permute-start | bytes 3145736 | tf_op jit(solution)/shard_map/ppermute | solution.py:400
  68.3 9.1 %collective-permute-start.3 = (bf16[32,16,256]{2,1,0:T(8,128)(2,1)S(1)}, bf16[32,16,256]{2,1,0:T(8,128)(2,1)S(1)}, u32[]{:S(2)}, u32[]{:S(2)}) collective-permute-start(bf16[32,16,256]{2,1,0:T(8,128)(2,1)S(1)} %get-tuple-element.56), channel_id=1, source_target_pairs={{0,2},{2,0},{1,3},{3,1},{4,6},{6,4},{5,7},{7,5},{8,10},{10,8},{9,1... | collective-permute-start | bytes 786440 | tf_op jit(solution)/shard_map/ppermute | solution.py:400
  103.2 3.9 %collective-permute-start.5 = (bf16[3,64,640]{2,1,0:T(8,128)(2,1)S(1)}, bf16[3,64,640]{2,1,0:T(8,128)(2,1)S(1)}, u32[]{:S(2)}, u32[]{:S(2)}) collective-permute-start(bf16[3,64,640]{2,1,0:T(8,128)(2,1)S(1)} %get-tuple-element.61), channel_id=1, source_target_pairs={{0,1},{1,0},{2,3},{3,2},{4,5},{5,4},{6,7},{7,6},{8,9},{9,8},{10,11... | collective-permute-start | bytes 737288 | tf_op jit(solution)/shard_map/ppermute | solution.py:400

commit v7 on v6

--- a/solution.py
+++ b/solution.py
@@ -66,27 +66,38 @@
     return lax.rem(place, PARTS)
 
 
-def split_tokens(*refs):
-    *arrays, gap, sent, kept, gap_here, sems, gap_sems = refs
-    copies = []
-    for at, ref in enumerate(arrays):
-        for half in range(2):
-            for side, (dst, who) in enumerate(((sent, 1 - core()), (kept, core()))):
-                copies.append(
-                    pltpu.make_async_copy(
-                        ref.at[pl.ds(half_row(half, who), 32), :],
-                        dst.at[at, 32 * half : 32 * half + 32, :],
-                        sems.at[at, half, side],
-                    )
-                )
+def split_tokens(arrays, dst, who, sems):
+    return [
+        pltpu.make_async_copy(
+            ref.at[pl.ds(half_row(half, who), 32), :],
+            dst.at[at, 32 * half : 32 * half + 32, :],
+            sems.at[at, half],
+        )
+        for at, ref in enumerate(arrays)
+        for half in range(2)
+    ]
+
+
+def run_all(copies):
+    for copy in copies:
+        copy.start()
+    for copy in copies:
+        copy.wait()
+
+
+def send_tokens(*refs):
+    *arrays, sent, sems = refs
+    run_all(split_tokens(arrays, sent, 1 - core(), sems))
+
+
+def keep_tokens(*refs):
+    *arrays, gap, kept, gap_here, sems, gap_sems = refs
+    copies = split_tokens(arrays, kept, core(), sems)
     wide = gap_here.shape[2]
     for at, who in enumerate((group(), 1 - group())):
         lanes = pl.ds(pl.multiple_of(who * wide, HD), wide)
         copies.append(pltpu.make_async_copy(gap.at[:, lanes], gap_here.at[at], gap_sems.at[at]))
-    for copy in copies:
-        copy.start()
-    for copy in copies:
-        copy.wait()
+    run_all(copies)
 
 
 def pack_heads(kept, got, gap, out, e_ref):
@@ -120,14 +131,12 @@
 
 
 def split_gaps(mine, sent, kept, sems):
-    copies = [
-        pltpu.make_async_copy(mine.at[:, low : low + 16, :], dst, sems.at[at])
-        for at, (dst, low) in enumerate(((sent, 312), (kept, 304)))
-    ]
-    for copy in copies:
-        copy.start()
-    for copy in copies:
-        copy.wait()
+    run_all(
+        [
+            pltpu.make_async_copy(mine.at[:, low : low + 16, :], dst, sems.at[at])
+            for at, (dst, low) in enumerate(((sent, 312), (kept, 304)))
+        ]
+    )
 
 
 def fold(x, op):
@@ -135,7 +144,7 @@
 
 
 def forward(keys, q_ref, qq_ref, w_ref, m_ref, sums_ref, acc_ref, s_ref, wt_ref, kk_ref, vt_ref,
-            ready=None, done=None, close=None):
+            done=None, close=None):
     tiles = q_ref.shape[0]
     per = SUB // KROWS
     subs = kk_ref.shape[0] // SUB
@@ -159,8 +168,6 @@
     lowest = jnp.full((8, QT), -jnp.inf, F32)
     peak = lowest
     for i in range(subs):
-        if ready is not None:
-            ready(i)
         slots = slice(per * i, per * i + per)
         for half in range(2):
             lanes = slice(HD * half, HD * half + HD)
@@ -216,6 +223,10 @@
         copy.wait()
 
 
+def rows_of(ref, low):
+    return lambda at, slots: ref[slots, low : low + KROWS, :].reshape(SUB, HD)
+
+
 def backward(key, value, q_ref, cot_ref, inner_ref, w_ref, share_ref, side, dst, dq, kt_ref, ds_ref, p_ref):
     tiles = q_ref.shape[0]
     per = SUB // KROWS
@@ -241,22 +252,10 @@
 
 
 def forward_theirs(
-    theirs_hbm, q_ref, qq_ref, m1_ref, sums1_ref, acc1_ref,
-    w_ref, pieces, cross, o_ref, share_ref, kv_ref,
-    theirs, sems, m_ref, sums_ref, acc_ref, stage, *scratch
+    theirs, q_ref, qq_ref, m1_ref, sums1_ref, acc1_ref,
+    w_ref, pieces, cross, o_ref, share_ref,
+    m_ref, sums_ref, acc_ref, stage, *scratch
 ):
-    per = SUB // KROWS
-    copies = [
-        pltpu.make_async_copy(
-            theirs_hbm.at[per * i : per * i + per, 0 : 4 * KROWS, :],
-            theirs.at[per * i : per * i + per],
-            sems.at[i],
-        )
-        for i in range(theirs.shape[0] // per)
-    ]
-    for copy in copies:
-        copy.start()
-
     def close(t):
         rows = slice(QT * t, QT * t + QT)
         top = jnp.maximum(m1_ref[t], m_ref[t])
@@ -274,13 +273,8 @@
         stage[rows, :] = o_ref[t].T
 
     forward(
-        theirs, q_ref, qq_ref, w_ref, m_ref, sums_ref, acc_ref, *scratch,
-        ready=lambda i: copies[i].wait(), close=close,
-    )
-    for i in range(len(copies)):
-        at, slots = slice(SUB * i, SUB * i + SUB), slice(per * i, per * i + per)
-        kv_ref[at, 0:HD] = theirs[slots, 0:KROWS, :].reshape(SUB, HD)
-        kv_ref[at, HD:] = theirs[slots, 2 * KROWS : 3 * KROWS, :].reshape(SUB, HD)
+        theirs, q_ref, qq_ref, w_ref, m_ref, sums_ref, acc_ref, *scratch, close=close
+    )
     for s in range(pieces.shape[0]):
         low = PIECE * s
         pieces[s] = stage[low : low + PIECE, :].astype(BF)
@@ -288,7 +282,7 @@
 
 
 def backward_theirs(
-    kv, gap_kept, gap_got, mask, q_ref, o_ref, w_ref, share_ref,
+    theirs, gap_kept, gap_got, q_ref, o_ref, w_ref, share_ref,
     dst, cot_ref, inner_ref, dq_ref, stage, *scratch
 ):
     first = part_here() == 0
@@ -300,12 +294,15 @@
         stage[low + 16 : low + 24, :] = got[8:16]
     for t in range(q_ref.shape[0]):
         rows = slice(QT * t, QT * t + QT)
-        cot = (LOSS * (stage[rows, :].T + o_ref[t, HD:, :])) * mask[:, rows]
+        place = lax.rem(QT * t + lax.broadcasted_iota(jnp.int32, (1, QT), 1), PIECE)
+        short = jnp.where(place >= 16, 1, 0) * jnp.where(part_here() == 1, 1, 0)
+        mask = jnp.where(short == 1, 0.0, 1.0)
+        cot = (LOSS * (stage[rows, :].T + o_ref[t, HD:, :])) * mask
         cot = cot.astype(BF).astype(F32)
         inner_ref[t] = jnp.sum(cot * o_ref[t, 0:HD, :], axis=0, keepdims=True)
         cot_ref[rows, :] = cot.T.astype(BF)
     dq_ref[...] = backward(
-        lambda at, slots: kv[at, 0:HD], lambda at, slots: kv[at, HD:],
+        rows_of(theirs, 0), rows_of(theirs, 2 * KROWS),
         q_ref, cot_ref, inner_ref, w_ref, share_ref, 1, dst, jnp.zeros(dq_ref.shape, F32), *scratch,
     )
 
@@ -313,11 +310,8 @@
 def backward_mine(
     mine, q_ref, cot_ref, inner_ref, w_ref, share_ref, dq_ref, out, dq_out, stage, *scratch
 ):
-    def rows_of(low):
-        return lambda at, slots: mine[slots, low : low + KROWS, :].reshape(SUB, HD)
-
     dq = backward(
-        rows_of(0), rows_of(2 * KROWS),
+        rows_of(mine, 0), rows_of(mine, 2 * KROWS),
         q_ref, cot_ref, inner_ref, w_ref, share_ref, 0, out, dq_ref[...], *scratch,
     )
     stage[...] = (dq * INV).T
@@ -400,7 +394,7 @@
     return lax.ppermute(array, axis, SWAP)
 
 
-def attention(chips, mine, mask):
+def attention(chips, mine):
     length, tiles = chips * KROWS, chips * PIECE // QT
     rows, subs = tiles * QT, length // SUB
     flops = 2 * length * rows * HD
@@ -436,16 +430,15 @@
         6 * flops, length * rows, 7_000_000,
     )(mine)
     key_piece = shape(chips, KROWS, 2 * HD)
-    w2, pieces, cross, o, share, kv = call(
+    w2, pieces, cross, o, share = call(
         forward_theirs,
         [
             (w, VMEM), (shape(chips, PIECE, 2 * HD), VMEM), (shape(chips, 16, 2 * HD), VMEM),
-            (acc, VMEM), (shape(2, tiles, 1, QT, dtype=F32), VMEM), (shape(length, 2 * HD), VMEM),
+            (acc, VMEM), (shape(2, tiles, 1, QT, dtype=F32), VMEM),
         ],
-        [ANY] + [VMEM] * 5,
+        [VMEM] * 6,
         30,
         (
-            pltpu.VMEM((chips, 4 * KROWS, HD), BF), pltpu.SemaphoreType.DMA((subs,)),
             pltpu.VMEM(stats.shape, F32), pltpu.VMEM(sums.shape, F32), pltpu.VMEM(acc.shape, F32),
             stage,
         ) + scratch,
@@ -458,11 +451,11 @@
             (key_piece, VMEM), (shape(rows, HD), VMEM), (stats, VMEM),
             (shape(HD, rows, dtype=F32), VMEM),
         ],
-        [VMEM] * 8,
+        [VMEM] * 7,
         30,
         (pltpu.VMEM((rows, HD), F32),) + back_scratch,
         8 * flops, 0, 7_000_000,
-    )(kv, gap_kept, gap_got, mask, q, o, w2, share)
+    )(theirs, gap_kept, gap_got, q, o, w2, share)
     partner = swap(dst, "c")
     out, dq = call(
         backward_mine,
@@ -482,15 +475,19 @@
     local, feat = q.shape
     wide = gap.shape[1] // 2
     piece = shape(6, KROWS, feat)
-    arrays = (q, k, v, tq, tk, tv, gap)
-    sent, kept, gap_here = call(
-        split_tokens,
-        [(piece, VMEM), (piece, VMEM), (shape(2, 32, wide), VMEM)],
+    arrays = [
+        pltpu.with_memory_space_constraint(one, pltpu.HBM) for one in (q, k, v, tq, tk, tv, gap)
+    ]
+    sems = pltpu.SemaphoreType.DMA((6, 2))
+    sent = call(send_tokens, [(piece, VMEM)], [HBM] * 6, 2, (sems,))(*arrays[:6])[0]
+    got = swap(sent, "c")
+    kept, gap_here = call(
+        keep_tokens,
+        [(piece, VMEM), (shape(2, 32, wide), VMEM)],
         [HBM] * 7,
-        4,
-        (pltpu.SemaphoreType.DMA((6, 2, 2)), pltpu.SemaphoreType.DMA((2,))),
-    )(*(pltpu.with_memory_space_constraint(one, pltpu.HBM) for one in arrays))
-    got = swap(sent, "c")
+        2,
+        (sems, pltpu.SemaphoreType.DMA((2,))),
+    )(*arrays)
     packed = call(
         pack_heads,
         [(shape(chips, SLOT, HD), VMEM)],
@@ -500,11 +497,7 @@
     )(kept, got, gap_here)[0]
     mine = exchange(packed)
 
-    rows = chips * PIECE
-    part = lax.axis_index(BLOCK_AXES) % PARTS
-    short = (jnp.arange(rows) % PIECE >= 16) & (part == 1)
-    mask = jnp.where(short, 0.0, 1.0).astype(F32)[None]
-    back = exchange(attention(chips, mine, mask))
+    back = exchange(attention(chips, mine))
 
     fpiece = shape(3, KROWS, feat)
     sent, kept = call(

time: 108 us -> 106 us (0.981)
  waiting for transfers between devices: 7.55 us -> 6.27 us
    pallas_call x1, Pallas kernels: 6.65 us -> 4.87 us  [attention(): call(forward_theirs, [(w, VMEM), (shape(chips, PIECE, 2 * HD), VMEM), (sh...]
    ppermute x6, waiting for transfers between devices: 7.55 us -> 6.27 us  [swap(): return lax.ppermute(array, axis, SWAP)]
    pallas_call x1 -> x2, Pallas kernels: 1.58 us -> 2.42 us  [the longest x1 1.3 us: per_device(): call(keep_tokens, [(piece, VMEM), (shape(2, 32, wide), VMEM)], [HBM] * 7,...]
where the time goes in v7:
time: 106 us
  blocking collectives  67 us (63%)
  Pallas kernels  21.7 us (20%)
  starting transfers between devices  10 us (9%)
  waiting for transfers between devices  6.27 us (6%)
    all_to_all x2, blocking collectives, exchange(): return lax.all_to_all(array, BLOCK_AXES, 0, 0, tiled=True)  67 us
    ppermute x6, starting transfers between devices, swap(): return lax.ppermute(array, axis, SWAP)  10 us
    ppermute x6, waiting for transfers between devices, swap(): return lax.ppermute(array, axis, SWAP)  6.27 us
    pallas_call x1, Pallas kernels, attention(): call(forward_theirs, [(w, VMEM), (shape(chips, PIECE, 2 * HD), VMEM), (sh...  4.87 us
    pallas_call x1, Pallas kernels, attention(): call(forward_mine, [(q, VMEM), (qq, VMEM), (w, HBM), (stats, VMEM), (sums...  4.72 us
    pallas_call x1, Pallas kernels, attention(): call(backward_theirs, [(key_piece, VMEM), (shape(rows, HD), VMEM), (stats...  3.69 us
    pallas_call x1, Pallas kernels, attention(): call(backward_mine, [(key_piece, VMEM), (shape(chips, PIECE, HD), VMEM)],...  3.38 us
  transfers between devices with their start and end apart: 6, of which 3 were waited for; matrix products, arithmetic and copies ran while one was open for 0% of the time, Pallas kernels for 14%

profile of v7, /device:TPU:1, one launch (start us, length us, event | category | flops | bytes accessed | tf_op | source)
XLA Modules:
  0.0 105.7 jit_solution(11794860289390281052)
XLA Ops:
  0.6 1.1 %shard_map.111 = bf16[6,64,640]{2,1,0:T(8,128)(2,1)S(1)} custom-call(bf16[128,640]{1,0:T(8,128)(2,1)} %refs_0_.3, bf16[128,640]{1,0:T(8,128)(2,1)} %refs_1_.3, bf16[128,640]{1,0:T(8,128)(2,1)} %refs_2_.3, bf16[128,640]{1,0:T(8,128)(2,1)} %refs_3_.3, bf16[128,640]{1,0:T(8,128)(2,1)} %refs_4_.3, bf16[128,640]{1,0:T(8,128)(2,1)} %refs_5_.3), custom_call_target="tpu_custom_call" | custom-call | bytes 1000000 | tf_op jit(solution)/shard_map/pallas_call | solution.py:482
  1.8 1.5 %collective-permute-start = (bf16[6,64,640]{2,1,0:T(8,128)(2,1)S(1)}, bf16[6,64,640]{2,1,0:T(8,128)(2,1)S(1)}, u32[]{:S(2)}, u32[]{:S(2)}) collective-permute-start(bf16[6,64,640]{2,1,0:T(8,128)(2,1)S(1)} %shard_map.111), channel_id=1, source_target_pairs={{0,1},{1,0},{2,3},{3,2},{4,5},{5,4},{6,7},{7,6},{8,9},{9,8},{10,11... | collective-permute-start | bytes 1474568 | tf_op jit(solution)/shard_map/ppermute | solution.py:394
  3.2 1.3 %shard_map.110 = (bf16[6,64,640]{2,1,0:T(8,128)(2,1)S(1)}, bf16[2,32,1280]{2,1,0:T(8,128)(2,1)S(1)}) custom-call(bf16[128,640]{1,0:T(8,128)(2,1)} %refs_0_.3, bf16[128,640]{1,0:T(8,128)(2,1)} %refs_1_.3, bf16[128,640]{1,0:T(8,128)(2,1)} %refs_2_.3, bf16[128,640]{1,0:T(8,128)(2,1)} %refs_3_.3, bf16[128,640]{1,0:T(8,128)(2,1)} %refs_4_.3, ...), custom_call_target="tpu_custom_call" | custom-call | bytes 1000000 | tf_op jit(solution)/shard_map/pallas_call | solution.py:484
  4.5 0.2 collective-permute-done.got
  4.7 0.4 shard_map.112
  5.1 41.6 %all_to_all.10.mine = bf16[32,328,128]{2,1,0:T(8,128)(2,1)S(1)} all-to-all(bf16[32,328,128]{2,1,0:T(8,128)(2,1)S(1)} %shard_map.112), channel_id=1, replica_groups=mesh['zl'=2,'y'=4,'x'=4,'zh'=2,'c'=2] {'zl','y','x'}, dimensions={0} | all-to-all | bytes 5373952 | tf_op jit(solution)/shard_map/all_to_all | solution.py:390
  46.8 2.1 %collective-permute-start.1 = (bf16[32,328,128]{2,1,0:T(8,128)(2,1)S(1)}, bf16[32,328,128]{2,1,0:T(8,128)(2,1)S(1)}, u32[]{:S(2)}, u32[]{:S(2)}) collective-permute-start(bf16[32,328,128]{2,1,0:T(8,128)(2,1)S(1)} %all_to_all.10.mine), channel_id=1, source_target_pairs={{0,1},{1,0},{2,3},{3,2},{4,5},{5,4},{6,7},{7,6},{8,9},{9,8},{10,11... | collective-permute-start | bytes 8060936 | tf_op jit(solution)/shard_map/ppermute | solution.py:394
  48.9 3.4 %collective-permute-start.2 = (bf16[32,16,128]{2,1,0:T(8,128)(2,1)S(1)}, bf16[32,16,128]{2,1,0:T(8,128)(2,1)S(1)}, u32[]{:S(2)}, u32[]{:S(2)}) collective-permute-start(bf16[32,16,128]{2,1,0:T(8,128)(2,1)S(1)} %get-tuple-element.37), channel_id=1, source_target_pairs={{0,2},{2,0},{1,3},{3,1},{4,6},{6,4},{5,7},{7,5},{8,10},{10,8},{9,1... | collective-permute-start | bytes 393224 | tf_op jit(solution)/shard_map/ppermute | solution.py:394
  52.3 4.7 %shard_map.113 = (bf16[3,256,128]{2,1,0:T(8,128)(2,1)S(1)}, bf16[3,256,256]{2,1,0:T(8,128)(2,1)S(1)}, bf16[3,2048,256]{2,1,0:T(8,128)(2,1)}, f32[3,1,256]{2,1,0:...) custom-call(bf16[32,328,128]{2,1,0:T(8,128)(2,1)S(1)} %all_to_all.10.mine), custom_call_target="tpu_custom_call" | custom-call | flops 2415919104 | bytes 7000000 | tf_op jit(solution)/shard_map/pallas_call | solution.py:424
  57.0 0.0 collective-permute-done.1.theirs
  57.0 4.9 %shard_map.115 = (bf16[3,2048,256]{2,1,0:T(8,128)(2,1)S(1)}, bf16[32,24,256]{2,1,0:T(8,128)(2,1)S(1)}, bf16[32,16,256]{2,1,0:T(8,128)(2,1)S(1)}, f32[3,256,256]{2,1,0:T(8,128)S(1)}, f32[2,3,1,256]{3,2,1,0:T(1,128)S(1)}) custom-call(bf16[32,328,128]{2,1,0:T(8,128)(2,1)S(1)} %collective-permute-done.1.theirs, ...), custom_call_target="tpu_custom_call" | custom-call | flops 2415919104 | bytes 7000000 | tf_op jit(solution)/shard_map/pallas_call | solution.py:433
  61.9 0.0 collective-permute-done.2.gap_got
  61.9 0.0 copy-start
  61.9 3.7 %shard_map.116 = (bf16[32,64,256]{2,1,0:T(8,128)(2,1)S(1)}, bf16[768,128]{1,0:T(8,128)(2,1)S(1)}, f32[3,1,256]{2,1,0:T(1,128)S(1)}, f32[128,768]{1,0:T(8,128)S(1)}) custom-call(bf16[32,328,128]{2,1,0:T(8,128)(2,1)S(1)} %collective-permute-done.1.theirs, bf16[32,16,128]{2,1,0:T(8,128)(2,1)S(1)} %get-tuple-element.36.gap_kept, ...), custom_call_target="tpu_custom_call" | custom-call | flops 3221225472 | bytes 7000000 | tf_op jit(solution)/shard_map/pallas_call | solution.py:448
  65.6 0.4 collective-permute-start.4
  66.0 0.0 collective-permute-start.3
  66.0 0.0 copy-done
  66.0 3.4 %shard_map.117 = (bf16[32,64,256]{2,1,0:T(8,128)(2,1)S(1)}, bf16[32,24,128]{2,1,0:T(8,128)(2,1)S(1)}) custom-call(bf16[32,328,128]{2,1,0:T(8,128)(2,1)S(1)} %all_to_all.10.mine, bf16[3,256,128]{2,1,0:T(8,128)(2,1)S(1)} %get-tuple-element.35.q_ref, bf16[768,128]{1,0:T(8,128)(2,1)S(1)} %get-tuple-element.45.cot_ref, ...), custom_call_target="tpu_custom_call" | custom-call | flops 3221225472 | bytes 7000000 | tf_op jit(solution)/shard_map/pallas_call | solution.py:460
  69.4 5.8 %collective-permute-done.3.got = bf16[32,16,256]{2,1,0:T(8,128)(2,1)S(1)} collective-permute-done((bf16[32,16,256]{2,1,0:T(8,128)(2,1)S(1)}, bf16[32,16,256]{2,1,0:T(8,128)(2,1)S(1)}, u32[]{:S(2)}, u32[]{:S(2)}) %collective-permute-start.3) | collective-permute-done | bytes 262176 | tf_op jit(solution)/shard_map/ppermute | solution.py:394
  75.1 0.0 collective-permute-done.4.theirs
  75.1 0.3 shard_map.118
  75.5 25.3 %all_to_all.11.r_ref = bf16[32,200,128]{2,1,0:T(8,128)(2,1)S(1)} all-to-all(bf16[32,200,128]{2,1,0:T(8,128)(2,1)S(1)} %shard_map.118), channel_id=1, replica_groups=mesh['zl'=2,'y'=4,'x'=4,'zh'=2,'c'=2] {'zl','y','x'}, dimensions={0} | all-to-all | bytes 3276800 | tf_op jit(solution)/shard_map/all_to_all | solution.py:390
  100.8 0.2 shard_map.120
  101.0 2.7 %collective-permute-start.5 = (bf16[3,64,640]{2,1,0:T(8,128)(2,1)S(1)}, bf16[3,64,640]{2,1,0:T(8,128)(2,1)S(1)}, u32[]{:S(2)}, u32[]{:S(2)}) collective-permute-start(bf16[3,64,640]{2,1,0:T(8,128)(2,1)S(1)} %get-tuple-element.57), channel_id=1, source_target_pairs={{0,1},{1,0},{2,3},{3,2},{4,5},{5,4},{6,7},{7,6},{8,9},{9,8},{10,11... | collective-permute-start | bytes 737288 | tf_op jit(solution)/shard_map/ppermute | solution.py:394
  103.7 0.8 shard_map.119
  104.5 0.3 collective-permute-done.5.got
  104.8 0.8 shard_map.121
  (1 shorter events, 0.0 us)
Async XLA Ops:
  1.8 3.0 %collective-permute-start = (bf16[6,64,640]{2,1,0:T(8,128)(2,1)S(1)}, bf16[6,64,640]{2,1,0:T(8,128)(2,1)S(1)}, u32[]{:S(2)}, u32[]{:S(2)}) collective-permute-start(bf16[6,64,640]{2,1,0:T(8,128)(2,1)S(1)} %shard_map.111), channel_id=1, source_target_pairs={{0,1},{1,0},{2,3},{3,2},{4,5},{5,4},{6,7},{7,6},{8,9},{9,8},{10,11... | collective-permute-start | bytes 1474568 | tf_op jit(solution)/shard_map/ppermute | solution.py:394
  46.8 10.2 %collective-permute-start.1 = (bf16[32,328,128]{2,1,0:T(8,128)(2,1)S(1)}, bf16[32,328,128]{2,1,0:T(8,128)(2,1)S(1)}, u32[]{:S(2)}, u32[]{:S(2)}) collective-permute-start(bf16[32,328,128]{2,1,0:T(8,128)(2,1)S(1)} %all_to_all.10.mine), channel_id=1, source_target_pairs={{0,1},{1,0},{2,3},{3,2},{4,5},{5,4},{6,7},{7,6},{8,9},{9,8},{10,11... | collective-permute-start | bytes 8060936 | tf_op jit(solution)/shard_map/ppermute | solution.py:394
  48.9 13.0 %collective-permute-start.2 = (bf16[32,16,128]{2,1,0:T(8,128)(2,1)S(1)}, bf16[32,16,128]{2,1,0:T(8,128)(2,1)S(1)}, u32[]{:S(2)}, u32[]{:S(2)}) collective-permute-start(bf16[32,16,128]{2,1,0:T(8,128)(2,1)S(1)} %get-tuple-element.37), channel_id=1, source_target_pairs={{0,2},{2,0},{1,3},{3,1},{4,6},{6,4},{5,7},{7,5},{8,10},{10,8},{9,1... | collective-permute-start | bytes 393224 | tf_op jit(solution)/shard_map/ppermute | solution.py:394
  61.9 4.1 %copy-start = (bf16[3,2048,256]{2,1,0:T(8,128)(2,1)S(1)}, bf16[3,2048,256]{2,1,0:T(8,128)(2,1)}, u32[]{:S(2)}) copy-start(bf16[3,2048,256]{2,1,0:T(8,128)(2,1)} %get-tuple-element.47.w_ref) | copy-start | bytes 9437188
  65.6 9.5 %collective-permute-start.4 = (bf16[32,64,256]{2,1,0:T(8,128)(2,1)S(1)}, bf16[32,64,256]{2,1,0:T(8,128)(2,1)S(1)}, u32[]{:S(2)}, u32[]{:S(2)}) collective-permute-start(bf16[32,64,256]{2,1,0:T(8,128)(2,1)S(1)} %get-tuple-element.53), channel_id=1, source_target_pairs={{0,1},{1,0},{2,3},{3,2},{4,5},{5,4},{6,7},{7,6},{8,9},{9,8},{10,11... | collective-permute-start | bytes 3145736 | tf_op jit(solution)/shard_map/ppermute | solution.py:394
  66.0 9.1 %collective-permute-start.3 = (bf16[32,16,256]{2,1,0:T(8,128)(2,1)S(1)}, bf16[32,16,256]{2,1,0:T(8,128)(2,1)S(1)}, u32[]{:S(2)}, u32[]{:S(2)}) collective-permute-start(bf16[32,16,256]{2,1,0:T(8,128)(2,1)S(1)} %get-tuple-element.52), channel_id=1, source_target_pairs={{0,2},{2,0},{1,3},{3,1},{4,6},{6,4},{5,7},{7,5},{8,10},{10,8},{9,1... | collective-permute-start | bytes 786440 | tf_op jit(solution)/shard_map/ppermute | solution.py:394
  101.0 3.9 %collective-permute-start.5 = (bf16[3,64,640]{2,1,0:T(8,128)(2,1)S(1)}, bf16[3,64,640]{2,1,0:T(8,128)(2,1)S(1)}, u32[]{:S(2)}, u32[]{:S(2)}) collective-permute-start(bf16[3,64,640]{2,1,0:T(8,128)(2,1)S(1)} %get-tuple-element.57), channel_id=1, source_target_pairs={{0,1},{1,0},{2,3},{3,2},{4,5},{5,4},{6,7},{7,6},{8,9},{9,8},{10,11... | collective-permute-start | bytes 737288 | tf_op jit(solution)/shard_map/ppermute | solution.py:394

commit v8 on v7

--- a/solution.py
+++ b/solution.py
@@ -27,7 +27,7 @@
 ANY = pl.BlockSpec(memory_space=pl.ANY)
 
 
-def call(body, outs, ins, limit, scratch=(), flops=0, exps=0, moved=1_000_000):
+def call(body, outs, ins, limit, scratch=(), flops=0, exps=0, moved=1_000_000, aliases=None):
     return pl.pallas_call(
         body,
         out_shape=[
@@ -36,6 +36,7 @@
         in_specs=ins,
         out_specs=[place for _, place in outs],
         scratch_shapes=list(scratch),
+        input_output_aliases=aliases or {},
         compiler_params=pltpu.CompilerParams(vmem_limit_bytes=limit * 1024 * 1024),
         cost_estimate=pl.CostEstimate(flops=flops, bytes_accessed=moved, transcendentals=exps),
     )
@@ -128,15 +129,6 @@
             else:
                 which, eight = GAPS[part][to]
                 out[chip, rows, :] = gap[which, 8 * eight : 8 * eight + 8, gcols]
-
-
-def split_gaps(mine, sent, kept, sems):
-    run_all(
-        [
-            pltpu.make_async_copy(mine.at[:, low : low + 16, :], dst, sems.at[at])
-            for at, (dst, low) in enumerate(((sent, 312), (kept, 304)))
-        ]
-    )
 
 
 def fold(x, op):
@@ -204,8 +196,13 @@
         close(tiles - 1)
 
 
-def forward_mine(mine, q_ref, qq_ref, w_hbm, m_ref, sums_ref, acc_ref, stage, w_ref, sems, *scratch):
+def forward_mine(
+    mine, q_ref, qq_ref, w_hbm, m_ref, sums_ref, acc_ref, gap_sent, gap_kept,
+    stage, w_ref, sems, *scratch
+):
     for s in range(mine.shape[0]):
+        gap_sent[s] = mine[s, 312:328, :]
+        gap_kept[s] = mine[s, 304:320, :]
         stage[PIECE * s : PIECE * s + PIECE, 0:HD] = mine[s, 256:280, :].astype(F32)
         stage[PIECE * s : PIECE * s + PIECE, HD:] = mine[s, 280:304, :].astype(F32)
     tiles = q_ref.shape[0]
@@ -351,7 +348,22 @@
     kept[...] = f_ref[core()]
 
 
-def finish_outs(r_ref, primal, tangent, o_ref):
+def place_grads(piece, who, outs, sems):
+    return [
+        pltpu.make_async_copy(
+            piece.at[at, 32 * half : 32 * half + 32, :],
+            ref.at[pl.ds(half_row(half, who), 32), :],
+            sems.at[at, half],
+        )
+        for at, ref in enumerate(outs)
+        for half in range(2)
+    ]
+
+
+def finish_outs(r_ref, kept, primal, tangent, dq, dk, dv, o_ref, sems):
+    copies = place_grads(kept, core(), (dq, dk, dv), sems)
+    for copy in copies:
+        copy.start()
     wide = o_ref.shape[3]
     for head in range(wide // HD):
         cols = slice(head * HD, head * HD + HD)
@@ -368,14 +380,12 @@
     for side, ref in enumerate((primal, tangent)):
         for which, who in enumerate((group(), 1 - group())):
             ref[:, pl.ds(pl.multiple_of(wide * who, HD), wide)] = o_ref[which, side]
-
-
-def finish_grads(kept, got, dq, dk, dv):
-    for at, ref in enumerate((dq, dk, dv)):
-        for half in range(2):
-            rows = slice(32 * half, 32 * half + 32)
-            for piece, who in ((kept, core()), (got, 1 - core())):
-                ref[pl.ds(half_row(half, who), 32), :] = piece[at, rows, :]
+    for copy in copies:
+        copy.wait()
+
+
+def finish_grads(got, dq_in, dk_in, dv_in, dq, dk, dv, sems):
+    run_all(place_grads(got, 1 - core(), (dq, dk, dv), sems))
 
 
 def shape(*dims, dtype=BF):
@@ -399,11 +409,6 @@
     rows, subs = tiles * QT, length // SUB
     flops = 2 * length * rows * HD
     gpiece = shape(chips, 16, HD)
-    gap_sent, gap_kept = call(
-        split_gaps, [(gpiece, VMEM), (gpiece, VMEM)], [ANY], 2, (pltpu.SemaphoreType.DMA((2,)),),
-        moved=500_000,
-    )(mine)
-    gap_got = swap(gap_sent, "zh")
     theirs = swap(mine, "c")
     q, qq = shape(tiles, QT, HD), shape(tiles, QT, 2 * HD)
     w = shape(tiles, length, QT)
@@ -421,14 +426,16 @@
         pltpu.VMEM((SUB, rows), BF),
     )
     stage = pltpu.VMEM((rows, 2 * HD), F32)
-    q, qq, w1, m1, sums1, acc1 = call(
+    q, qq, w1, m1, sums1, acc1, gap_sent, gap_kept = call(
         forward_mine,
-        [(q, VMEM), (qq, VMEM), (w, HBM), (stats, VMEM), (sums, VMEM), (acc, VMEM)],
+        [(q, VMEM), (qq, VMEM), (w, HBM), (stats, VMEM), (sums, VMEM), (acc, VMEM)]
+        + [(gpiece, VMEM)] * 2,
         [VMEM],
         30,
         (stage,) + tiles_of + scratch,
         6 * flops, length * rows, 7_000_000,
     )(mine)
+    gap_got = swap(gap_sent, "zh")
     key_piece = shape(chips, KROWS, 2 * HD)
     w2, pieces, cross, o, share = call(
         forward_theirs,
@@ -506,10 +513,14 @@
     )(back)
     got = swap(sent, "c")
     small, large = shape(32, 2 * wide), shape(local, feat)
-    primal, tangent = call(
-        finish_outs, [(small, VMEM)] * 2, [VMEM], 8, (pltpu.VMEM((2, 2, 32, wide), BF),)
-    )(back)
-    dq, dk, dv = call(finish_grads, [(large, VMEM)] * 3, [VMEM] * 2, 8)(kept, got)
+    sems = pltpu.SemaphoreType.DMA((3, 2))
+    primal, tangent, *grads = call(
+        finish_outs, [(small, VMEM)] * 2 + [(large, HBM)] * 3, [VMEM] * 2, 8,
+        (pltpu.VMEM((2, 2, 32, wide), BF), sems),
+    )(back, kept)
+    dq, dk, dv = call(
+        finish_grads, [(large, HBM)] * 3, [VMEM] + [HBM] * 3, 4, (sems,), aliases={1: 0, 2: 1, 3: 2}
+    )(got, *grads)
     return primal, tangent, dq, dk, dv
 
 

time: 106 us -> 106 us (level)
  waiting for transfers between devices: 6.27 us -> 3.71 us
  starting transfers between devices: 10 us -> 12.5 us
    ppermute x6, waiting for transfers between devices: 6.27 us -> 3.71 us  [swap(): return lax.ppermute(array, axis, SWAP)]
    ppermute x6, starting transfers between devices: 10 us -> 12.5 us  [swap(): return lax.ppermute(array, axis, SWAP)]
    pallas_call x3 -> x2, Pallas kernels: 1.68 us -> 2.24 us  [the longest x1 1.48 us: per_device(): call(finish_outs, [(small, VMEM)] * 2 + [(large, HBM)] * 3, [VMEM] * 2, 8...]
  transfers between devices with their start and end apart: 6 -> 6, of which waited for: 3 -> 2; matrix products, arithmetic and copies ran while one was open for 0% -> 0% of each run, Pallas kernels for 14% -> 15%
where the time goes in v8:
time: 106 us
  blocking collectives  66.9 us (63%)
  Pallas kernels  22.1 us (21%)
  starting transfers between devices  12.5 us (12%)
  waiting for transfers between devices  3.71 us (4%)
    all_to_all x2, blocking collectives, exchange(): return lax.all_to_all(array, BLOCK_AXES, 0, 0, tiled=True)  66.9 us
    ppermute x6, starting transfers between devices, swap(): return lax.ppermute(array, axis, SWAP)  12.5 us
    pallas_call x1, Pallas kernels, attention(): call(forward_theirs, [(w, VMEM), (shape(chips, PIECE, 2 * HD), VMEM), (sh...  4.86 us
    pallas_call x1, Pallas kernels, attention(): call(forward_mine, [(q, VMEM), (qq, VMEM), (w, HBM), (stats, VMEM), (sums...  4.76 us
    ppermute x6, waiting for transfers between devices, swap(): return lax.ppermute(array, axis, SWAP)  3.71 us
    pallas_call x1, Pallas kernels, attention(): call(backward_theirs, [(key_piece, VMEM), (shape(rows, HD), VMEM), (stats...  3.49 us
    pallas_call x1, Pallas kernels, attention(): call(backward_mine, [(key_piece, VMEM), (shape(chips, PIECE, HD), VMEM)],...  3.39 us
  transfers between devices with their start and end apart: 6, of which 2 were waited for; matrix products, arithmetic and copies ran while one was open for 0% of the time, Pallas kernels for 15%

profile of v8, /device:TPU:1, one launch (start us, length us, event | category | flops | bytes accessed | tf_op | source)
XLA Modules:
  0.0 106.1 jit_solution(11325253770312541796)
XLA Ops:
  0.6 1.1 %shard_map.111 = bf16[6,64,640]{2,1,0:T(8,128)(2,1)S(1)} custom-call(bf16[128,640]{1,0:T(8,128)(2,1)} %refs_0_.3, bf16[128,640]{1,0:T(8,128)(2,1)} %refs_1_.3, bf16[128,640]{1,0:T(8,128)(2,1)} %refs_2_.3, bf16[128,640]{1,0:T(8,128)(2,1)} %refs_3_.3, bf16[128,640]{1,0:T(8,128)(2,1)} %refs_4_.3, bf16[128,640]{1,0:T(8,128)(2,1)} %refs_5_.3), custom_call_target="tpu_custom_call" | custom-call | bytes 1000000 | tf_op jit(solution)/shard_map/pallas_call | solution.py:489
  1.8 1.5 %collective-permute-start = (bf16[6,64,640]{2,1,0:T(8,128)(2,1)S(1)}, bf16[6,64,640]{2,1,0:T(8,128)(2,1)S(1)}, u32[]{:S(2)}, u32[]{:S(2)}) collective-permute-start(bf16[6,64,640]{2,1,0:T(8,128)(2,1)S(1)} %shard_map.111), channel_id=1, source_target_pairs={{0,1},{1,0},{2,3},{3,2},{4,5},{5,4},{6,7},{7,6},{8,9},{9,8},{10,11... | collective-permute-start | bytes 1474568 | tf_op jit(solution)/shard_map/ppermute | solution.py:404
  3.2 1.3 %shard_map.110 = (bf16[6,64,640]{2,1,0:T(8,128)(2,1)S(1)}, bf16[2,32,1280]{2,1,0:T(8,128)(2,1)S(1)}) custom-call(bf16[128,640]{1,0:T(8,128)(2,1)} %refs_0_.3, bf16[128,640]{1,0:T(8,128)(2,1)} %refs_1_.3, bf16[128,640]{1,0:T(8,128)(2,1)} %refs_2_.3, bf16[128,640]{1,0:T(8,128)(2,1)} %refs_3_.3, bf16[128,640]{1,0:T(8,128)(2,1)} %refs_4_.3, ...), custom_call_target="tpu_custom_call" | custom-call | bytes 1000000 | tf_op jit(solution)/shard_map/pallas_call | solution.py:491
  4.5 0.2 collective-permute-done.got
  4.7 0.4 shard_map.112
  5.1 41.6 %all_to_all.10.mine = bf16[32,328,128]{2,1,0:T(8,128)(2,1)S(1)} all-to-all(bf16[32,328,128]{2,1,0:T(8,128)(2,1)S(1)} %shard_map.112), channel_id=1, replica_groups=mesh['zl'=2,'y'=4,'x'=4,'zh'=2,'c'=2] {'zl','y','x'}, dimensions={0} | all-to-all | bytes 5373952 | tf_op jit(solution)/shard_map/all_to_all | solution.py:400
  46.8 2.1 %collective-permute-start.1 = (bf16[32,328,128]{2,1,0:T(8,128)(2,1)S(1)}, bf16[32,328,128]{2,1,0:T(8,128)(2,1)S(1)}, u32[]{:S(2)}, u32[]{:S(2)}) collective-permute-start(bf16[32,328,128]{2,1,0:T(8,128)(2,1)S(1)} %all_to_all.10.mine), channel_id=1, source_target_pairs={{0,1},{1,0},{2,3},{3,2},{4,5},{5,4},{6,7},{7,6},{8,9},{9,8},{10,11... | collective-permute-start | bytes 8060936 | tf_op jit(solution)/shard_map/ppermute | solution.py:404
  48.9 4.8 %shard_map.113 = (bf16[3,256,128]{2,1,0:T(8,128)(2,1)S(1)}, bf16[3,256,256]{2,1,0:T(8,128)(2,1)S(1)}, bf16[3,2048,256]{2,1,0:T(8,128)(2,1)}, f32[3,1,256]{2,1,0:...) custom-call(bf16[32,328,128]{2,1,0:T(8,128)(2,1)S(1)} %all_to_all.10, ...), custom_call_target="tpu_custom_call" | custom-call | flops 2415919104 | bytes 7000000 | tf_op jit(solution)/shard_map/pallas_call | solution.py:429
  53.6 3.6 %collective-permute-start.2 = (bf16[32,16,128]{2,1,0:T(8,128)(2,1)S(1)}, bf16[32,16,128]{2,1,0:T(8,128)(2,1)S(1)}, u32[]{:S(2)}, u32[]{:S(2)}) collective-permute-start(bf16[32,16,128]{2,1,0:T(8,128)(2,1)S(1)} %get-tuple-element.40), channel_id=1, source_target_pairs={{0,2},{2,0},{1,3},{3,1},{4,6},{6,4},{5,7},{7,5},{8,10},{10,8},{9,1... | collective-permute-start | bytes 393224 | tf_op jit(solution)/shard_map/ppermute | solution.py:404
  57.2 0.0 collective-permute-done.1.theirs
  57.2 4.9 %shard_map.114 = (bf16[3,2048,256]{2,1,0:T(8,128)(2,1)S(1)}, bf16[32,24,256]{2,1,0:T(8,128)(2,1)S(1)}, bf16[32,16,256]{2,1,0:T(8,128)(2,1)S(1)}, f32[3,256,256]{2,1,0:T(8,128)S(1)}, f32[2,3,1,256]{3,2,1,0:T(1,128)S(1)}) custom-call(bf16[32,328,128]{2,1,0:T(8,128)(2,1)S(1)} %collective-permute-done.1.theirs, ...), custom_call_target="tpu_custom_call" | custom-call | flops 2415919104 | bytes 7000000 | tf_op jit(solution)/shard_map/pallas_call | solution.py:440
  62.1 0.0 collective-permute-done.2.gap_got
  62.1 0.0 copy-start
  62.1 3.5 %shard_map.115 = (bf16[32,64,256]{2,1,0:T(8,128)(2,1)S(1)}, bf16[768,128]{1,0:T(8,128)(2,1)S(1)}, f32[3,1,256]{2,1,0:T(1,128)S(1)}, f32[128,768]{1,0:T(8,128)S(1)}) custom-call(bf16[32,328,128]{2,1,0:T(8,128)(2,1)S(1)} %collective-permute-done.1.theirs, bf16[32,16,128]{2,1,0:T(8,128)(2,1)S(1)} %get-tuple-element.39.gap_kept, ...), custom_call_target="tpu_custom_call" | custom-call | flops 3221225472 | bytes 7000000 | tf_op jit(solution)/shard_map/pallas_call | solution.py:455
  65.6 0.4 collective-permute-start.4
  65.9 2.2 %collective-permute-start.3 = (bf16[32,16,256]{2,1,0:T(8,128)(2,1)S(1)}, bf16[32,16,256]{2,1,0:T(8,128)(2,1)S(1)}, u32[]{:S(2)}, u32[]{:S(2)}) collective-permute-start(bf16[32,16,256]{2,1,0:T(8,128)(2,1)S(1)} %get-tuple-element.55), channel_id=1, source_target_pairs={{0,2},{2,0},{1,3},{3,1},{4,6},{6,4},{5,7},{7,5},{8,10},{10,8},{9,1... | collective-permute-start | bytes 786440 | tf_op jit(solution)/shard_map/ppermute | solution.py:404
  68.2 0.0 copy-done
  68.2 3.4 %shard_map.116 = (bf16[32,64,256]{2,1,0:T(8,128)(2,1)S(1)}, bf16[32,24,128]{2,1,0:T(8,128)(2,1)S(1)}) custom-call(bf16[32,328,128]{2,1,0:T(8,128)(2,1)S(1)} %all_to_all.10.mine, bf16[3,256,128]{2,1,0:T(8,128)(2,1)S(1)} %get-tuple-element.38.q_ref, bf16[768,128]{1,0:T(8,128)(2,1)S(1)} %get-tuple-element.48.cot_ref, ...), custom_call_target="tpu_custom_call" | custom-call | flops 3221225472 | bytes 7000000 | tf_op jit(solution)/shard_map/pallas_call | solution.py:467
  71.6 3.5 %collective-permute-done.3.got = bf16[32,16,256]{2,1,0:T(8,128)(2,1)S(1)} collective-permute-done((bf16[32,16,256]{2,1,0:T(8,128)(2,1)S(1)}, bf16[32,16,256]{2,1,0:T(8,128)(2,1)S(1)}, u32[]{:S(2)}, u32[]{:S(2)}) %collective-permute-start.3) | collective-permute-done | bytes 262176 | tf_op jit(solution)/shard_map/ppermute | solution.py:404
  75.1 0.0 collective-permute-done.4.theirs
  75.1 0.3 shard_map.117
  75.4 25.3 %all_to_all.11.r_ref = bf16[32,200,128]{2,1,0:T(8,128)(2,1)S(1)} all-to-all(bf16[32,200,128]{2,1,0:T(8,128)(2,1)S(1)} %shard_map.117), channel_id=1, replica_groups=mesh['zl'=2,'y'=4,'x'=4,'zh'=2,'c'=2] {'zl','y','x'}, dimensions={0} | all-to-all | bytes 3276800 | tf_op jit(solution)/shard_map/all_to_all | solution.py:400
  100.7 0.2 shard_map.118
  100.9 2.7 %collective-permute-start.5 = (bf16[3,64,640]{2,1,0:T(8,128)(2,1)S(1)}, bf16[3,64,640]{2,1,0:T(8,128)(2,1)S(1)}, u32[]{:S(2)}, u32[]{:S(2)}) collective-permute-start(bf16[3,64,640]{2,1,0:T(8,128)(2,1)S(1)} %get-tuple-element.60), channel_id=1, source_target_pairs={{0,1},{1,0},{2,3},{3,2},{4,5},{5,4},{6,7},{7,6},{8,9},{9,8},{10,11... | collective-permute-start | bytes 737288 | tf_op jit(solution)/shard_map/ppermute | solution.py:404
  103.6 1.5 %shard_map.119 = (bf16[32,2560]{1,0:T(8,128)(2,1)}, bf16[32,2560]{1,0:T(8,128)(2,1)}, bf16[128,640]{1,0:T(8,128)(2,1)}, bf16[128,640]{1,0:T(8,128)(2,1)}, bf16[128,640]{1,0:T(8,128)(2,1)}) custom-call(bf16[32,200,128]{2,1,0:T(8,128)(2,1)S(1)} %all_to_all.11.r_ref, bf16[3,64,640]{2,1,0:T(8,128)(2,1)S(1)} %get-tuple-element.57.kept), custom_call_target="tpu_custom_call" | custom-call | bytes 1000000 | tf_op jit(solution)/shard_map/pallas_call | solution.py:517
  105.1 0.0 collective-permute-done.5.got
  105.1 0.8 shard_map.120
Async XLA Ops:
  1.8 3.0 %collective-permute-start = (bf16[6,64,640]{2,1,0:T(8,128)(2,1)S(1)}, bf16[6,64,640]{2,1,0:T(8,128)(2,1)S(1)}, u32[]{:S(2)}, u32[]{:S(2)}) collective-permute-start(bf16[6,64,640]{2,1,0:T(8,128)(2,1)S(1)} %shard_map.111), channel_id=1, source_target_pairs={{0,1},{1,0},{2,3},{3,2},{4,5},{5,4},{6,7},{7,6},{8,9},{9,8},{10,11... | collective-permute-start | bytes 1474568 | tf_op jit(solution)/shard_map/ppermute | solution.py:404
  46.8 10.4 %collective-permute-start.1 = (bf16[32,328,128]{2,1,0:T(8,128)(2,1)S(1)}, bf16[32,328,128]{2,1,0:T(8,128)(2,1)S(1)}, u32[]{:S(2)}, u32[]{:S(2)}) collective-permute-start(bf16[32,328,128]{2,1,0:T(8,128)(2,1)S(1)} %all_to_all.10.mine), channel_id=1, source_target_pairs={{0,1},{1,0},{2,3},{3,2},{4,5},{5,4},{6,7},{7,6},{8,9},{9,8},{10,11... | collective-permute-start | bytes 8060936 | tf_op jit(solution)/shard_map/ppermute | solution.py:404
  53.6 8.4 %collective-permute-start.2 = (bf16[32,16,128]{2,1,0:T(8,128)(2,1)S(1)}, bf16[32,16,128]{2,1,0:T(8,128)(2,1)S(1)}, u32[]{:S(2)}, u32[]{:S(2)}) collective-permute-start(bf16[32,16,128]{2,1,0:T(8,128)(2,1)S(1)} %get-tuple-element.40), channel_id=1, source_target_pairs={{0,2},{2,0},{1,3},{3,1},{4,6},{6,4},{5,7},{7,5},{8,10},{10,8},{9,1... | collective-permute-start | bytes 393224 | tf_op jit(solution)/shard_map/ppermute | solution.py:404
  62.1 6.1 %copy-start = (bf16[3,2048,256]{2,1,0:T(8,128)(2,1)S(1)}, bf16[3,2048,256]{2,1,0:T(8,128)(2,1)}, u32[]{:S(2)}) copy-start(bf16[3,2048,256]{2,1,0:T(8,128)(2,1)} %get-tuple-element.50.w_ref) | copy-start | bytes 9437188
  65.6 9.5 %collective-permute-start.4 = (bf16[32,64,256]{2,1,0:T(8,128)(2,1)S(1)}, bf16[32,64,256]{2,1,0:T(8,128)(2,1)S(1)}, u32[]{:S(2)}, u32[]{:S(2)}) collective-permute-start(bf16[32,64,256]{2,1,0:T(8,128)(2,1)S(1)} %get-tuple-element.56), channel_id=1, source_target_pairs={{0,1},{1,0},{2,3},{3,2},{4,5},{5,4},{6,7},{7,6},{8,9},{9,8},{10,11... | collective-permute-start | bytes 3145736 | tf_op jit(solution)/shard_map/ppermute | solution.py:404
  65.9 9.1 %collective-permute-start.3 = (bf16[32,16,256]{2,1,0:T(8,128)(2,1)S(1)}, bf16[32,16,256]{2,1,0:T(8,128)(2,1)S(1)}, u32[]{:S(2)}, u32[]{:S(2)}) collective-permute-start(bf16[32,16,256]{2,1,0:T(8,128)(2,1)S(1)} %get-tuple-element.55), channel_id=1, source_target_pairs={{0,2},{2,0},{1,3},{3,1},{4,6},{6,4},{5,7},{7,5},{8,10},{10,8},{9,1... | collective-permute-start | bytes 786440 | tf_op jit(solution)/shard_map/ppermute | solution.py:404
  100.9 4.2 %collective-permute-start.5 = (bf16[3,64,640]{2,1,0:T(8,128)(2,1)S(1)}, bf16[3,64,640]{2,1,0:T(8,128)(2,1)S(1)}, u32[]{:S(2)}, u32[]{:S(2)}) collective-permute-start(bf16[3,64,640]{2,1,0:T(8,128)(2,1)S(1)} %get-tuple-element.60), channel_id=1, source_target_pairs={{0,1},{1,0},{2,3},{3,2},{4,5},{5,4},{6,7},{7,6},{8,9},{9,8},{10,11... | collective-permute-start | bytes 737288 | tf_op jit(solution)/shard_map/ppermute | solution.py:404

commit v9 on v8

--- a/solution.py
+++ b/solution.py
@@ -63,7 +63,7 @@
 
 
 def part_here():
-    place = lax.axis_index("zl") * 16 + lax.axis_index("y") * 4 + lax.axis_index("x")
+    place = lax.axis_index("x") * 8 + lax.axis_index("zl") * 4 + lax.axis_index("y")
     return lax.rem(place, PARTS)
 
 
@@ -360,7 +360,7 @@
     ]
 
 
-def finish_outs(r_ref, kept, primal, tangent, dq, dk, dv, o_ref, sems):
+def finish_outs(r_ref, kept, primal, tangent, dq, dk, dv, o_ref, sems, out_sems):
     copies = place_grads(kept, core(), (dq, dk, dv), sems)
     for copy in copies:
         copy.start()
@@ -379,7 +379,11 @@
                     ]
     for side, ref in enumerate((primal, tangent)):
         for which, who in enumerate((group(), 1 - group())):
-            ref[:, pl.ds(pl.multiple_of(wide * who, HD), wide)] = o_ref[which, side]
+            lanes = pl.ds(pl.multiple_of(wide * who, HD), wide)
+            copies.append(
+                pltpu.make_async_copy(o_ref.at[which, side], ref.at[:, lanes], out_sems.at[which, side])
+            )
+            copies[-1].start()
     for copy in copies:
         copy.wait()
 
@@ -394,10 +398,11 @@
 
 SWAP = [(0, 1), (1, 0)]
 BLOCK_AXES = ("zl", "y", "x")
+CHIP_AXES = ("x", "zl", "y")
 
 
 def exchange(array):
-    return lax.all_to_all(array, BLOCK_AXES, 0, 0, tiled=True)
+    return lax.all_to_all(array, CHIP_AXES, 0, 0, tiled=True)
 
 
 def swap(array, axis):
@@ -515,8 +520,8 @@
     small, large = shape(32, 2 * wide), shape(local, feat)
     sems = pltpu.SemaphoreType.DMA((3, 2))
     primal, tangent, *grads = call(
-        finish_outs, [(small, VMEM)] * 2 + [(large, HBM)] * 3, [VMEM] * 2, 8,
-        (pltpu.VMEM((2, 2, 32, wide), BF), sems),
+        finish_outs, [(small, HBM)] * 2 + [(large, HBM)] * 3, [VMEM] * 2, 8,
+        (pltpu.VMEM((2, 2, 32, wide), BF), sems, pltpu.SemaphoreType.DMA((2, 2))),
     )(back, kept)
     dq, dk, dv = call(
         finish_grads, [(large, HBM)] * 3, [VMEM] + [HBM] * 3, 4, (sems,), aliases={1: 0, 2: 1, 3: 2}

time: 106 us -> 106 us (level)
  transfers between devices with their start and end apart: 6 -> 6, of which waited for: 2 -> 3; matrix products, arithmetic and copies ran while one was open for 0% -> 0% of each run, Pallas kernels for 15% -> 14%
where the time goes in v9:
time: 106 us
  blocking collectives  65.9 us (62%)
  Pallas kernels  21.5 us (20%)
  starting transfers between devices  13.5 us (13%)
  waiting for transfers between devices  3.9 us (4%)
    all_to_all x2, blocking collectives, exchange(): return lax.all_to_all(array, CHIP_AXES, 0, 0, tiled=True)  65.9 us
    ppermute x6, starting transfers between devices, swap(): return lax.ppermute(array, axis, SWAP)  13.5 us
    pallas_call x1, Pallas kernels, attention(): call(forward_theirs, [(w, VMEM), (shape(chips, PIECE, 2 * HD), VMEM), (sh...  4.87 us
    pallas_call x1, Pallas kernels, attention(): call(forward_mine, [(q, VMEM), (qq, VMEM), (w, HBM), (stats, VMEM), (sums...  4.76 us
    ppermute x6, waiting for transfers between devices, swap(): return lax.ppermute(array, axis, SWAP)  3.9 us
    pallas_call x1, Pallas kernels, attention(): call(backward_theirs, [(key_piece, VMEM), (shape(rows, HD), VMEM), (stats...  3.49 us
    pallas_call x1, Pallas kernels, attention(): call(backward_mine, [(key_piece, VMEM), (shape(chips, PIECE, HD), VMEM)],...  3.39 us
  transfers between devices with their start and end apart: 6, of which 3 were waited for; matrix products, arithmetic and copies ran while one was open for 0% of the time, Pallas kernels for 14%

profile of v9, /device:TPU:1, one launch (start us, length us, event | category | flops | bytes accessed | tf_op | source)
XLA Modules:
  0.0 105.7 jit_solution(18089508476442420647)
XLA Ops:
  0.6 1.1 %shard_map.111 = bf16[6,64,640]{2,1,0:T(8,128)(2,1)S(1)} custom-call(bf16[128,640]{1,0:T(8,128)(2,1)} %refs_0_.3, bf16[128,640]{1,0:T(8,128)(2,1)} %refs_1_.3, bf16[128,640]{1,0:T(8,128)(2,1)} %refs_2_.3, bf16[128,640]{1,0:T(8,128)(2,1)} %refs_3_.3, bf16[128,640]{1,0:T(8,128)(2,1)} %refs_4_.3, bf16[128,640]{1,0:T(8,128)(2,1)} %refs_5_.3), custom_call_target="tpu_custom_call" | custom-call | bytes 1000000 | tf_op jit(solution)/shard_map/pallas_call | solution.py:494
  1.8 1.5 %collective-permute-start = (bf16[6,64,640]{2,1,0:T(8,128)(2,1)S(1)}, bf16[6,64,640]{2,1,0:T(8,128)(2,1)S(1)}, u32[]{:S(2)}, u32[]{:S(2)}) collective-permute-start(bf16[6,64,640]{2,1,0:T(8,128)(2,1)S(1)} %shard_map.111), channel_id=1, source_target_pairs={{0,1},{1,0},{2,3},{3,2},{4,5},{5,4},{6,7},{7,6},{8,9},{9,8},{10,11... | collective-permute-start | bytes 1474568 | tf_op jit(solution)/shard_map/ppermute | solution.py:409
  3.2 1.3 %shard_map.110 = (bf16[6,64,640]{2,1,0:T(8,128)(2,1)S(1)}, bf16[2,32,1280]{2,1,0:T(8,128)(2,1)S(1)}) custom-call(bf16[128,640]{1,0:T(8,128)(2,1)} %refs_0_.3, bf16[128,640]{1,0:T(8,128)(2,1)} %refs_1_.3, bf16[128,640]{1,0:T(8,128)(2,1)} %refs_2_.3, bf16[128,640]{1,0:T(8,128)(2,1)} %refs_3_.3, bf16[128,640]{1,0:T(8,128)(2,1)} %refs_4_.3, ...), custom_call_target="tpu_custom_call" | custom-call | bytes 1000000 | tf_op jit(solution)/shard_map/pallas_call | solution.py:496
  4.5 0.2 collective-permute-done.got
  4.7 0.4 shard_map.112
  5.1 41.4 %all_to_all.10.mine = bf16[32,328,128]{2,1,0:T(8,128)(2,1)S(1)} all-to-all(bf16[32,328,128]{2,1,0:T(8,128)(2,1)S(1)} %shard_map.112), channel_id=1, replica_groups=mesh['zl'=2,'y'=4,'x'=4,'zh'=2,'c'=2] {'x','zl','y'}, dimensions={0} | all-to-all | bytes 5373952 | tf_op jit(solution)/shard_map/all_to_all | solution.py:405
  46.5 2.6 %collective-permute-start.1 = (bf16[32,328,128]{2,1,0:T(8,128)(2,1)S(1)}, bf16[32,328,128]{2,1,0:T(8,128)(2,1)S(1)}, u32[]{:S(2)}, u32[]{:S(2)}) collective-permute-start(bf16[32,328,128]{2,1,0:T(8,128)(2,1)S(1)} %all_to_all.10.mine), channel_id=1, source_target_pairs={{0,1},{1,0},{2,3},{3,2},{4,5},{5,4},{6,7},{7,6},{8,9},{9,8},{10,11... | collective-permute-start | bytes 8060936 | tf_op jit(solution)/shard_map/ppermute | solution.py:409
  49.1 4.8 %shard_map.113 = (bf16[3,256,128]{2,1,0:T(8,128)(2,1)S(1)}, bf16[3,256,256]{2,1,0:T(8,128)(2,1)S(1)}, bf16[3,2048,256]{2,1,0:T(8,128)(2,1)}, f32[3,1,256]{2,1,0:...) custom-call(bf16[32,328,128]{2,1,0:T(8,128)(2,1)S(1)} %all_to_all.10, ...), custom_call_target="tpu_custom_call" | custom-call | flops 2415919104 | bytes 7000000 | tf_op jit(solution)/shard_map/pallas_call | solution.py:434
  53.9 3.6 %collective-permute-start.2 = (bf16[32,16,128]{2,1,0:T(8,128)(2,1)S(1)}, bf16[32,16,128]{2,1,0:T(8,128)(2,1)S(1)}, u32[]{:S(2)}, u32[]{:S(2)}) collective-permute-start(bf16[32,16,128]{2,1,0:T(8,128)(2,1)S(1)} %get-tuple-element.40), channel_id=1, source_target_pairs={{0,2},{2,0},{1,3},{3,1},{4,6},{6,4},{5,7},{7,5},{8,10},{10,8},{9,1... | collective-permute-start | bytes 393224 | tf_op jit(solution)/shard_map/ppermute | solution.py:409
  57.5 0.0 collective-permute-done.1.theirs
  57.5 4.9 %shard_map.114 = (bf16[3,2048,256]{2,1,0:T(8,128)(2,1)S(1)}, bf16[32,24,256]{2,1,0:T(8,128)(2,1)S(1)}, bf16[32,16,256]{2,1,0:T(8,128)(2,1)S(1)}, f32[3,256,256]{2,1,0:T(8,128)S(1)}, f32[2,3,1,256]{3,2,1,0:T(1,128)S(1)}) custom-call(bf16[32,328,128]{2,1,0:T(8,128)(2,1)S(1)} %collective-permute-done.1.theirs, ...), custom_call_target="tpu_custom_call" | custom-call | flops 2415919104 | bytes 7000000 | tf_op jit(solution)/shard_map/pallas_call | solution.py:445
  62.3 0.0 collective-permute-done.2.gap_got
  62.4 0.0 copy-start
  62.4 3.5 %shard_map.115 = (bf16[32,64,256]{2,1,0:T(8,128)(2,1)S(1)}, bf16[768,128]{1,0:T(8,128)(2,1)S(1)}, f32[3,1,256]{2,1,0:T(1,128)S(1)}, f32[128,768]{1,0:T(8,128)S(1)}) custom-call(bf16[32,328,128]{2,1,0:T(8,128)(2,1)S(1)} %collective-permute-done.1.theirs, bf16[32,16,128]{2,1,0:T(8,128)(2,1)S(1)} %get-tuple-element.39.gap_kept, ...), custom_call_target="tpu_custom_call" | custom-call | flops 3221225472 | bytes 7000000 | tf_op jit(solution)/shard_map/pallas_call | solution.py:460
  65.9 0.4 collective-permute-start.4
  66.2 2.2 %collective-permute-start.3 = (bf16[32,16,256]{2,1,0:T(8,128)(2,1)S(1)}, bf16[32,16,256]{2,1,0:T(8,128)(2,1)S(1)}, u32[]{:S(2)}, u32[]{:S(2)}) collective-permute-start(bf16[32,16,256]{2,1,0:T(8,128)(2,1)S(1)} %get-tuple-element.55), channel_id=1, source_target_pairs={{0,2},{2,0},{1,3},{3,1},{4,6},{6,4},{5,7},{7,5},{8,10},{10,8},{9,1... | collective-permute-start | bytes 786440 | tf_op jit(solution)/shard_map/ppermute | solution.py:409
  68.5 0.0 copy-done
  68.5 3.4 %shard_map.116 = (bf16[32,64,256]{2,1,0:T(8,128)(2,1)S(1)}, bf16[32,24,128]{2,1,0:T(8,128)(2,1)S(1)}) custom-call(bf16[32,328,128]{2,1,0:T(8,128)(2,1)S(1)} %all_to_all.10.mine, bf16[3,256,128]{2,1,0:T(8,128)(2,1)S(1)} %get-tuple-element.38.q_ref, bf16[768,128]{1,0:T(8,128)(2,1)S(1)} %get-tuple-element.48.cot_ref, ...), custom_call_target="tpu_custom_call" | custom-call | flops 3221225472 | bytes 7000000 | tf_op jit(solution)/shard_map/pallas_call | solution.py:472
  71.9 3.5 %collective-permute-done.3.got = bf16[32,16,256]{2,1,0:T(8,128)(2,1)S(1)} collective-permute-done((bf16[32,16,256]{2,1,0:T(8,128)(2,1)S(1)}, bf16[32,16,256]{2,1,0:T(8,128)(2,1)S(1)}, u32[]{:S(2)}, u32[]{:S(2)}) %collective-permute-start.3) | collective-permute-done | bytes 262176 | tf_op jit(solution)/shard_map/ppermute | solution.py:409
  75.4 0.0 collective-permute-done.4.theirs
  75.4 0.3 shard_map.117
  75.7 24.5 %all_to_all.11.r_ref = bf16[32,200,128]{2,1,0:T(8,128)(2,1)S(1)} all-to-all(bf16[32,200,128]{2,1,0:T(8,128)(2,1)S(1)} %shard_map.117), channel_id=1, replica_groups=mesh['zl'=2,'y'=4,'x'=4,'zh'=2,'c'=2] {'x','zl','y'}, dimensions={0} | all-to-all | bytes 3276800 | tf_op jit(solution)/shard_map/all_to_all | solution.py:405
  100.2 0.2 shard_map.118
  100.4 3.2 %collective-permute-start.5 = (bf16[3,64,640]{2,1,0:T(8,128)(2,1)S(1)}, bf16[3,64,640]{2,1,0:T(8,128)(2,1)S(1)}, u32[]{:S(2)}, u32[]{:S(2)}) collective-permute-start(bf16[3,64,640]{2,1,0:T(8,128)(2,1)S(1)} %get-tuple-element.60), channel_id=1, source_target_pairs={{0,1},{1,0},{2,3},{3,2},{4,5},{5,4},{6,7},{7,6},{8,9},{9,8},{10,11... | collective-permute-start | bytes 737288 | tf_op jit(solution)/shard_map/ppermute | solution.py:409
  103.6 0.9 shard_map.119
  104.6 0.2 collective-permute-done.5.got
  104.8 0.7 shard_map.120
Async XLA Ops:
  1.8 3.0 %collective-permute-start = (bf16[6,64,640]{2,1,0:T(8,128)(2,1)S(1)}, bf16[6,64,640]{2,1,0:T(8,128)(2,1)S(1)}, u32[]{:S(2)}, u32[]{:S(2)}) collective-permute-start(bf16[6,64,640]{2,1,0:T(8,128)(2,1)S(1)} %shard_map.111), channel_id=1, source_target_pairs={{0,1},{1,0},{2,3},{3,2},{4,5},{5,4},{6,7},{7,6},{8,9},{9,8},{10,11... | collective-permute-start | bytes 1474568 | tf_op jit(solution)/shard_map/ppermute | solution.py:409
  46.5 11.0 %collective-permute-start.1 = (bf16[32,328,128]{2,1,0:T(8,128)(2,1)S(1)}, bf16[32,328,128]{2,1,0:T(8,128)(2,1)S(1)}, u32[]{:S(2)}, u32[]{:S(2)}) collective-permute-start(bf16[32,328,128]{2,1,0:T(8,128)(2,1)S(1)} %all_to_all.10.mine), channel_id=1, source_target_pairs={{0,1},{1,0},{2,3},{3,2},{4,5},{5,4},{6,7},{7,6},{8,9},{9,8},{10,11... | collective-permute-start | bytes 8060936 | tf_op jit(solution)/shard_map/ppermute | solution.py:409
  53.9 8.4 %collective-permute-start.2 = (bf16[32,16,128]{2,1,0:T(8,128)(2,1)S(1)}, bf16[32,16,128]{2,1,0:T(8,128)(2,1)S(1)}, u32[]{:S(2)}, u32[]{:S(2)}) collective-permute-start(bf16[32,16,128]{2,1,0:T(8,128)(2,1)S(1)} %get-tuple-element.40), channel_id=1, source_target_pairs={{0,2},{2,0},{1,3},{3,1},{4,6},{6,4},{5,7},{7,5},{8,10},{10,8},{9,1... | collective-permute-start | bytes 393224 | tf_op jit(solution)/shard_map/ppermute | solution.py:409
  62.4 6.1 %copy-start = (bf16[3,2048,256]{2,1,0:T(8,128)(2,1)S(1)}, bf16[3,2048,256]{2,1,0:T(8,128)(2,1)}, u32[]{:S(2)}) copy-start(bf16[3,2048,256]{2,1,0:T(8,128)(2,1)} %get-tuple-element.50.w_ref) | copy-start | bytes 9437188
  65.9 9.5 %collective-permute-start.4 = (bf16[32,64,256]{2,1,0:T(8,128)(2,1)S(1)}, bf16[32,64,256]{2,1,0:T(8,128)(2,1)S(1)}, u32[]{:S(2)}, u32[]{:S(2)}) collective-permute-start(bf16[32,64,256]{2,1,0:T(8,128)(2,1)S(1)} %get-tuple-element.56), channel_id=1, source_target_pairs={{0,1},{1,0},{2,3},{3,2},{4,5},{5,4},{6,7},{7,6},{8,9},{9,8},{10,11... | collective-permute-start | bytes 3145736 | tf_op jit(solution)/shard_map/ppermute | solution.py:409
  66.2 9.1 %collective-permute-start.3 = (bf16[32,16,256]{2,1,0:T(8,128)(2,1)S(1)}, bf16[32,16,256]{2,1,0:T(8,128)(2,1)S(1)}, u32[]{:S(2)}, u32[]{:S(2)}) collective-permute-start(bf16[32,16,256]{2,1,0:T(8,128)(2,1)S(1)} %get-tuple-element.55), channel_id=1, source_target_pairs={{0,2},{2,0},{1,3},{3,1},{4,6},{6,4},{5,7},{7,5},{8,10},{10,8},{9,1... | collective-permute-start | bytes 786440 | tf_op jit(solution)/shard_map/ppermute | solution.py:409
  100.4 4.4 %collective-permute-start.5 = (bf16[3,64,640]{2,1,0:T(8,128)(2,1)S(1)}, bf16[3,64,640]{2,1,0:T(8,128)(2,1)S(1)}, u32[]{:S(2)}, u32[]{:S(2)}) collective-permute-start(bf16[3,64,640]{2,1,0:T(8,128)(2,1)S(1)} %get-tuple-element.60), channel_id=1, source_target_pairs={{0,1},{1,0},{2,3},{3,2},{4,5},{5,4},{6,7},{7,6},{8,9},{9,8},{10,11... | collective-permute-start | bytes 737288 | tf_op jit(solution)/shard_map/ppermute | solution.py:409

commit v10 on v9

--- a/solution.py
+++ b/solution.py
@@ -63,7 +63,7 @@
 
 
 def part_here():
-    place = lax.axis_index("x") * 8 + lax.axis_index("zl") * 4 + lax.axis_index("y")
+    place = lax.axis_index("zl") * 16 + lax.axis_index("y") * 4 + lax.axis_index("x")
     return lax.rem(place, PARTS)
 
 
@@ -129,6 +129,15 @@
             else:
                 which, eight = GAPS[part][to]
                 out[chip, rows, :] = gap[which, 8 * eight : 8 * eight + 8, gcols]
+
+
+def split_gaps(mine, sent, kept, sems):
+    run_all(
+        [
+            pltpu.make_async_copy(mine.at[:, low : low + 16, :], dst, sems.at[at])
+            for at, (dst, low) in enumerate(((sent, 312), (kept, 304)))
+        ]
+    )
 
 
 def fold(x, op):
@@ -196,13 +205,8 @@
         close(tiles - 1)
 
 
-def forward_mine(
-    mine, q_ref, qq_ref, w_hbm, m_ref, sums_ref, acc_ref, gap_sent, gap_kept,
-    stage, w_ref, sems, *scratch
-):
+def forward_mine(mine, q_ref, qq_ref, w_hbm, m_ref, sums_ref, acc_ref, stage, w_ref, sems, *scratch):
     for s in range(mine.shape[0]):
-        gap_sent[s] = mine[s, 312:328, :]
-        gap_kept[s] = mine[s, 304:320, :]
         stage[PIECE * s : PIECE * s + PIECE, 0:HD] = mine[s, 256:280, :].astype(F32)
         stage[PIECE * s : PIECE * s + PIECE, HD:] = mine[s, 280:304, :].astype(F32)
     tiles = q_ref.shape[0]
@@ -398,11 +402,10 @@
 
 SWAP = [(0, 1), (1, 0)]
 BLOCK_AXES = ("zl", "y", "x")
-CHIP_AXES = ("x", "zl", "y")
 
 
 def exchange(array):
-    return lax.all_to_all(array, CHIP_AXES, 0, 0, tiled=True)
+    return lax.all_to_all(array, BLOCK_AXES, 0, 0, tiled=True)
 
 
 def swap(array, axis):
@@ -414,6 +417,11 @@
     rows, subs = tiles * QT, length // SUB
     flops = 2 * length * rows * HD
     gpiece = shape(chips, 16, HD)
+    gap_sent, gap_kept = call(
+        split_gaps, [(gpiece, VMEM), (gpiece, VMEM)], [ANY], 2, (pltpu.SemaphoreType.DMA((2,)),),
+        moved=500_000,
+    )(mine)
+    gap_got = swap(gap_sent, "zh")
     theirs = swap(mine, "c")
     q, qq = shape(tiles, QT, HD), shape(tiles, QT, 2 * HD)
     w = shape(tiles, length, QT)
@@ -431,16 +439,14 @@
         pltpu.VMEM((SUB, rows), BF),
     )
     stage = pltpu.VMEM((rows, 2 * HD), F32)
-    q, qq, w1, m1, sums1, acc1, gap_sent, gap_kept = call(
+    q, qq, w1, m1, sums1, acc1 = call(
         forward_mine,
-        [(q, VMEM), (qq, VMEM), (w, HBM), (stats, VMEM), (sums, VMEM), (acc, VMEM)]
-        + [(gpiece, VMEM)] * 2,
+        [(q, VMEM), (qq, VMEM), (w, HBM), (stats, VMEM), (sums, VMEM), (acc, VMEM)],
         [VMEM],
         30,
         (stage,) + tiles_of + scratch,
         6 * flops, length * rows, 7_000_000,
     )(mine)
-    gap_got = swap(gap_sent, "zh")
     key_piece = shape(chips, KROWS, 2 * HD)
     w2, pieces, cross, o, share = call(
         forward_theirs,

time: 106 us -> 106 us (level)
  starting transfers between devices: 13.5 us -> 10 us
  waiting for transfers between devices: 3.9 us -> 6.15 us
  blocking collectives: 65.9 us -> 67 us
    ppermute x6, starting transfers between devices: 13.5 us -> 10 us  [swap(): return lax.ppermute(array, axis, SWAP)]
    ppermute x6, waiting for transfers between devices: 3.9 us -> 6.15 us  [swap(): return lax.ppermute(array, axis, SWAP)]
where the time goes in v10:
time: 106 us
  blocking collectives  67 us (63%)
  Pallas kernels  21.7 us (20%)
  starting transfers between devices  10 us (9%)
  waiting for transfers between devices  6.15 us (6%)
    all_to_all x2, blocking collectives, exchange(): return lax.all_to_all(array, BLOCK_AXES, 0, 0, tiled=True)  67 us
    ppermute x6, starting transfers between devices, swap(): return lax.ppermute(array, axis, SWAP)  10 us
    ppermute x6, waiting for transfers between devices, swap(): return lax.ppermute(array, axis, SWAP)  6.15 us
    pallas_call x1, Pallas kernels, attention(): call(forward_theirs, [(w, VMEM), (shape(chips, PIECE, 2 * HD), VMEM), (sh...  4.87 us
    pallas_call x1, Pallas kernels, attention(): call(forward_mine, [(q, VMEM), (qq, VMEM), (w, HBM), (stats, VMEM), (sums...  4.72 us
    pallas_call x1, Pallas kernels, attention(): call(backward_theirs, [(key_piece, VMEM), (shape(rows, HD), VMEM), (stats...  3.69 us
    pallas_call x1, Pallas kernels, attention(): call(backward_mine, [(key_piece, VMEM), (shape(chips, PIECE, HD), VMEM)],...  3.38 us
  transfers between devices with their start and end apart: 6, of which 3 were waited for; matrix products, arithmetic and copies ran while one was open for 0% of the time, Pallas kernels for 14%

profile of v10, /device:TPU:1, one launch (start us, length us, event | category | flops | bytes accessed | tf_op | source)
XLA Modules:
  0.0 105.7 jit_solution(4905706541903815189)
XLA Ops:
  0.6 1.1 %shard_map.111 = bf16[6,64,640]{2,1,0:T(8,128)(2,1)S(1)} custom-call(bf16[128,640]{1,0:T(8,128)(2,1)} %refs_0_.3, bf16[128,640]{1,0:T(8,128)(2,1)} %refs_1_.3, bf16[128,640]{1,0:T(8,128)(2,1)} %refs_2_.3, bf16[128,640]{1,0:T(8,128)(2,1)} %refs_3_.3, bf16[128,640]{1,0:T(8,128)(2,1)} %refs_4_.3, bf16[128,640]{1,0:T(8,128)(2,1)} %refs_5_.3), custom_call_target="tpu_custom_call" | custom-call | bytes 1000000 | tf_op jit(solution)/shard_map/pallas_call | solution.py:500
  1.8 1.5 %collective-permute-start = (bf16[6,64,640]{2,1,0:T(8,128)(2,1)S(1)}, bf16[6,64,640]{2,1,0:T(8,128)(2,1)S(1)}, u32[]{:S(2)}, u32[]{:S(2)}) collective-permute-start(bf16[6,64,640]{2,1,0:T(8,128)(2,1)S(1)} %shard_map.111), channel_id=1, source_target_pairs={{0,1},{1,0},{2,3},{3,2},{4,5},{5,4},{6,7},{7,6},{8,9},{9,8},{10,11... | collective-permute-start | bytes 1474568 | tf_op jit(solution)/shard_map/ppermute | solution.py:412
  3.2 1.3 %shard_map.110 = (bf16[6,64,640]{2,1,0:T(8,128)(2,1)S(1)}, bf16[2,32,1280]{2,1,0:T(8,128)(2,1)S(1)}) custom-call(bf16[128,640]{1,0:T(8,128)(2,1)} %refs_0_.3, bf16[128,640]{1,0:T(8,128)(2,1)} %refs_1_.3, bf16[128,640]{1,0:T(8,128)(2,1)} %refs_2_.3, bf16[128,640]{1,0:T(8,128)(2,1)} %refs_3_.3, bf16[128,640]{1,0:T(8,128)(2,1)} %refs_4_.3, ...), custom_call_target="tpu_custom_call" | custom-call | bytes 1000000 | tf_op jit(solution)/shard_map/pallas_call | solution.py:502
  4.5 0.2 collective-permute-done.got
  4.7 0.4 shard_map.112
  5.1 41.6 %all_to_all.10.mine = bf16[32,328,128]{2,1,0:T(8,128)(2,1)S(1)} all-to-all(bf16[32,328,128]{2,1,0:T(8,128)(2,1)S(1)} %shard_map.112), channel_id=1, replica_groups=mesh['zl'=2,'y'=4,'x'=4,'zh'=2,'c'=2] {'zl','y','x'}, dimensions={0} | all-to-all | bytes 5373952 | tf_op jit(solution)/shard_map/all_to_all | solution.py:408
  46.8 2.1 %collective-permute-start.1 = (bf16[32,328,128]{2,1,0:T(8,128)(2,1)S(1)}, bf16[32,328,128]{2,1,0:T(8,128)(2,1)S(1)}, u32[]{:S(2)}, u32[]{:S(2)}) collective-permute-start(bf16[32,328,128]{2,1,0:T(8,128)(2,1)S(1)} %all_to_all.10.mine), channel_id=1, source_target_pairs={{0,1},{1,0},{2,3},{3,2},{4,5},{5,4},{6,7},{7,6},{8,9},{9,8},{10,11... | collective-permute-start | bytes 8060936 | tf_op jit(solution)/shard_map/ppermute | solution.py:412
  48.9 3.4 %collective-permute-start.2 = (bf16[32,16,128]{2,1,0:T(8,128)(2,1)S(1)}, bf16[32,16,128]{2,1,0:T(8,128)(2,1)S(1)}, u32[]{:S(2)}, u32[]{:S(2)}) collective-permute-start(bf16[32,16,128]{2,1,0:T(8,128)(2,1)S(1)} %get-tuple-element.40), channel_id=1, source_target_pairs={{0,2},{2,0},{1,3},{3,1},{4,6},{6,4},{5,7},{7,5},{8,10},{10,8},{9,1... | collective-permute-start | bytes 393224 | tf_op jit(solution)/shard_map/ppermute | solution.py:412
  52.3 4.7 %shard_map.113 = (bf16[3,256,128]{2,1,0:T(8,128)(2,1)S(1)}, bf16[3,256,256]{2,1,0:T(8,128)(2,1)S(1)}, bf16[3,2048,256]{2,1,0:T(8,128)(2,1)}, f32[3,1,256]{2,1,0:...) custom-call(bf16[32,328,128]{2,1,0:T(8,128)(2,1)S(1)} %all_to_all.10.mine), custom_call_target="tpu_custom_call" | custom-call | flops 2415919104 | bytes 7000000 | tf_op jit(solution)/shard_map/pallas_call | solution.py:442
  57.0 0.0 collective-permute-done.1.theirs
  57.0 4.9 %shard_map.115 = (bf16[3,2048,256]{2,1,0:T(8,128)(2,1)S(1)}, bf16[32,24,256]{2,1,0:T(8,128)(2,1)S(1)}, bf16[32,16,256]{2,1,0:T(8,128)(2,1)S(1)}, f32[3,256,256]{2,1,0:T(8,128)S(1)}, f32[2,3,1,256]{3,2,1,0:T(1,128)S(1)}) custom-call(bf16[32,328,128]{2,1,0:T(8,128)(2,1)S(1)} %collective-permute-done.1.theirs, ...), custom_call_target="tpu_custom_call" | custom-call | flops 2415919104 | bytes 7000000 | tf_op jit(solution)/shard_map/pallas_call | solution.py:451
  61.9 0.0 collective-permute-done.2.gap_got
  61.9 0.0 copy-start
  61.9 3.7 %shard_map.116 = (bf16[32,64,256]{2,1,0:T(8,128)(2,1)S(1)}, bf16[768,128]{1,0:T(8,128)(2,1)S(1)}, f32[3,1,256]{2,1,0:T(1,128)S(1)}, f32[128,768]{1,0:T(8,128)S(1)}) custom-call(bf16[32,328,128]{2,1,0:T(8,128)(2,1)S(1)} %collective-permute-done.1.theirs, bf16[32,16,128]{2,1,0:T(8,128)(2,1)S(1)} %get-tuple-element.39.gap_kept, ...), custom_call_target="tpu_custom_call" | custom-call | flops 3221225472 | bytes 7000000 | tf_op jit(solution)/shard_map/pallas_call | solution.py:466
  65.6 0.4 collective-permute-start.4
  66.0 0.0 collective-permute-start.3
  66.0 0.0 copy-done
  66.0 3.4 %shard_map.117 = (bf16[32,64,256]{2,1,0:T(8,128)(2,1)S(1)}, bf16[32,24,128]{2,1,0:T(8,128)(2,1)S(1)}) custom-call(bf16[32,328,128]{2,1,0:T(8,128)(2,1)S(1)} %all_to_all.10.mine, bf16[3,256,128]{2,1,0:T(8,128)(2,1)S(1)} %get-tuple-element.38.q_ref, bf16[768,128]{1,0:T(8,128)(2,1)S(1)} %get-tuple-element.48.cot_ref, ...), custom_call_target="tpu_custom_call" | custom-call | flops 3221225472 | bytes 7000000 | tf_op jit(solution)/shard_map/pallas_call | solution.py:478
  69.4 5.8 %collective-permute-done.3.got = bf16[32,16,256]{2,1,0:T(8,128)(2,1)S(1)} collective-permute-done((bf16[32,16,256]{2,1,0:T(8,128)(2,1)S(1)}, bf16[32,16,256]{2,1,0:T(8,128)(2,1)S(1)}, u32[]{:S(2)}, u32[]{:S(2)}) %collective-permute-start.3) | collective-permute-done | bytes 262176 | tf_op jit(solution)/shard_map/ppermute | solution.py:412
  75.1 0.0 collective-permute-done.4.theirs
  75.1 0.3 shard_map.118
  75.5 25.3 %all_to_all.11.r_ref = bf16[32,200,128]{2,1,0:T(8,128)(2,1)S(1)} all-to-all(bf16[32,200,128]{2,1,0:T(8,128)(2,1)S(1)} %shard_map.118), channel_id=1, replica_groups=mesh['zl'=2,'y'=4,'x'=4,'zh'=2,'c'=2] {'zl','y','x'}, dimensions={0} | all-to-all | bytes 3276800 | tf_op jit(solution)/shard_map/all_to_all | solution.py:408
  100.8 0.2 shard_map.119
  101.0 2.7 %collective-permute-start.5 = (bf16[3,64,640]{2,1,0:T(8,128)(2,1)S(1)}, bf16[3,64,640]{2,1,0:T(8,128)(2,1)S(1)}, u32[]{:S(2)}, u32[]{:S(2)}) collective-permute-start(bf16[3,64,640]{2,1,0:T(8,128)(2,1)S(1)} %get-tuple-element.60), channel_id=1, source_target_pairs={{0,1},{1,0},{2,3},{3,2},{4,5},{5,4},{6,7},{7,6},{8,9},{9,8},{10,11... | collective-permute-start | bytes 737288 | tf_op jit(solution)/shard_map/ppermute | solution.py:412
  103.7 0.9 shard_map.120
  104.6 0.2 collective-permute-done.5.got
  104.8 0.7 shard_map.121
  (1 shorter events, 0.0 us)
Async XLA Ops:
  1.8 3.0 %collective-permute-start = (bf16[6,64,640]{2,1,0:T(8,128)(2,1)S(1)}, bf16[6,64,640]{2,1,0:T(8,128)(2,1)S(1)}, u32[]{:S(2)}, u32[]{:S(2)}) collective-permute-start(bf16[6,64,640]{2,1,0:T(8,128)(2,1)S(1)} %shard_map.111), channel_id=1, source_target_pairs={{0,1},{1,0},{2,3},{3,2},{4,5},{5,4},{6,7},{7,6},{8,9},{9,8},{10,11... | collective-permute-start | bytes 1474568 | tf_op jit(solution)/shard_map/ppermute | solution.py:412
  46.8 10.2 %collective-permute-start.1 = (bf16[32,328,128]{2,1,0:T(8,128)(2,1)S(1)}, bf16[32,328,128]{2,1,0:T(8,128)(2,1)S(1)}, u32[]{:S(2)}, u32[]{:S(2)}) collective-permute-start(bf16[32,328,128]{2,1,0:T(8,128)(2,1)S(1)} %all_to_all.10.mine), channel_id=1, source_target_pairs={{0,1},{1,0},{2,3},{3,2},{4,5},{5,4},{6,7},{7,6},{8,9},{9,8},{10,11... | collective-permute-start | bytes 8060936 | tf_op jit(solution)/shard_map/ppermute | solution.py:412
  48.9 13.0 %collective-permute-start.2 = (bf16[32,16,128]{2,1,0:T(8,128)(2,1)S(1)}, bf16[32,16,128]{2,1,0:T(8,128)(2,1)S(1)}, u32[]{:S(2)}, u32[]{:S(2)}) collective-permute-start(bf16[32,16,128]{2,1,0:T(8,128)(2,1)S(1)} %get-tuple-element.40), channel_id=1, source_target_pairs={{0,2},{2,0},{1,3},{3,1},{4,6},{6,4},{5,7},{7,5},{8,10},{10,8},{9,1... | collective-permute-start | bytes 393224 | tf_op jit(solution)/shard_map/ppermute | solution.py:412
  61.9 4.1 %copy-start = (bf16[3,2048,256]{2,1,0:T(8,128)(2,1)S(1)}, bf16[3,2048,256]{2,1,0:T(8,128)(2,1)}, u32[]{:S(2)}) copy-start(bf16[3,2048,256]{2,1,0:T(8,128)(2,1)} %get-tuple-element.50.w_ref) | copy-start | bytes 9437188
  65.6 9.5 %collective-permute-start.4 = (bf16[32,64,256]{2,1,0:T(8,128)(2,1)S(1)}, bf16[32,64,256]{2,1,0:T(8,128)(2,1)S(1)}, u32[]{:S(2)}, u32[]{:S(2)}) collective-permute-start(bf16[32,64,256]{2,1,0:T(8,128)(2,1)S(1)} %get-tuple-element.56), channel_id=1, source_target_pairs={{0,1},{1,0},{2,3},{3,2},{4,5},{5,4},{6,7},{7,6},{8,9},{9,8},{10,11... | collective-permute-start | bytes 3145736 | tf_op jit(solution)/shard_map/ppermute | solution.py:412
  66.0 9.1 %collective-permute-start.3 = (bf16[32,16,256]{2,1,0:T(8,128)(2,1)S(1)}, bf16[32,16,256]{2,1,0:T(8,128)(2,1)S(1)}, u32[]{:S(2)}, u32[]{:S(2)}) collective-permute-start(bf16[32,16,256]{2,1,0:T(8,128)(2,1)S(1)} %get-tuple-element.55), channel_id=1, source_target_pairs={{0,2},{2,0},{1,3},{3,1},{4,6},{6,4},{5,7},{7,5},{8,10},{10,8},{9,1... | collective-permute-start | bytes 786440 | tf_op jit(solution)/shard_map/ppermute | solution.py:412
  101.0 3.9 %collective-permute-start.5 = (bf16[3,64,640]{2,1,0:T(8,128)(2,1)S(1)}, bf16[3,64,640]{2,1,0:T(8,128)(2,1)S(1)}, u32[]{:S(2)}, u32[]{:S(2)}) collective-permute-start(bf16[3,64,640]{2,1,0:T(8,128)(2,1)S(1)} %get-tuple-element.60), channel_id=1, source_target_pairs={{0,1},{1,0},{2,3},{3,2},{4,5},{5,4},{6,7},{7,6},{8,9},{9,8},{10,11... | collective-permute-start | bytes 737288 | tf_op jit(solution)/shard_map/ppermute | solution.py:412

commit v11 on v7

--- a/solution.py
+++ b/solution.py
@@ -62,7 +62,7 @@
 
 
 def part_here():
-    place = lax.axis_index("zl") * 16 + lax.axis_index("y") * 4 + lax.axis_index("x")
+    place = lax.axis_index("x") * 8 + lax.axis_index("zl") * 4 + lax.axis_index("y")
     return lax.rem(place, PARTS)
 
 
@@ -384,10 +384,11 @@
 
 SWAP = [(0, 1), (1, 0)]
 BLOCK_AXES = ("zl", "y", "x")
+CHIP_AXES = ("x", "zl", "y")
 
 
 def exchange(array):
-    return lax.all_to_all(array, BLOCK_AXES, 0, 0, tiled=True)
+    return lax.all_to_all(array, CHIP_AXES, 0, 0, tiled=True)
 
 
 def swap(array, axis):

time: 106 us -> 106 us (level)
  starting transfers between devices: 10 us -> 11.1 us
  blocking collectives: 67 us -> 65.9 us
where the time goes in v11:
time: 106 us
  blocking collectives  65.9 us (62%)
  Pallas kernels  21.7 us (20%)
  starting transfers between devices  11.1 us (10%)
  waiting for transfers between devices  6.27 us (6%)
    all_to_all x2, blocking collectives, exchange(): return lax.all_to_all(array, CHIP_AXES, 0, 0, tiled=True)  65.9 us
    ppermute x6, starting transfers between devices, swap(): return lax.ppermute(array, axis, SWAP)  11.1 us
    ppermute x6, waiting for transfers between devices, swap(): return lax.ppermute(array, axis, SWAP)  6.27 us
    pallas_call x1, Pallas kernels, attention(): call(forward_theirs, [(w, VMEM), (shape(chips, PIECE, 2 * HD), VMEM), (sh...  4.87 us
    pallas_call x1, Pallas kernels, attention(): call(forward_mine, [(q, VMEM), (qq, VMEM), (w, HBM), (stats, VMEM), (sums...  4.72 us
    pallas_call x1, Pallas kernels, attention(): call(backward_theirs, [(key_piece, VMEM), (shape(rows, HD), VMEM), (stats...  3.69 us
    pallas_call x1, Pallas kernels, attention(): call(backward_mine, [(key_piece, VMEM), (shape(chips, PIECE, HD), VMEM)],...  3.38 us
  transfers between devices with their start and end apart: 6, of which 3 were waited for; matrix products, arithmetic and copies ran while one was open for 0% of the time, Pallas kernels for 14%

profile of v11, /device:TPU:1, one launch (start us, length us, event | category | flops | bytes accessed | tf_op | source)
XLA Modules:
  0.0 105.7 jit_solution(17186250955112606045)
XLA Ops:
  0.6 1.1 %shard_map.111 = bf16[6,64,640]{2,1,0:T(8,128)(2,1)S(1)} custom-call(bf16[128,640]{1,0:T(8,128)(2,1)} %refs_0_.3, bf16[128,640]{1,0:T(8,128)(2,1)} %refs_1_.3, bf16[128,640]{1,0:T(8,128)(2,1)} %refs_2_.3, bf16[128,640]{1,0:T(8,128)(2,1)} %refs_3_.3, bf16[128,640]{1,0:T(8,128)(2,1)} %refs_4_.3, bf16[128,640]{1,0:T(8,128)(2,1)} %refs_5_.3), custom_call_target="tpu_custom_call" | custom-call | bytes 1000000 | tf_op jit(solution)/shard_map/pallas_call | solution.py:483
  1.8 1.5 %collective-permute-start = (bf16[6,64,640]{2,1,0:T(8,128)(2,1)S(1)}, bf16[6,64,640]{2,1,0:T(8,128)(2,1)S(1)}, u32[]{:S(2)}, u32[]{:S(2)}) collective-permute-start(bf16[6,64,640]{2,1,0:T(8,128)(2,1)S(1)} %shard_map.111), channel_id=1, source_target_pairs={{0,1},{1,0},{2,3},{3,2},{4,5},{5,4},{6,7},{7,6},{8,9},{9,8},{10,11... | collective-permute-start | bytes 1474568 | tf_op jit(solution)/shard_map/ppermute | solution.py:395
  3.2 1.3 %shard_map.110 = (bf16[6,64,640]{2,1,0:T(8,128)(2,1)S(1)}, bf16[2,32,1280]{2,1,0:T(8,128)(2,1)S(1)}) custom-call(bf16[128,640]{1,0:T(8,128)(2,1)} %refs_0_.3, bf16[128,640]{1,0:T(8,128)(2,1)} %refs_1_.3, bf16[128,640]{1,0:T(8,128)(2,1)} %refs_2_.3, bf16[128,640]{1,0:T(8,128)(2,1)} %refs_3_.3, bf16[128,640]{1,0:T(8,128)(2,1)} %refs_4_.3, ...), custom_call_target="tpu_custom_call" | custom-call | bytes 1000000 | tf_op jit(solution)/shard_map/pallas_call | solution.py:485
  4.5 0.2 collective-permute-done.got
  4.7 0.4 shard_map.112
  5.1 41.4 %all_to_all.10.mine = bf16[32,328,128]{2,1,0:T(8,128)(2,1)S(1)} all-to-all(bf16[32,328,128]{2,1,0:T(8,128)(2,1)S(1)} %shard_map.112), channel_id=1, replica_groups=mesh['zl'=2,'y'=4,'x'=4,'zh'=2,'c'=2] {'x','zl','y'}, dimensions={0} | all-to-all | bytes 5373952 | tf_op jit(solution)/shard_map/all_to_all | solution.py:391
  46.5 2.6 %collective-permute-start.1 = (bf16[32,328,128]{2,1,0:T(8,128)(2,1)S(1)}, bf16[32,328,128]{2,1,0:T(8,128)(2,1)S(1)}, u32[]{:S(2)}, u32[]{:S(2)}) collective-permute-start(bf16[32,328,128]{2,1,0:T(8,128)(2,1)S(1)} %all_to_all.10.mine), channel_id=1, source_target_pairs={{0,1},{1,0},{2,3},{3,2},{4,5},{5,4},{6,7},{7,6},{8,9},{9,8},{10,11... | collective-permute-start | bytes 8060936 | tf_op jit(solution)/shard_map/ppermute | solution.py:395
  49.2 3.4 %collective-permute-start.2 = (bf16[32,16,128]{2,1,0:T(8,128)(2,1)S(1)}, bf16[32,16,128]{2,1,0:T(8,128)(2,1)S(1)}, u32[]{:S(2)}, u32[]{:S(2)}) collective-permute-start(bf16[32,16,128]{2,1,0:T(8,128)(2,1)S(1)} %get-tuple-element.37), channel_id=1, source_target_pairs={{0,2},{2,0},{1,3},{3,1},{4,6},{6,4},{5,7},{7,5},{8,10},{10,8},{9,1... | collective-permute-start | bytes 393224 | tf_op jit(solution)/shard_map/ppermute | solution.py:395
  52.6 4.7 %shard_map.113 = (bf16[3,256,128]{2,1,0:T(8,128)(2,1)S(1)}, bf16[3,256,256]{2,1,0:T(8,128)(2,1)S(1)}, bf16[3,2048,256]{2,1,0:T(8,128)(2,1)}, f32[3,1,256]{2,1,0:...) custom-call(bf16[32,328,128]{2,1,0:T(8,128)(2,1)S(1)} %all_to_all.10.mine), custom_call_target="tpu_custom_call" | custom-call | flops 2415919104 | bytes 7000000 | tf_op jit(solution)/shard_map/pallas_call | solution.py:425
  57.3 0.0 collective-permute-done.1.theirs
  57.3 4.9 %shard_map.115 = (bf16[3,2048,256]{2,1,0:T(8,128)(2,1)S(1)}, bf16[32,24,256]{2,1,0:T(8,128)(2,1)S(1)}, bf16[32,16,256]{2,1,0:T(8,128)(2,1)S(1)}, f32[3,256,256]{2,1,0:T(8,128)S(1)}, f32[2,3,1,256]{3,2,1,0:T(1,128)S(1)}) custom-call(bf16[32,328,128]{2,1,0:T(8,128)(2,1)S(1)} %collective-permute-done.1.theirs, ...), custom_call_target="tpu_custom_call" | custom-call | flops 2415919104 | bytes 7000000 | tf_op jit(solution)/shard_map/pallas_call | solution.py:434
  62.2 0.0 collective-permute-done.2.gap_got
  62.2 0.0 copy-start
  62.2 3.7 %shard_map.116 = (bf16[32,64,256]{2,1,0:T(8,128)(2,1)S(1)}, bf16[768,128]{1,0:T(8,128)(2,1)S(1)}, f32[3,1,256]{2,1,0:T(1,128)S(1)}, f32[128,768]{1,0:T(8,128)S(1)}) custom-call(bf16[32,328,128]{2,1,0:T(8,128)(2,1)S(1)} %collective-permute-done.1.theirs, bf16[32,16,128]{2,1,0:T(8,128)(2,1)S(1)} %get-tuple-element.36.gap_kept, ...), custom_call_target="tpu_custom_call" | custom-call | flops 3221225472 | bytes 7000000 | tf_op jit(solution)/shard_map/pallas_call | solution.py:449
  65.9 0.4 collective-permute-start.4
  66.3 0.0 collective-permute-start.3
  66.3 0.0 copy-done
  66.3 3.4 %shard_map.117 = (bf16[32,64,256]{2,1,0:T(8,128)(2,1)S(1)}, bf16[32,24,128]{2,1,0:T(8,128)(2,1)S(1)}) custom-call(bf16[32,328,128]{2,1,0:T(8,128)(2,1)S(1)} %all_to_all.10.mine, bf16[3,256,128]{2,1,0:T(8,128)(2,1)S(1)} %get-tuple-element.35.q_ref, bf16[768,128]{1,0:T(8,128)(2,1)S(1)} %get-tuple-element.45.cot_ref, ...), custom_call_target="tpu_custom_call" | custom-call | flops 3221225472 | bytes 7000000 | tf_op jit(solution)/shard_map/pallas_call | solution.py:461
  69.7 5.8 %collective-permute-done.3.got = bf16[32,16,256]{2,1,0:T(8,128)(2,1)S(1)} collective-permute-done((bf16[32,16,256]{2,1,0:T(8,128)(2,1)S(1)}, bf16[32,16,256]{2,1,0:T(8,128)(2,1)S(1)}, u32[]{:S(2)}, u32[]{:S(2)}) %collective-permute-start.3) | collective-permute-done | bytes 262176 | tf_op jit(solution)/shard_map/ppermute | solution.py:395
  75.4 0.0 collective-permute-done.4.theirs
  75.4 0.3 shard_map.118
  75.7 24.5 %all_to_all.11.r_ref = bf16[32,200,128]{2,1,0:T(8,128)(2,1)S(1)} all-to-all(bf16[32,200,128]{2,1,0:T(8,128)(2,1)S(1)} %shard_map.118), channel_id=1, replica_groups=mesh['zl'=2,'y'=4,'x'=4,'zh'=2,'c'=2] {'x','zl','y'}, dimensions={0} | all-to-all | bytes 3276800 | tf_op jit(solution)/shard_map/all_to_all | solution.py:391
  100.3 0.2 shard_map.120
  100.4 3.2 %collective-permute-start.5 = (bf16[3,64,640]{2,1,0:T(8,128)(2,1)S(1)}, bf16[3,64,640]{2,1,0:T(8,128)(2,1)S(1)}, u32[]{:S(2)}, u32[]{:S(2)}) collective-permute-start(bf16[3,64,640]{2,1,0:T(8,128)(2,1)S(1)} %get-tuple-element.57), channel_id=1, source_target_pairs={{0,1},{1,0},{2,3},{3,2},{4,5},{5,4},{6,7},{7,6},{8,9},{9,8},{10,11... | collective-permute-start | bytes 737288 | tf_op jit(solution)/shard_map/ppermute | solution.py:395
  103.7 0.8 shard_map.119
  104.5 0.3 collective-permute-done.5.got
  104.8 0.8 shard_map.121
  (1 shorter events, 0.0 us)
Async XLA Ops:
  1.8 3.0 %collective-permute-start = (bf16[6,64,640]{2,1,0:T(8,128)(2,1)S(1)}, bf16[6,64,640]{2,1,0:T(8,128)(2,1)S(1)}, u32[]{:S(2)}, u32[]{:S(2)}) collective-permute-start(bf16[6,64,640]{2,1,0:T(8,128)(2,1)S(1)} %shard_map.111), channel_id=1, source_target_pairs={{0,1},{1,0},{2,3},{3,2},{4,5},{5,4},{6,7},{7,6},{8,9},{9,8},{10,11... | collective-permute-start | bytes 1474568 | tf_op jit(solution)/shard_map/ppermute | solution.py:395
  46.5 10.8 %collective-permute-start.1 = (bf16[32,328,128]{2,1,0:T(8,128)(2,1)S(1)}, bf16[32,328,128]{2,1,0:T(8,128)(2,1)S(1)}, u32[]{:S(2)}, u32[]{:S(2)}) collective-permute-start(bf16[32,328,128]{2,1,0:T(8,128)(2,1)S(1)} %all_to_all.10.mine), channel_id=1, source_target_pairs={{0,1},{1,0},{2,3},{3,2},{4,5},{5,4},{6,7},{7,6},{8,9},{9,8},{10,11... | collective-permute-start | bytes 8060936 | tf_op jit(solution)/shard_map/ppermute | solution.py:395
  49.2 13.0 %collective-permute-start.2 = (bf16[32,16,128]{2,1,0:T(8,128)(2,1)S(1)}, bf16[32,16,128]{2,1,0:T(8,128)(2,1)S(1)}, u32[]{:S(2)}, u32[]{:S(2)}) collective-permute-start(bf16[32,16,128]{2,1,0:T(8,128)(2,1)S(1)} %get-tuple-element.37), channel_id=1, source_target_pairs={{0,2},{2,0},{1,3},{3,1},{4,6},{6,4},{5,7},{7,5},{8,10},{10,8},{9,1... | collective-permute-start | bytes 393224 | tf_op jit(solution)/shard_map/ppermute | solution.py:395
  62.2 4.1 %copy-start = (bf16[3,2048,256]{2,1,0:T(8,128)(2,1)S(1)}, bf16[3,2048,256]{2,1,0:T(8,128)(2,1)}, u32[]{:S(2)}) copy-start(bf16[3,2048,256]{2,1,0:T(8,128)(2,1)} %get-tuple-element.47.w_ref) | copy-start | bytes 9437188
  65.9 9.5 %collective-permute-start.4 = (bf16[32,64,256]{2,1,0:T(8,128)(2,1)S(1)}, bf16[32,64,256]{2,1,0:T(8,128)(2,1)S(1)}, u32[]{:S(2)}, u32[]{:S(2)}) collective-permute-start(bf16[32,64,256]{2,1,0:T(8,128)(2,1)S(1)} %get-tuple-element.53), channel_id=1, source_target_pairs={{0,1},{1,0},{2,3},{3,2},{4,5},{5,4},{6,7},{7,6},{8,9},{9,8},{10,11... | collective-permute-start | bytes 3145736 | tf_op jit(solution)/shard_map/ppermute | solution.py:395
  66.3 9.1 %collective-permute-start.3 = (bf16[32,16,256]{2,1,0:T(8,128)(2,1)S(1)}, bf16[32,16,256]{2,1,0:T(8,128)(2,1)S(1)}, u32[]{:S(2)}, u32[]{:S(2)}) collective-permute-start(bf16[32,16,256]{2,1,0:T(8,128)(2,1)S(1)} %get-tuple-element.52), channel_id=1, source_target_pairs={{0,2},{2,0},{1,3},{3,1},{4,6},{6,4},{5,7},{7,5},{8,10},{10,8},{9,1... | collective-permute-start | bytes 786440 | tf_op jit(solution)/shard_map/ppermute | solution.py:395
  100.4 4.4 %collective-permute-start.5 = (bf16[3,64,640]{2,1,0:T(8,128)(2,1)S(1)}, bf16[3,64,640]{2,1,0:T(8,128)(2,1)S(1)}, u32[]{:S(2)}, u32[]{:S(2)}) collective-permute-start(bf16[3,64,640]{2,1,0:T(8,128)(2,1)S(1)} %get-tuple-element.57), channel_id=1, source_target_pairs={{0,1},{1,0},{2,3},{3,2},{4,5},{5,4},{6,7},{7,6},{8,9},{9,8},{10,11... | collective-permute-start | bytes 737288 | tf_op jit(solution)/shard_map/ppermute | solution.py:395
